TPU v7x, 32 devices: a whole 2x2x4 slice. The times are simulated.
32 devices in a mesh: gz: 4 (over y, x), ba: 8 (over z, core).
Axes of the slice: x: 2, y: 2, z: 4, core: 2. Of those that a mesh axis runs over, the one named last changes fastest.
Arguments:
- material_fraction: float32 [128, 32, 1024], P(('gz', 'ba')), may hold values from 0.05 to 1
- primal_heat_solution: float32 [128, 32, 1024], P(('gz', 'ba')), may hold values from -6 to 6
- dual_load: float32 [128, 32, 1024], P(('gz', 'ba')), may hold values from -6 to 6
- dual_prior_design: float32 [128, 32, 1024], P(('gz', 'ba')), may hold values from -3 to 3
- holder_cube_location: int32 [128], P(('gz', 'ba')), may hold values from -1 to 31, as said below
Outputs:
- dual_solution: float32 [128, 32, 1024], P(('gz', 'ba'))
- filtered: float32 [256, 64, 256], P(('gz', 'ba'))
Inputs may be any that keep to these rules, and one draw needn't show every extreme that they name: `holder_cube_location`: each device's 4 entries list distinct brick positions of 0 to 31 in increasing order, followed by -1 for empty slots; every device's list holds positions 0 and (3) * 4 * 2, every device fills at least a third of its slots and at least two, and some device fills all of them.
All inputs are finite; a program needn't handle non-finite values.
Results may differ from a plain program's by a relative error of at most 0.0003.
Values sent between devices are 32-bit elements; how exact they have to be, the bound alone decides.
No kernel may reach another device: no remote copies, remote signals or barrier semaphores. Data moves between devices by JAX's collectives and lax.ppermute only.
A program may use at most 64 MiB of HBM per device.

v0:
```python
import jax
import jax.numpy as jnp
from jax import lax
from jax.sharding import PartitionSpec as P

TBX = 2
BY = 4
BZ = 4
SWEEPS = 2
FILTER_SWEEPS = 2


KMIN = 0.01
HEAT = 0.05
RADIUS2 = 2.0


def padded(shard, sides, width):
    for axis, dim in sides:
        size, length = (lax.axis_size(axis), shard.shape[dim])
        up = [(i, (i + 1) % size) for i in range(size - 1)]
        down = [(j, i) for i, j in up]
        last = lax.slice_in_dim(shard, length - width, length, axis=dim)
        initial = lax.slice_in_dim(shard, 0, width, axis=dim)
        before = lax.ppermute(last, axis, up)
        after = lax.ppermute(initial, axis, down)
        shard = jnp.concatenate([before, shard, after], axis=dim)
    return shard


def face_tables(brick_edge):
    face_cells = brick_edge * brick_edge
    cell = jnp.arange(face_cells, dtype=jnp.int32)
    column = cell % brick_edge
    row_of = cell // brick_edge
    lane = jnp.arange(brick_edge, dtype=jnp.int32)
    same_row = row_of[:, None] == lane[None, :]
    pick_west = (same_row & (column[:, None] == 0)).astype(jnp.float32)
    pick_east = (same_row & (column[:, None] == brick_edge - 1)).astype(jnp.float32)
    half_edge = brick_edge // 2
    coarse_cell = row_of // 2 * half_edge + column // 2
    shrink = jnp.where(
        coarse_cell[:, None] == jnp.arange(half_edge * half_edge, dtype=jnp.int32)[None, :],
        0.125,
        0.0,
    ).astype(jnp.float32)
    return (pick_west, pick_east, shrink)


def lane_product(field_data, table):
    return jnp.einsum("szc,ch->szh", field_data, table, precision=lax.Precision.HIGHEST)


def own_faces(field_data, pick_west, pick_east):
    slot_count, brick_edge, face_cells = field_data.shape
    return (
        lane_product(field_data, pick_west),
        lane_product(field_data, pick_east),
        field_data[:, :, :brick_edge],
        field_data[:, :, face_cells - brick_edge :],
        field_data[:, 0, :].reshape(slot_count, brick_edge, brick_edge),
        field_data[:, brick_edge - 1, :].reshape(slot_count, brick_edge, brick_edge),
    )


def adjacent_holder(field_data, far_faces, pick_west, pick_east):
    slot_count, brick_edge, face_cells = field_data.shape
    column = jnp.arange(face_cells, dtype=jnp.int32) % brick_edge
    placed_east = lane_product(far_faces[0], pick_east.T)
    placed_west = lane_product(far_faces[1], pick_west.T)
    shifted = jnp.concatenate([field_data[:, :, 1:], field_data[:, :, :1]], axis=2)
    east = jnp.where(column == brick_edge - 1, placed_east, shifted)
    shifted = jnp.concatenate([field_data[:, :, -1:], field_data[:, :, :-1]], axis=2)
    west = jnp.where(column == 0, placed_west, shifted)
    north = jnp.concatenate([field_data[:, :, brick_edge:], far_faces[2]], axis=2)
    south = jnp.concatenate([far_faces[3], field_data[:, :, :-brick_edge]], axis=2)
    upper = jnp.concatenate(
        [field_data[:, 1:], far_faces[4].reshape(slot_count, 1, face_cells)], axis=1
    )
    lower = jnp.concatenate(
        [far_faces[5].reshape(slot_count, 1, face_cells), field_data[:, :-1]], axis=1
    )
    return (east, west, north, south, upper, lower)


def select_rows(boundary_layers, slot_rows):
    picked = boundary_layers[jnp.clip(slot_rows, 0)]
    return jnp.where((slot_rows >= 0)[:, None, None], picked, 0.0)


def brick_grid(blocks, slot_map):
    picked = select_rows(blocks.reshape(blocks.shape[0], blocks.shape[1], -1), slot_map)
    depth_cells, height_cells, width_cells = blocks.shape[1:]
    shaped = picked.reshape(BZ, BY, TBX, depth_cells, height_cells, width_cells).transpose(
        0, 3, 1, 4, 2, 5
    )
    return shaped.reshape(BZ * depth_cells, BY * height_cells, TBX * width_cells)


def relax(extended, rhs_planes):
    middle = extended[1:-1]
    zero_row = jnp.zeros_like(middle[:, :1])
    zero_col = jnp.zeros_like(middle[:, :, :1])
    near = extended[2:] + extended[:-2]
    near = (
        near
        + jnp.concatenate([middle[:, 1:], zero_row], axis=1)
        + jnp.concatenate([zero_row, middle[:, :-1]], axis=1)
    )
    near = (
        near
        + jnp.concatenate([middle[:, :, 1:], zero_col], axis=2)
        + jnp.concatenate([zero_col, middle[:, :, :-1]], axis=2)
    )
    return (rhs_planes + RADIUS2 * near) / (1.0 + 6.0 * RADIUS2)


def per_device(
    material_fraction, primal_heat_solution, dual_load, dual_prior_design, holder_cube_location
):
    slot_count, brick_edge, face_cells = material_fraction.shape
    coarse_edge = brick_edge // 2
    spot_count = TBX * BY * BZ
    pick_west, pick_east, shrink = face_tables(brick_edge)
    active = holder_cube_location >= 0
    position = jnp.maximum(holder_cube_location, 0)
    brick_x = position % TBX
    brick_y = position // TBX % BY
    brick_z = position // (TBX * BY)
    matches = holder_cube_location[:, None] == jnp.arange(spot_count, dtype=jnp.int32)[None, :]
    slot_ids = jnp.arange(slot_count, dtype=jnp.int32)[:, None]
    slot_map = jnp.where(
        jnp.any(matches, axis=0), jnp.sum(jnp.where(matches, slot_ids, 0), axis=0), -1
    )
    rows_x = jnp.arange(BZ * BY, dtype=jnp.int32)
    rows_z = jnp.arange(BY * TBX, dtype=jnp.int32)
    x_low = slot_map[rows_x * TBX]
    x_high = slot_map[rows_x * TBX + TBX - 1]
    z_low = slot_map[rows_z]
    z_high = slot_map[(BZ - 1) * BY * TBX + rows_z]

    def plan_index(step_x, step_y, step_z, cross_width):
        near_x = brick_x + step_x
        near_y = brick_y + step_y
        near_z = brick_z + step_z
        inside = (
            (near_x >= 0)
            & (near_x < TBX)
            & (near_y >= 0)
            & (near_y < BY)
            & (near_z >= 0)
            & (near_z < BZ)
        )
        target = slot_map[jnp.clip((near_z * BY + near_y) * TBX + near_x, 0, spot_count - 1)]
        blank_row = slot_count + cross_width
        local_row = jnp.where(inside & (target >= 0), target, blank_row)
        if step_x != 0:
            crossing = (near_x < 0) | (near_x >= TBX)
            cross_row = brick_z * BY + brick_y
        elif step_z != 0:
            crossing = (near_z < 0) | (near_z >= BZ)
            cross_row = brick_y * TBX + brick_x
        else:
            crossing = jnp.zeros_like(active)
            cross_row = jnp.zeros_like(brick_x)
        chosen = jnp.where(crossing, slot_count + cross_row, local_row)
        return jnp.where(active, chosen, blank_row)

    plans = (
        plan_index(1, 0, 0, BZ * BY),
        plan_index(-1, 0, 0, BZ * BY),
        plan_index(0, 1, 0, 0),
        plan_index(0, -1, 0, 0),
        plan_index(0, 0, 1, BY * TBX),
        plan_index(0, 0, -1, BY * TBX),
    )
    zero_face = jnp.zeros((1, brick_edge, brick_edge), jnp.float32)

    def trade_boundary_layers(fields):
        owned = [own_faces(item, pick_west, pick_east) for item in fields]
        send_x = jnp.stack(
            [
                jnp.stack(
                    [
                        select_rows(boundary_layers[0], x_low),
                        select_rows(boundary_layers[1], x_high),
                    ]
                )
                for boundary_layers in owned
            ]
        )
        send_z = jnp.stack(
            [
                jnp.stack(
                    [
                        select_rows(boundary_layers[4], z_low),
                        select_rows(boundary_layers[5], z_high),
                    ]
                )
                for boundary_layers in owned
            ]
        )
        channels = len(fields)
        send_x = send_x.reshape(channels, 2, BZ * BY, face_cells)
        send_z = send_z.reshape(channels, 2, BY * TBX, face_cells)
        moved_x = padded(send_x, (("ba", 1),), 1)
        moved_z = padded(send_z, (("gz", 1),), 1)
        result = []
        for channel, boundary_layers in enumerate(owned):
            x_prev = moved_x[channel, 0].reshape(BZ * BY, brick_edge, brick_edge)
            x_next = moved_x[channel, 3].reshape(BZ * BY, brick_edge, brick_edge)
            z_prev = moved_z[channel, 0].reshape(BY * TBX, brick_edge, brick_edge)
            z_next = moved_z[channel, 3].reshape(BY * TBX, brick_edge, brick_edge)
            tables = (
                jnp.concatenate([boundary_layers[0], x_next, zero_face]),
                jnp.concatenate([boundary_layers[1], x_prev, zero_face]),
                jnp.concatenate([boundary_layers[2], zero_face]),
                jnp.concatenate([boundary_layers[3], zero_face]),
                jnp.concatenate([boundary_layers[4], z_next, zero_face]),
                jnp.concatenate([boundary_layers[5], z_prev, zero_face]),
            )
            result.append(tuple((tables[direction][plans[direction]] for direction in range(6))))
        return result

    active_three = active[:, None, None]
    thermal_kappa_cells = jnp.where(
        active_three,
        KMIN + (1.0 - KMIN) * material_fraction * material_fraction * material_fraction,
        0.0,
    )
    rhs = jnp.where(active_three, dual_load, 0.0)
    foreign_kappa_layers, foreign_heat_layers, foreign_dual_layers = trade_boundary_layers(
        (thermal_kappa_cells, primal_heat_solution, dual_prior_design)
    )
    adjacent_kappa_value = adjacent_holder(
        thermal_kappa_cells, foreign_kappa_layers, pick_west, pick_east
    )
    weights = [
        2.0
        * thermal_kappa_cells
        * kappa_adjacent_cell
        / jnp.maximum(thermal_kappa_cells + kappa_adjacent_cell, KMIN)
        for kappa_adjacent_cell in adjacent_kappa_value
    ]
    total = HEAT
    for weight in weights:
        total = total + weight
    dual_solution = dual_prior_design
    for sweep_index in range(SWEEPS):
        if sweep_index > 0:
            foreign_dual_layers = trade_boundary_layers((dual_solution,))[0]
        adjacent_dual_value = adjacent_holder(
            dual_solution, foreign_dual_layers, pick_west, pick_east
        )
        flux = rhs
        for weight, value_near in zip(weights, adjacent_dual_value):
            flux = flux + weight * value_near
        dual_solution = flux / total
    foreign_dual_layers = trade_boundary_layers((dual_solution,))[0]
    adjacent_heat_value = adjacent_holder(
        primal_heat_solution, foreign_heat_layers, pick_west, pick_east
    )
    adjacent_dual_value = adjacent_holder(dual_solution, foreign_dual_layers, pick_west, pick_east)
    cumulative_sum = jnp.zeros_like(material_fraction)
    for kappa_adjacent_cell, heat_adjacent_cell, dual_adjacent_cell in zip(
        adjacent_kappa_value, adjacent_heat_value, adjacent_dual_value
    ):
        cumulative_sum = cumulative_sum + jnp.where(
            kappa_adjacent_cell > 0,
            (heat_adjacent_cell - primal_heat_solution) * (dual_adjacent_cell - dual_solution),
            0.0,
        )
    sens = jnp.where(
        thermal_kappa_cells > 0,
        -1.5 * (1.0 - KMIN) * material_fraction * material_fraction * cumulative_sum,
        0.0,
    )
    paired = sens.reshape(slot_count, coarse_edge, 2, face_cells).sum(axis=2)
    restricted_grid = lane_product(paired, shrink).reshape(
        slot_count, coarse_edge, coarse_edge, coarse_edge
    )
    region = brick_grid(restricted_grid, slot_map)
    slab = lax.all_to_all(region, "ba", split_axis=0, concat_axis=2, tiled=True)
    smoothed = slab
    for filter_index in range(FILTER_SWEEPS):
        extended = padded(smoothed, ((("gz", "ba"), 0),), 1)
        smoothed = relax(extended, slab)
    return (dual_solution, smoothed)


def solution(mesh):
    in_specs = (
        P(("gz", "ba"), None, None),
        P(("gz", "ba"), None, None),
        P(("gz", "ba"), None, None),
        P(("gz", "ba"), None, None),
        P(("gz", "ba")),
    )
    out_specs = (P(("gz", "ba"), None, None), P(("gz", "ba"), None, None))
    return jax.shard_map(
        per_device, mesh=mesh, in_specs=in_specs, out_specs=out_specs, check_vma=False
    )
```

profile of v0, /device:TPU:4, one launch (start us, length us, event | category | flops | bytes accessed | tf_op | source)
XLA Modules:
  0.0 285.2 jit_solution(8354101377838119366)
XLA Ops:
  12.6 3.3 %collective-permute-start.2 = (f32[3,1,8,1024]{3,2,1,0:T(8,128)}, f32[3,1,8,1024]{3,2,1,0:T(8,128)}, u32[]{:S(2)}, u32[]{:S(2)}) collective-permute-start(f32[3,1,8,1024]{3,2,1,0:T(8,128)} %get-tuple-element.93), channel_id=1, source_target_pairs={{8,0},{16,8},{24,16},{9,1},{17,9},{25,17},{10,2},{18,10},{26,18},{... | collective-permute-start | bytes 294920 | tf_op jit(solution)/shard_map/ppermute | solution.py:26
  16.0 3.1 %collective-permute-start.3 = (f32[3,1,8,1024]{3,2,1,0:T(8,128)}, f32[3,1,8,1024]{3,2,1,0:T(8,128)}, u32[]{:S(2)}, u32[]{:S(2)}) collective-permute-start(f32[3,1,8,1024]{3,2,1,0:T(8,128)} %get-tuple-element.92), channel_id=1, source_target_pairs={{0,8},{8,16},{16,24},{1,9},{9,17},{17,25},{2,10},{10,18},{18,26},{... | collective-permute-start | bytes 294920 | tf_op jit(solution)/shard_map/ppermute | solution.py:25
  33.8 3.7 %collective-permute-start.1 = (f32[3,1,16,1024]{3,2,1,0:T(8,128)}, f32[3,1,16,1024]{3,2,1,0:T(8,128)}, u32[]{:S(2)}, u32[]{:S(2)}) collective-permute-start(f32[3,1,16,1024]{3,2,1,0:T(8,128)} %get-tuple-element.85), channel_id=1, source_target_pairs={{0,1},{1,2},{2,3},{3,4},{4,5},{5,6},{6,7},{8,9},{9,10},{10,11},{11... | collective-permute-start | bytes 589832 | tf_op jit(solution)/shard_map/ppermute | solution.py:25
  77.2 1.6 fusion.152
  81.4 1.7 reshape_squeeze.92
  83.0 1.7 reshape_squeeze.93
  84.7 2.7 pad_maximum_fusion.3
  87.4 1.6 gather_fusion.12
  89.0 2.1 gather_fusion.13
  92.7 2.2 gather_fusion.10
  97.6 1.6 fusion.8
  99.2 3.8 %fusion.7 = f32[4,32,1024]{2,1,0:T(8,128)S(1)} fusion(f32[4,32,1024]{2,1,0:T(8,128)S(1)} %fusion.8, f32[4,32,32]{2,1,0:T(8,128)S(1)} %copy-done.43, f32[4,32,1]{2,1,0:T(8,128)} %get-tuple-element.82, f32[4,32,1023]{2,1,0:T(8,128)} %get-tuple-element.80, f32[4,32,32]{2,1,0:T(8,128)S(1)} %copy-done.40, f32[4,32,992]{2,1,0:T(8,128)} %get-tuple-element.153, ...), kind=kOutput, calls=%fused_computation.89 | convolution fusion | flops 58130432 | bytes 7885828 | tf_op jit(solution)/shard_map/szc,ch->szh/dot_general | solution.py:51
  109.1 3.6 %collective-permute-start.6 = (f32[1,1,8,1024]{3,2,1,0:T(8,128)S(1)}, f32[1,1,8,1024]{3,2,1,0:T(8,128)S(1)}, u32[]{:S(2)}, u32[]{:S(2)}) collective-permute-start(f32[1,1,8,1024]{3,2,1,0:T(8,128)S(1)} %broadcast_select_fusion.13), channel_id=1, source_target_pairs={{8,0},{16,8},{24,16},{9,1},{17,9},{25,17},{10,2},{18,10},{26,18},{... | collective-permute-start | bytes 98312 | tf_op jit(solution)/shard_map/ppermute | solution.py:26
  113.5 2.2 collective-permute-start.7
  117.3 2.7 collective-permute-start.5
  125.4 2.3 gather_fusion.47
  127.7 2.3 gather_fusion.44
  130.9 1.6 gather_fusion.43
  136.9 1.6 gather_fusion.37
  138.6 1.7 gather_fusion.35
  141.9 3.9 %fusion.16 = f32[4,32,1024]{2,1,0:T(8,128)S(1)} fusion(f32[4,32,1024]{2,1,0:T(8,128)S(1)} %fusion.17, f32[4,32,32]{2,1,0:T(8,128)S(1)} %gather_fusion.35, f32[4,32,1]{2,1,0:T(8,128)} %get-tuple-element.62, f32[4,32,1023]{2,1,0:T(8,128)} %get-tuple-element.60, f32[4,32,32]{2,1,0:T(8,128)S(1)} %copy-done.41, f32[4,32,992]{2,1,0:T(8,128)} %get-tuple-element.59, ...), kind=kOutput, calls=%fused_computation.98 | convolution fusion | flops 58130432 | bytes 7885828 | tf_op jit(solution)/shard_map/szc,ch->szh/dot_general | solution.py:51
  153.6 4.5 %collective-permute-start.10 = (f32[1,1,8,1024]{3,2,1,0:T(8,128)}, f32[1,1,8,1024]{3,2,1,0:T(8,128)}, u32[]{:S(2)}, u32[]{:S(2)}) collective-permute-start(f32[1,1,8,1024]{3,2,1,0:T(8,128)} %broadcast_select_fusion.11), channel_id=1, source_target_pairs={{8,0},{16,8},{24,16},{9,1},{17,9},{25,17},{10,2},{18,10},{26,18},{... | collective-permute-start | bytes 98312 | tf_op jit(solution)/shard_map/ppermute | solution.py:26
  160.9 1.9 collective-permute-start.11
  165.9 3.4 %collective-permute-start.9 = (f32[1,1,16,1024]{3,2,1,0:T(8,128)}, f32[1,1,16,1024]{3,2,1,0:T(8,128)}, u32[]{:S(2)}, u32[]{:S(2)}) collective-permute-start(f32[1,1,16,1024]{3,2,1,0:T(8,128)} %broadcast_select_fusion), channel_id=1, source_target_pairs={{0,1},{1,2},{2,3},{3,4},{4,5},{5,6},{6,7},{8,9},{9,10},{10,11},{11... | collective-permute-start | bytes 196616 | tf_op jit(solution)/shard_map/ppermute | solution.py:25
  179.8 2.1 pad_maximum_fusion.10
  181.8 1.6 gather_fusion.56
  184.1 1.6 gather_fusion.57
  186.4 1.6 gather_fusion.59
  188.7 1.6 gather_fusion.54
  192.0 1.7 reshape_squeeze.111
  193.7 1.9 pad_maximum_fusion.2
  195.7 2.3 gather_fusion.46
  198.0 2.3 gather_fusion.49
  200.4 1.6 fusion.28
  202.1 1.7 fusion.32
  205.6 2.6 fusion.27
  210.7 2.7 gather.306
  213.4 5.3 %copy.32 = f32[4,4,2,16,16,16]{4,1,5,2,3,0:T(4,128)} copy(f32[4,4,2,16,16,16]{5,4,3,2,1,0:T(8,128)} %gather.306) | data formatting | bytes 1048576 | tf_op jit(solution)/shard_map/gather | solution.py:87
  218.7 6.3 %select_bitcast_fusion = f32[4,16,4,16,2,16]{3,2,5,4,1,0:T(4,128)} fusion(f32[4,4,2,16,16,16]{4,1,5,2,3,0:T(4,128)} %copy.32, pred[4,4,2]{1,2,0:T(4,128)(4,1)S(1)} %copy-done.55), kind=kLoop, calls=%fused_computation.61 | loop fusion | flops 131072 | bytes 1048608 | tf_op jit(solution)/shard_map/transpose | solution.py:94
  225.0 3.7 %reshape.683 = f32[64,64,32]{1,2,0:T(8,128)S(1)} reshape(f32[4,16,4,16,2,16]{3,2,5,4,1,0:T(4,128)} %select_bitcast_fusion) | data formatting | bytes 1048576 | tf_op jit(solution)/shard_map/reshape | solution.py:97
  229.4 22.7 %all_to_all.18 = f32[8,1,16384]{2,1,0:T(1,128)S(1)} all-to-all(f32[8,1,16384]{2,1,0:T(1,128)S(1)} %reshape.1242), channel_id=1, replica_groups=mesh['gz'=4,'ba'=8] {'ba'}, dimensions={0} | all-to-all | bytes 1048576 | tf_op jit(solution)/shard_map/all_to_all | solution.py:283
  252.6 1.9 reduce.20
  255.4 5.2 %collective-permute-start.12 = (f32[1,64,256]{1,2,0:T(8,128)S(1)}, f32[1,64,256]{1,2,0:T(8,128)S(1)}, u32[]{:S(2)}, u32[]{:S(2)}) collective-permute-start(f32[1,64,256]{1,2,0:T(8,128)S(1)} %bitcast.120), channel_id=1, source_target_pairs={{1,0},{2,1},{3,2},{4,3},{5,4},{6,5},{7,6},{8,7},{9,8},{10,9},{11,1... | collective-permute-start | bytes 196616 | tf_op jit(solution)/shard_map/ppermute | solution.py:26
  260.6 1.9 collective-permute-start.13
  263.6 6.8 %collective-permute-done.13 = f32[1,64,256]{1,2,0:T(8,128)S(1)} collective-permute-done((f32[1,64,256]{1,2,0:T(8,128)S(1)}, f32[1,64,256]{1,2,0:T(8,128)S(1)}, u32[]{:S(2)}, u32[]{:S(2)}) %collective-permute-start.13) | collective-permute-done | bytes 65568 | tf_op jit(solution)/shard_map/ppermute | solution.py:25
  271.5 1.9 collective-permute-start.14
  273.5 2.4 collective-permute-start.15
  276.1 7.3 %collective-permute-done.15 = f32[1,64,256]{1,2,0:T(8,128)S(1)} collective-permute-done((f32[1,64,256]{1,2,0:T(8,128)S(1)}, f32[1,64,256]{1,2,0:T(8,128)S(1)}, u32[]{:S(2)}, u32[]{:S(2)}) %collective-permute-start.15) | collective-permute-done | bytes 65568 | tf_op jit(solution)/shard_map/ppermute | solution.py:25
  (404 shorter events, 131.0 us)
Async XLA Ops:
  0.6 18.5 %copy-start.3 = (f32[4,32,1024]{2,1,0:T(8,128)S(1)}, f32[4,32,1024]{2,1,0:T(8,128)}, u32[]{:S(2)}) copy-start(f32[4,32,1024]{2,1,0:T(8,128)} %param.5) | copy-start | bytes 1572868
  0.6 19.0 %copy-start.1 = (f32[4,32,1024]{2,1,0:T(8,128)S(1)}, f32[4,32,1024]{2,1,0:T(8,128)}, u32[]{:S(2)}) copy-start(f32[4,32,1024]{2,1,0:T(8,128)} %param.6) | copy-start | bytes 1572868
  2.9 18.0 %copy-start.65 = (pred[4]{0:T(512)(128)(4,1)}, pred[4]{0:T(512)(128)(4,1)S(1)}, u32[]{:S(2)}) copy-start(pred[4]{0:T(512)(128)(4,1)S(1)} %broadcast_compare_fusion.9) | copy-start | bytes 16
  4.1 16.8 %copy-start.56 = (pred[8]{0:T(512)(128)(4,1)}, pred[8]{0:T(512)(128)(4,1)S(1)}, u32[]{:S(2)}) copy-start(pred[8]{0:T(512)(128)(4,1)S(1)} %broadcast_compare_fusion.1) | copy-start | bytes 28
  4.8 16.9 %copy-start.58 = (pred[8]{0:T(512)(128)(4,1)}, pred[8]{0:T(512)(128)(4,1)S(1)}, u32[]{:S(2)}) copy-start(pred[8]{0:T(512)(128)(4,1)S(1)} %broadcast_compare_fusion.2) | copy-start | bytes 28
  8.8 10.4 %copy-start.17 = (f32[4,32,32]{2,1,0:T(8,128)}, f32[4,32,32]{2,1,0:T(8,128)S(1)}, u32[]{:S(2)}) copy-start(f32[4,32,32]{2,1,0:T(8,128)S(1)} %reshape_squeeze.96) | copy-start | bytes 49156
  9.5 10.9 %copy-start.18 = (f32[4,32,32]{2,1,0:T(8,128)}, f32[4,32,32]{2,1,0:T(8,128)S(1)}, u32[]{:S(2)}) copy-start(f32[4,32,32]{2,1,0:T(8,128)S(1)} %reshape_squeeze.97) | copy-start | bytes 49156
  12.6 51.9 %collective-permute-start.2 = (f32[3,1,8,1024]{3,2,1,0:T(8,128)}, f32[3,1,8,1024]{3,2,1,0:T(8,128)}, u32[]{:S(2)}, u32[]{:S(2)}) collective-permute-start(f32[3,1,8,1024]{3,2,1,0:T(8,128)} %get-tuple-element.93), channel_id=1, source_target_pairs={{8,0},{16,8},{24,16},{9,1},{17,9},{25,17},{10,2},{18,10},{26,18},{... | collective-permute-start | bytes 294920 | tf_op jit(solution)/shard_map/ppermute | solution.py:26
  16.0 49.3 %collective-permute-start.3 = (f32[3,1,8,1024]{3,2,1,0:T(8,128)}, f32[3,1,8,1024]{3,2,1,0:T(8,128)}, u32[]{:S(2)}, u32[]{:S(2)}) collective-permute-start(f32[3,1,8,1024]{3,2,1,0:T(8,128)} %get-tuple-element.92), channel_id=1, source_target_pairs={{0,8},{8,16},{16,24},{1,9},{9,17},{17,25},{2,10},{10,18},{18,26},{... | collective-permute-start | bytes 294920 | tf_op jit(solution)/shard_map/ppermute | solution.py:25
  25.8 11.6 %copy-start.67 = (s32[4]{0:T(128)S(1)}, s32[4]{0:T(128)}, u32[]{:S(2)}) copy-start(s32[4]{0:T(128)} %param.9) | copy-start | bytes 52
  32.5 43.7 %collective-permute-start = (f32[3,1,16,1024]{3,2,1,0:T(8,128)}, f32[3,1,16,1024]{3,2,1,0:T(8,128)}, u32[]{:S(2)}, u32[]{:S(2)}) collective-permute-start(f32[3,1,16,1024]{3,2,1,0:T(8,128)} %get-tuple-element.84), channel_id=1, source_target_pairs={{1,0},{2,1},{3,2},{4,3},{5,4},{6,5},{7,6},{9,8},{10,9},{11,10},{12... | collective-permute-start | bytes 589832 | tf_op jit(solution)/shard_map/ppermute | solution.py:26
  33.8 43.4 %collective-permute-start.1 = (f32[3,1,16,1024]{3,2,1,0:T(8,128)}, f32[3,1,16,1024]{3,2,1,0:T(8,128)}, u32[]{:S(2)}, u32[]{:S(2)}) collective-permute-start(f32[3,1,16,1024]{3,2,1,0:T(8,128)} %get-tuple-element.85), channel_id=1, source_target_pairs={{0,1},{1,2},{2,3},{3,4},{4,5},{5,6},{6,7},{8,9},{9,10},{10,11},{11... | collective-permute-start | bytes 589832 | tf_op jit(solution)/shard_map/ppermute | solution.py:25
  45.8 53.4 %copy-start.12 = (f32[4,32,992]{2,1,0:T(8,128)}, f32[4,32,992]{2,1,0:T(8,128)S(1)}, u32[]{:S(2)}) copy-start(f32[4,32,992]{2,1,0:T(8,128)S(1)} %get-tuple-element.66) | copy-start | bytes 1523716
  49.0 14.1 %copy-start.69 = (pred[32]{0:T(512)(128)(4,1)S(1)}, pred[32]{0:T(512)(128)(4,1)}, u32[]{:S(2)}) copy-start(pred[32]{0:T(512)(128)(4,1)} %get-tuple-element.16) | copy-start | bytes 100
  55.8 28.9 %copy-start.51 = (s32[1024]{0:T(1024)}, s32[1024]{0:T(1024)S(1)}, u32[]{:S(2)}) copy-start(s32[1024]{0:T(1024)S(1)} %pad_clamp_fusion.3) | copy-start | bytes 12292
  55.8 28.9 %copy-start.52 = (s32[1024]{0:T(1024)}, s32[1024]{0:T(1024)S(1)}, u32[]{:S(2)}) copy-start(s32[1024]{0:T(1024)S(1)} %pad_clamp_fusion.1) | copy-start | bytes 12292
  55.9 33.2 %copy-start.49 = (s32[1024]{0:T(1024)}, s32[1024]{0:T(1024)S(1)}, u32[]{:S(2)}) copy-start(s32[1024]{0:T(1024)S(1)} %pad_clamp_fusion.13) | copy-start | bytes 12292
  55.9 36.8 %copy-start.50 = (s32[1024]{0:T(1024)}, s32[1024]{0:T(1024)S(1)}, u32[]{:S(2)}) copy-start(s32[1024]{0:T(1024)S(1)} %pad_clamp_fusion.15) | copy-start | bytes 12292
  55.9 28.8 %copy-start.54 = (s32[1024]{0:T(1024)}, s32[1024]{0:T(1024)S(1)}, u32[]{:S(2)}) copy-start(s32[1024]{0:T(1024)S(1)} %pad_clamp_fusion.11) | copy-start | bytes 12292
  55.9 31.4 %copy-start.53 = (s32[1024]{0:T(1024)}, s32[1024]{0:T(1024)S(1)}, u32[]{:S(2)}) copy-start(s32[1024]{0:T(1024)S(1)} %pad_clamp_fusion.9) | copy-start | bytes 12292
  66.5 69.5 %copy-start.21 = (f32[1,32,32]{2,1,0:T(8,128)}, f32[1,32,32]{2,1,0:T(8,128)S(1)}, u32[]{:S(2)}) copy-start(f32[1,32,32]{2,1,0:T(8,128)S(1)} %broadcast_in_dim.336) | copy-start | bytes 12292
  68.9 26.0 %copy-start.16 = (f32[4,32,1023]{2,1,0:T(8,128)S(1)}, f32[4,32,1023]{2,1,0:T(8,128)}, u32[]{:S(2)}) copy-start(f32[4,32,1023]{2,1,0:T(8,128)} %get-tuple-element.71) | copy-start | bytes 1571332
  69.0 72.8 %copy-start.32 = (f32[4,1,1024]{2,1,0:T(1,128)}, f32[4,1,1024]{2,1,0:T(1,128)S(1)}, u32[]{:S(2)}) copy-start(f32[4,1,1024]{2,1,0:T(1,128)S(1)} %reshape.672) | copy-start | bytes 49156
  87.4 11.8 %copy-start.22 = (f32[4,32,32]{2,1,0:T(8,128)S(1)}, f32[4,32,32]{2,1,0:T(8,128)}, u32[]{:S(2)}) copy-start(f32[4,32,32]{2,1,0:T(8,128)} %gather_fusion.15) | copy-start | bytes 49156
  87.4 11.8 %copy-start.24 = (f32[4,32,32]{2,1,0:T(8,128)S(1)}, f32[4,32,32]{2,1,0:T(8,128)}, u32[]{:S(2)}) copy-start(f32[4,32,32]{2,1,0:T(8,128)} %gather_fusion.18) | copy-start | bytes 49156
  87.4 11.8 %copy-start.34 = (f32[4,1,1024]{2,1,0:T(1,128)S(1)}, f32[4,1,1024]{2,1,0:T(1,128)}, u32[]{:S(2)}) copy-start(f32[4,1,1024]{2,1,0:T(1,128)} %reshape.674) | copy-start | bytes 49156
  87.4 11.8 %copy-start.40 = (f32[4,32,32]{2,1,0:T(8,128)S(1)}, f32[4,32,32]{2,1,0:T(8,128)}, u32[]{:S(2)}) copy-start(f32[4,32,32]{2,1,0:T(8,128)} %gather_fusion.16) | copy-start | bytes 49156
  87.4 11.8 %copy-start.44 = (f32[4,1,1024]{2,1,0:T(1,128)S(1)}, f32[4,1,1024]{2,1,0:T(1,128)}, u32[]{:S(2)}) copy-start(f32[4,1,1024]{2,1,0:T(1,128)} %reshape.675) | copy-start | bytes 49156
  103.6 9.9 %copy-start.57 = (pred[8]{0:T(512)(128)(4,1)S(1)}, pred[8]{0:T(512)(128)(4,1)}, u32[]{:S(2)}) copy-start(pred[8]{0:T(512)(128)(4,1)} %copy-done.56) | copy-start | bytes 28
  104.0 12.6 %copy-start.63 = (pred[16]{0:T(512)(128)(4,1)S(1)}, pred[16]{0:T(512)(128)(4,1)}, u32[]{:S(2)}) copy-start(pred[16]{0:T(512)(128)(4,1)} %copy-done.62) | copy-start | bytes 52
  105.1 15.7 %copy-start.61 = (pred[16]{0:T(512)(128)(4,1)S(1)}, pred[16]{0:T(512)(128)(4,1)}, u32[]{:S(2)}) copy-start(pred[16]{0:T(512)(128)(4,1)} %copy-done.60) | copy-start | bytes 52
  109.1 20.9 %collective-permute-start.6 = (f32[1,1,8,1024]{3,2,1,0:T(8,128)S(1)}, f32[1,1,8,1024]{3,2,1,0:T(8,128)S(1)}, u32[]{:S(2)}, u32[]{:S(2)}) collective-permute-start(f32[1,1,8,1024]{3,2,1,0:T(8,128)S(1)} %broadcast_select_fusion.13), channel_id=1, source_target_pairs={{8,0},{16,8},{24,16},{9,1},{17,9},{25,17},{10,2},{18,10},{26,18},{... | collective-permute-start | bytes 98312 | tf_op jit(solution)/shard_map/ppermute | solution.py:26
  113.5 16.5 %collective-permute-start.7 = (f32[1,1,8,1024]{3,2,1,0:T(8,128)S(1)}, f32[1,1,8,1024]{3,2,1,0:T(8,128)S(1)}, u32[]{:S(2)}, u32[]{:S(2)}) collective-permute-start(f32[1,1,8,1024]{3,2,1,0:T(8,128)S(1)} %broadcast_select_fusion.12), channel_id=1, source_target_pairs={{0,8},{8,16},{16,24},{1,9},{9,17},{17,25},{2,10},{10,18},{18,26},{... | collective-permute-start | bytes 98312 | tf_op jit(solution)/shard_map/ppermute | solution.py:25
  117.3 16.7 %collective-permute-start.5 = (f32[1,1,16,1024]{3,2,1,0:T(8,128)}, f32[1,1,16,1024]{3,2,1,0:T(8,128)}, u32[]{:S(2)}, u32[]{:S(2)}) collective-permute-start(f32[1,1,16,1024]{3,2,1,0:T(8,128)} %broadcast_select_fusion.2), channel_id=1, source_target_pairs={{0,1},{1,2},{2,3},{3,4},{4,5},{5,6},{6,7},{8,9},{9,10},{10,11},{11... | collective-permute-start | bytes 196616 | tf_op jit(solution)/shard_map/ppermute | solution.py:25
  121.5 13.5 %collective-permute-start.4 = (f32[1,1,16,1024]{3,2,1,0:T(8,128)}, f32[1,1,16,1024]{3,2,1,0:T(8,128)}, u32[]{:S(2)}, u32[]{:S(2)}) collective-permute-start(f32[1,1,16,1024]{3,2,1,0:T(8,128)} %broadcast_select_fusion.3), channel_id=1, source_target_pairs={{1,0},{2,1},{3,2},{4,3},{5,4},{6,5},{7,6},{9,8},{10,9},{11,10},{12... | collective-permute-start | bytes 196616 | tf_op jit(solution)/shard_map/ppermute | solution.py:26
  145.8 59.5 %copy-start = (f32[4,32,1024]{2,1,0:T(8,128)}, f32[4,32,1024]{2,1,0:T(8,128)S(1)}, u32[]{:S(2)}) copy-start(f32[4,32,1024]{2,1,0:T(8,128)S(1)} %fusion.16) | copy-start | bytes 1572868
  153.6 24.4 %collective-permute-start.10 = (f32[1,1,8,1024]{3,2,1,0:T(8,128)}, f32[1,1,8,1024]{3,2,1,0:T(8,128)}, u32[]{:S(2)}, u32[]{:S(2)}) collective-permute-start(f32[1,1,8,1024]{3,2,1,0:T(8,128)} %broadcast_select_fusion.11), channel_id=1, source_target_pairs={{8,0},{16,8},{24,16},{9,1},{17,9},{25,17},{10,2},{18,10},{26,18},{... | collective-permute-start | bytes 98312 | tf_op jit(solution)/shard_map/ppermute | solution.py:26
  160.9 17.9 %collective-permute-start.11 = (f32[1,1,8,1024]{3,2,1,0:T(8,128)}, f32[1,1,8,1024]{3,2,1,0:T(8,128)}, u32[]{:S(2)}, u32[]{:S(2)}) collective-permute-start(f32[1,1,8,1024]{3,2,1,0:T(8,128)} %broadcast_select_fusion.10), channel_id=1, source_target_pairs={{0,8},{8,16},{16,24},{1,9},{9,17},{17,25},{2,10},{10,18},{18,26},{... | collective-permute-start | bytes 98312 | tf_op jit(solution)/shard_map/ppermute | solution.py:25
  165.9 25.2 %collective-permute-start.9 = (f32[1,1,16,1024]{3,2,1,0:T(8,128)}, f32[1,1,16,1024]{3,2,1,0:T(8,128)}, u32[]{:S(2)}, u32[]{:S(2)}) collective-permute-start(f32[1,1,16,1024]{3,2,1,0:T(8,128)} %broadcast_select_fusion), channel_id=1, source_target_pairs={{0,1},{1,2},{2,3},{3,4},{4,5},{5,6},{6,7},{8,9},{9,10},{10,11},{11... | collective-permute-start | bytes 196616 | tf_op jit(solution)/shard_map/ppermute | solution.py:25
  172.2 19.8 %collective-permute-start.8 = (f32[1,1,16,1024]{3,2,1,0:T(8,128)}, f32[1,1,16,1024]{3,2,1,0:T(8,128)}, u32[]{:S(2)}, u32[]{:S(2)}) collective-permute-start(f32[1,1,16,1024]{3,2,1,0:T(8,128)} %broadcast_select_fusion.1), channel_id=1, source_target_pairs={{1,0},{2,1},{3,2},{4,3},{5,4},{6,5},{7,6},{9,8},{10,9},{11,10},{12... | collective-permute-start | bytes 196616 | tf_op jit(solution)/shard_map/ppermute | solution.py:26
  191.0 14.3 %copy-start.66 = (pred[4]{0:T(512)(128)(4,1)S(1)}, pred[4]{0:T(512)(128)(4,1)}, u32[]{:S(2)}) copy-start(pred[4]{0:T(512)(128)(4,1)} %copy-done.65) | copy-start | bytes 16
  195.6 9.7 %copy-start.27 = (f32[4,32,32]{2,1,0:T(8,128)S(1)}, f32[4,32,32]{2,1,0:T(8,128)}, u32[]{:S(2)}) copy-start(f32[4,32,32]{2,1,0:T(8,128)} %gather_fusion.52) | copy-start | bytes 49156
  195.6 9.7 %copy-start.28 = (f32[4,32,32]{2,1,0:T(8,128)S(1)}, f32[4,32,32]{2,1,0:T(8,128)}, u32[]{:S(2)}) copy-start(f32[4,32,32]{2,1,0:T(8,128)} %gather_fusion.44) | copy-start | bytes 49156
  195.7 9.7 %copy-start.29 = (f32[4,32,32]{2,1,0:T(8,128)S(1)}, f32[4,32,32]{2,1,0:T(8,128)}, u32[]{:S(2)}) copy-start(f32[4,32,32]{2,1,0:T(8,128)} %gather_fusion.51) | copy-start | bytes 49156
  255.4 8.2 %collective-permute-start.12 = (f32[1,64,256]{1,2,0:T(8,128)S(1)}, f32[1,64,256]{1,2,0:T(8,128)S(1)}, u32[]{:S(2)}, u32[]{:S(2)}) collective-permute-start(f32[1,64,256]{1,2,0:T(8,128)S(1)} %bitcast.120), channel_id=1, source_target_pairs={{1,0},{2,1},{3,2},{4,3},{5,4},{6,5},{7,6},{8,7},{9,8},{10,9},{11,1... | collective-permute-start | bytes 196616 | tf_op jit(solution)/shard_map/ppermute | solution.py:26
  260.6 9.9 %collective-permute-start.13 = (f32[1,64,256]{1,2,0:T(8,128)S(1)}, f32[1,64,256]{1,2,0:T(8,128)S(1)}, u32[]{:S(2)}, u32[]{:S(2)}) collective-permute-start(f32[1,64,256]{1,2,0:T(8,128)S(1)} %bitcast.119), channel_id=1, source_target_pairs={{0,1},{1,2},{2,3},{3,4},{4,5},{5,6},{6,7},{7,8},{8,9},{9,10},{10,1... | collective-permute-start | bytes 196616 | tf_op jit(solution)/shard_map/ppermute | solution.py:25
  271.5 4.5 %collective-permute-start.14 = (f32[1,64,256]{1,2,0:T(8,128)S(1)}, f32[1,64,256]{1,2,0:T(8,128)S(1)}, u32[]{:S(2)}, u32[]{:S(2)}) collective-permute-start(f32[1,64,256]{1,2,0:T(8,128)S(1)} %get-tuple-element.26), channel_id=1, source_target_pairs={{1,0},{2,1},{3,2},{4,3},{5,4},{6,5},{7,6},{8,7},{9,8},{10,9},{11,1... | collective-permute-start | bytes 196616 | tf_op jit(solution)/shard_map/ppermute | solution.py:26
  273.5 9.9 %collective-permute-start.15 = (f32[1,64,256]{1,2,0:T(8,128)S(1)}, f32[1,64,256]{1,2,0:T(8,128)S(1)}, u32[]{:S(2)}, u32[]{:S(2)}) collective-permute-start(f32[1,64,256]{1,2,0:T(8,128)S(1)} %get-tuple-element.27), channel_id=1, source_target_pairs={{0,1},{1,2},{2,3},{3,4},{4,5},{5,6},{6,7},{7,8},{8,9},{9,10},{10,1... | collective-permute-start | bytes 196616 | tf_op jit(solution)/shard_map/ppermute | solution.py:25
  (38 other events, 235.6 us)
where the time goes:
time: 288 us; the launch traced here: 285 us
  local copies, waits for them, and re-layouts  140 us (49%)
  starting transfers between devices  43.9 us (15%)
  other arithmetic  33.2 us (12%)
  matrix products  27.2 us (9%)
  blocking collectives  22.7 us (8%)
  waiting for transfers between devices  15.1 us (5%)
    gather x30, local copies, waits for them, and re-layouts, trade_boundary_layers(): tables[direction][plans[direction]]  45.9 us
    dot_general x21, matrix products, lane_product(): jnp.einsum('szc,ch->szh', field_data, table, precision=lax.Precision.HIGH...  27.2 us
    gather x47, local copies, waits for them, and re-layouts, select_rows(): picked = boundary_layers[jnp.clip(slot_rows, 0)]  26.8 us
    all_to_all x1, blocking collectives, per_device(): slab = lax.all_to_all(region, 'ba', split_axis=0, concat_axis=2, tiled=True)  22.7 us
    ppermute x8, starting transfers between devices, padded(): after = lax.ppermute(initial, axis, down)  22.6 us
    ppermute x8, starting transfers between devices, padded(): before = lax.ppermute(last, axis, up)  21.3 us
    ppermute x8, waiting for transfers between devices, padded(): before = lax.ppermute(last, axis, up)  14.1 us
    select_n x10, other arithmetic, select_rows(): return jnp.where((slot_rows >= 0)[:, None, None], picked, 0.0)  8.4 us
  transfers between devices with their start and end apart: 16, of which 3 were waited for; matrix products, arithmetic and copies ran while one was open for 34% of the time, Pallas kernels for 0%

commit v1 on v0

v1 whole, which is shorter than its diff:
```python
import functools

import jax
import jax.numpy as jnp
from jax import lax
from jax.experimental import pallas as pl
from jax.experimental.pallas import tpu as pltpu
from jax.sharding import PartitionSpec as P

SLOTS = 4
KMIN = 0.01
HEAT = 0.05
F32 = jnp.float32
I32 = jnp.int32

Z_UP = 128
Z_DOWN = 152
SLAB = 176
SLAB_SIZE = 22
ZERO = 220
TILES = 252
X_TILES = 49
Z_SLABS = 96
Z_TILES = 115
DUMMY = 29


def lanes():
    return lax.broadcasted_iota(I32, (8, 128), 1)


def rows():
    return lax.broadcasted_iota(I32, (8, 128), 0)


def take(tile, index):
    return jnp.take_along_axis(tile, index, axis=1)


def row_of(values):
    lane = lanes()
    result = jnp.zeros((8, 128), F32)
    for index, value in enumerate(values):
        result = jnp.where(lane == index, (value + 1).astype(F32), result)
    return result


def position_at(meta, index):
    return meta[0, 0, index].astype(I32) - 1


def as_int(flag):
    return jnp.where(flag, 1, 0).astype(I32)


def pack_kernel(place, parity_ref, mat, heat, load, prior, near, far, up, down):
    parity = parity_ref[0]
    lane = lanes()
    depth = lane // 32
    inside = 32 * (lane % 4)
    pick = (lane % 32) // 4
    first = place[0] >= 0
    start = as_int(place[SLOTS - 1] >= 0)
    low = inside + depth
    high = inside + 31 - depth
    near_side = jnp.where(parity == 0, high, low)
    far_side = jnp.where(parity == 0, low, high)
    last_low = inside + jnp.where(depth == 3, 0, depth)
    last_high = inside + 31 - jnp.where(depth == 3, 0, depth)
    near_last = jnp.where(parity == 0, last_high, last_low)
    far_last = jnp.where(parity == 0, last_low, last_high)

    def slab(unit, carry):
        row = pl.multiple_of(unit * 8, 8)
        for field, ref in enumerate((mat, prior)):
            for out, side in ((near, near_side), (far, far_side)):
                tile = jnp.zeros((8, 128), F32)
                for j in range(8):
                    got = take(ref[pl.ds(row, 8), 128 * j : 128 * j + 128], side)
                    tile = jnp.where(pick == j, got, tile)
                out[field * 16 + unit] = tile
        for out, side in ((near, near_last), (far, far_last)):
            tile = jnp.zeros((8, 128), F32)
            for j in range(8):
                got = jnp.where(
                    depth == 3,
                    take(heat[pl.ds(row, 8), 128 * j : 128 * j + 128], side),
                    take(load[pl.ds(row, 8), 128 * j : 128 * j + 128], side),
                )
                tile = jnp.where(pick == j, got, tile)
            out[32 + unit] = tile
        return carry

    lax.fori_loop(0, 16, slab, 0)
    meta = row_of([place[s] for s in range(SLOTS)])
    near[48] = meta
    far[48] = meta
    for field, ref in enumerate((mat, prior, load, heat)):
        for i in range(3):
            top = pl.multiple_of((start + i) * 32 + 24, 8)
            for j in range(8):
                up[(field * 3 + i) * 8 + j] = ref[pl.ds(top, 8), 128 * j : 128 * j + 128]
                down[(field * 3 + i) * 8 + j] = ref[32 * i : 32 * i + 8, 128 * j : 128 * j + 128]


def corner_kernel(
    place, near_meta, far_meta, near, far, up_in, down_in, up, down, meta_tile, sems
):
    del up_in, down_in
    values = [place[s] for s in range(SLOTS)]
    copies = []
    for b, (meta, source) in enumerate(((near_meta, near), (far_meta, far))):
        listed = [position_at(meta, s) for s in range(SLOTS)]
        values = values + listed
        start = as_int(listed[SLOTS - 1] >= 0)
        for field in range(3):
            for i in range(3):
                to = Z_SLABS + b * 9 + field * 3 + i
                copies.append((source.at[field * 16 + (start + i) * 4 + 3], up.at[to]))
                copies.append((source.at[field * 16 + i * 4], down.at[to]))
    meta_tile[...] = row_of(values)
    copies.append((meta_tile, up.at[Z_TILES - 1]))
    copies.append((meta_tile, down.at[Z_TILES - 1]))
    started = [
        pltpu.make_async_copy(source, target, sems.at[index])
        for index, (source, target) in enumerate(copies)
    ]
    for copy in started:
        copy.start()
    for copy in started:
        copy.wait()


def conduct(own, beside):
    return (2.0 * own) * beside / jnp.maximum(own + beside, KMIN)


def main_kernel(
    parts,
    place,
    parity_ref,
    near_meta,
    far_meta,
    up_meta,
    down_meta,
    mat,
    heat,
    load,
    prior,
    near,
    far,
    z_up,
    z_down,
    dual_out,
    chunks,
    cells,
    brick_table,
    slab_table,
    kappa,
    temperature,
    source,
    dual0,
    dual1,
    dual2,
    weights,
    inverse,
    sens,
    summed,
    turned,
):
    parity = parity_ref[0]
    lane = lanes()
    row = rows()

    def clear(index, carry):
        cells[index] = ZERO
        return carry

    lax.fori_loop(0, 144, clear, 0, unroll=8)

    def cell_of(x, y, z):
        return ((z + 1) * 6 + y + 1) * 4 + x + 1

    def enter(position, wanted, x, z, tile):
        here = jnp.where(wanted, cell_of(x, position // 2 % 4, z), 144)
        cells[here] = tile
        return jnp.where(wanted, here, DUMMY)

    own = [place[s] for s in range(SLOTS)]
    own_cell = [
        enter(q, q >= 0, q % 2, q // 8, 32 * s) for s, q in enumerate(own)
    ]
    lists_up = [[position_at(up_meta, 4 * k + s) for s in range(SLOTS)] for k in range(3)]
    lists_down = [[position_at(down_meta, 4 * k + s) for s in range(SLOTS)] for k in range(3)]

    def shifted(listed):
        full = listed[SLOTS - 1] >= 0
        return [jnp.where(full, listed[i + 1], listed[i]) for i in range(3)]

    ups = [listed[:3] for listed in lists_up]
    downs = [shifted(listed) for listed in lists_down]
    up_cell = [
        enter(q, (q >= 0) & (q < 8), q % 2, 4, Z_UP + 8 * i) for i, q in enumerate(ups[0])
    ]
    down_cell = [
        enter(q, q >= 24, q % 2, -1, Z_DOWN + 8 * i) for i, q in enumerate(downs[0])
    ]
    slab_cell = []
    for b, meta in enumerate((near_meta, far_meta)):
        east = parity == b
        column = jnp.where(east, 0, 1)
        x = jnp.where(east, 2, -1)
        base = SLAB + SLAB_SIZE * b
        mine = [position_at(meta, s) for s in range(SLOTS)]
        slab_cell.append(
            [
                enter(q, (q >= 0) & (q % 2 == column), x, q // 8, base + 4 * s)
                for s, q in enumerate(mine)
            ]
            + [
                enter(q, (q >= 0) & (q < 8) & (q % 2 == column), x, 4, base + 16 + i)
                for i, q in enumerate(ups[1 + b])
            ]
            + [
                enter(q, (q >= 24) & (q % 2 == column), x, -1, base + 19 + i)
                for i, q in enumerate(downs[1 + b])
            ]
        )

    def set_brick(unit, up, down, north, south, east, west, px):
        for k, value in enumerate((up, down, north, south, east, west, px)):
            brick_table[unit * 8 + k] = value

    for s in range(SLOTS):
        here = own_cell[s]
        px = jnp.where(own[s] >= 0, own[s] % 2, 0)
        lift = jnp.where(own[s] >= 8, 24, 0)
        north, south = (cells[here + 4], cells[here - 4])
        east, west = (cells[here + 1], cells[here - 1])
        above, below = (cells[here + 24], cells[here - 24] + lift)
        for c in range(4):
            base = s * 32 + c * 8
            set_brick(
                s * 4 + c,
                base + 8 if c < 3 else above,
                base - 8 if c > 0 else below,
                north + 8 * c,
                south + 8 * c,
                east + jnp.where(px == 1, c, 8 * c),
                west + jnp.where(px == 0, c, 8 * c),
                px,
            )
    for k, (listed, cell_list) in enumerate(((ups[0], up_cell), (downs[0], down_cell))):
        for i in range(3):
            here = cell_list[i]
            px = jnp.where(listed[i] >= 0, listed[i] % 2, 0)
            set_brick(
                16 + 3 * k + i,
                ZERO if k == 0 else cells[here + 24],
                cells[here - 24] + 24 if k == 0 else ZERO,
                cells[here + 4],
                cells[here - 4],
                cells[here + 1],
                cells[here - 1],
                px,
            )

    def set_slab(unit, up, down, north, south, face):
        for k, value in enumerate((up, down, north, south, face)):
            slab_table[unit * 8 + k] = value

    for b, meta in enumerate((near_meta, far_meta)):
        inward = jnp.where(parity == b, -1, 1)
        for s in range(SLOTS):
            here = slab_cell[b][s]
            lift = jnp.where(position_at(meta, s) >= 8, 3, 0)
            north, south = (cells[here + 4], cells[here - 4])
            above, below = (cells[here + 24], cells[here - 24] + lift)
            face = cells[here + inward]
            for c in range(4):
                unit = SLAB_SIZE * b + 4 * s + c
                set_slab(
                    unit,
                    SLAB + unit + 1 if c < 3 else above,
                    SLAB + unit - 1 if c > 0 else below,
                    north + c,
                    south + c,
                    face + 8 * c,
                )
        for i in range(6):
            here = slab_cell[b][4 + i]
            set_slab(
                SLAB_SIZE * b + 16 + i,
                ZERO if i < 3 else cells[here + 24],
                cells[here - 24] + 3 if i < 3 else ZERO,
                cells[here + 4],
                cells[here - 4],
                cells[here + inward],
            )

    zeros = jnp.zeros((8, 128), F32)
    for ref in (kappa, temperature, dual0, dual1, dual2):
        for t in range(32):
            ref[ZERO + t] = zeros

    def conductivity(fraction):
        return KMIN + (1.0 - KMIN) * fraction * fraction * fraction

    def own_unit(unit, carry):
        at = pl.multiple_of(unit * 8, 8)
        active = place[unit // 4] >= 0
        for j in range(8):
            span = slice(128 * j, 128 * j + 128)
            t = unit * 8 + j
            kappa[t] = jnp.where(active, conductivity(mat[pl.ds(at, 8), span]), 0.0)
            source[t] = jnp.where(active, load[pl.ds(at, 8), span], 0.0)
            dual0[t] = prior[pl.ds(at, 8), span]
            temperature[t] = heat[pl.ds(at, 8), span]
        return carry

    lax.fori_loop(0, 16, own_unit, 0)

    def halo_tile(t, carry):
        for to, message in ((Z_UP, z_up), (Z_DOWN, z_down)):
            kappa[to + t] = conductivity(message[t])
            dual0[to + t] = message[24 + t]
            source[to + t] = message[48 + t]
            temperature[to + t] = message[72 + t]
        return carry

    lax.fori_loop(0, 24, halo_tile, 0, unroll=4)

    def slab_tile(to, message, at, step):
        third = message[at + 2 * step]
        kappa[to] = conductivity(message[at])
        dual0[to] = message[at + step]
        source[to] = third
        temperature[to] = pltpu.roll(third, 32, 1)

    for b, message in enumerate((near, far)):
        base = SLAB + SLAB_SIZE * b

        def side_tile(t, carry):
            slab_tile(base + t, message, t, 16)
            return carry

        lax.fori_loop(0, 16, side_tile, 0, unroll=4)
        for i in range(3):
            slab_tile(base + 16 + i, z_up, Z_SLABS + 9 * b + i, 3)
            slab_tile(base + 19 + i, z_down, Z_SLABS + 9 * b + i, 3)

    top_row = row == 0
    last_row = row == 7
    x_cell = lane % 32
    y_block = lane // 32

    def above_of(tile, other):
        return pltpu.roll(jnp.where(top_row, other, tile), 7, 0)

    def below_of(tile, other):
        return pltpu.roll(jnp.where(last_row, other, tile), 1, 0)

    def brick_unit(unit):
        up, down, north, south, east, west, px = (brick_table[unit * 8 + k] for k in range(7))
        inner = 1 - px
        east_index = jnp.where(px == 1, y_block, jnp.maximum(lane - 31, 0))
        west_index = jnp.where(px == 0, y_block, jnp.minimum(lane + 31, 127))

        def around(ref, j):
            base = unit * 8
            tile = ref[base + j]
            after = ref[base + j + 1] if j < 7 else ref[north]
            before = ref[base + j - 1] if j > 0 else ref[south + 7]
            over = take(ref[east + inner * j], east_index + 4 * j * px)
            under = take(ref[west + px * j], west_index + 4 * j * inner)
            return tile, (
                jnp.where(x_cell == 31, over, pltpu.roll(tile, 127, 1)),
                jnp.where(x_cell == 0, under, pltpu.roll(tile, 1, 1)),
                pltpu.roll(jnp.where(lane < 32, after, tile), 96, 1),
                pltpu.roll(jnp.where(lane >= 96, before, tile), 32, 1),
                above_of(tile, ref[up + j]),
                below_of(tile, ref[down + j]),
            )

        return around

    def slab_unit(unit, column):
        up, down, north, south, face = (slab_table[unit * 8 + k] for k in range(5))
        index = 32 * (lane % 4) + column
        block = lane // 4

        def around(ref):
            tile = ref[SLAB + unit]
            edge = take(ref[face], index)
            for j in range(1, 8):
                edge = jnp.where(block == j, take(ref[face + j], index), edge)
            return tile, (
                pltpu.roll(tile, 96, 1),
                jnp.where(lane < 32, edge, pltpu.roll(tile, 32, 1)),
                jnp.where(x_cell == 31, pltpu.roll(ref[north], 31, 1), pltpu.roll(tile, 127, 1)),
                jnp.where(x_cell == 0, pltpu.roll(ref[south], 97, 1), pltpu.roll(tile, 1, 1)),
                above_of(tile, ref[up]),
                below_of(tile, ref[down]),
            )

        return around

    def first_sweep(t, own_kappa, beside_kappa, beside):
        total = jnp.full((8, 128), HEAT, F32)
        flux = source[t]
        for k in range(6):
            weight = conduct(own_kappa, beside_kappa[k])
            weights[k * TILES + t] = weight
            total = total + weight
            flux = flux + weight * beside[k]
        scale = 1.0 / total
        inverse[t] = scale
        dual1[t] = flux * scale

    def later_sweep(t, beside):
        flux = source[t]
        for k in range(6):
            flux = flux + weights[k * TILES + t] * beside[k]
        return flux * inverse[t]

    def slabs(body):
        for b in range(2):
            column = jnp.where(parity == b, 31, 0)

            def two(step, carry):
                for k in range(2):
                    unit = SLAB_SIZE * b + 2 * step + k
                    body(SLAB + unit, slab_unit(unit, column))
                return carry

            lax.fori_loop(0, SLAB_SIZE // 2, two, 0)

    def brick_first(unit, carry):
        around = brick_unit(unit)
        for j in range(8):
            own_kappa, beside_kappa = around(kappa, j)
            first_sweep(unit * 8 + j, own_kappa, beside_kappa, around(dual0, j)[1])
        return carry

    lax.fori_loop(0, 22, brick_first, 0)

    def slab_first(t, around):
        own_kappa, beside_kappa = around(kappa)
        first_sweep(t, own_kappa, beside_kappa, around(dual0)[1])

    slabs(slab_first)

    def brick_second(unit, carry):
        around = brick_unit(unit)
        for j in range(8):
            dual2[unit * 8 + j] = later_sweep(unit * 8 + j, around(dual1, j)[1])
        return carry

    lax.fori_loop(0, 22, brick_second, 0)

    def slab_second(t, around):
        dual2[t] = later_sweep(t, around(dual1)[1])

    slabs(slab_second)

    def sensitivity(unit, carry):
        around = brick_unit(unit)
        at = pl.multiple_of(unit * 8, 8)
        for j in range(8):
            t = unit * 8 + j
            dual, duals = around(dual2, j)
            warm, warms = around(temperature, j)
            total = jnp.zeros((8, 128), F32)
            for k in range(6):
                total = total + jnp.where(
                    weights[k * TILES + t] > 0, (warms[k] - warm) * (duals[k] - dual), 0.0
                )
            fraction = sens[pl.ds(at, 8), 128 * j : 128 * j + 128]
            sens[pl.ds(at, 8), 128 * j : 128 * j + 128] = (
                -1.5 * (1.0 - KMIN) * fraction * fraction * total
            )
        return carry

    def stage_own(unit, carry):
        at = pl.multiple_of(unit * 8, 8)
        sens[pl.ds(at, 8), :] = mat[pl.ds(at, 8), :]
        for j in range(8):
            dual_out[pl.ds(at, 8), 128 * j : 128 * j + 128] = dual2[unit * 8 + j]
        return carry

    lax.fori_loop(0, 16, stage_own, 0)
    for k, message in enumerate((z_up, z_down)):
        for i in range(3):
            for j in range(8):
                at = 128 + 24 * k + 8 * i
                sens[at : at + 8, 128 * j : 128 * j + 128] = message[8 * i + j]
    lax.fori_loop(0, 22, sensitivity, 0)

    cell = lax.broadcasted_iota(I32, (512, 128), 0)
    coarse = lax.broadcasted_iota(I32, (512, 128), 1)
    matches = (cell // 64 == coarse // 16) & (cell % 32 // 2 == coarse % 16)
    shrink = jnp.where(matches, 0.125, 0.0).astype(F32)
    for half in range(2):
        summed[...] = jnp.dot(
            sens[:, 512 * half : 512 * half + 512],
            shrink,
            precision=lax.Precision.HIGHEST,
            preferred_element_type=F32,
        )
        for r in range(11):
            tile = summed[pl.ds(16 * r, 8, stride=2), :] + summed[pl.ds(16 * r + 1, 8, stride=2), :]
            for bit in (1, 2, 4):
                low_row = (row & bit) == 0
                low_lane = (lane & (16 * bit)) == 0
                swap_a = pltpu.roll(pltpu.roll(tile, 8 - bit, 0), 16 * bit, 1)
                swap_b = pltpu.roll(pltpu.roll(tile, bit, 0), 128 - 16 * bit, 1)
                tile = jnp.where(low_row == low_lane, tile, jnp.where(low_row, swap_a, swap_b))
            turned[2 * r + half] = tile

    planes = 64 // parts
    level = [jnp.where(q >= 0, q // 8, 9) for q in own]

    def count(test):
        return functools.reduce(lambda a, b: a + b, [as_int(test(v)) for v in level])

    before = [count(lambda v, z=z: v < z) for z in range(5)]

    def nth(z, e):
        index = before[z] + e
        valid = index < before[z + 1]
        slot = jnp.minimum(index, SLOTS - 1)
        code = jnp.where(valid, place[slot] - 8 * z, -1)
        return slot, code

    for d in range(parts):
        z = d * planes // 16
        half = d * planes % 16 // 8
        codes = []
        for e in range(3):
            slot, code = nth(z, e)
            codes.append(code)
            for k in range(2):
                chunks[d * 8 + 2 * e + k] = turned[(slot * 2 + half) * 2 + k]
        start = d * planes % 8 == 0
        end = (d + 1) * planes % 8 == 0
        if planes >= 8:
            outside = -1 if half == 0 else 1
        else:
            outside = -1 if start else 1 if end else 0
        beyond = half + outside
        beside = [zeros, zeros]
        for e in range(3):
            if outside == 0:
                tile_at, lane_at, code = (0, 0, jnp.int32(-1))
            elif beyond in (0, 1):
                slot, code = nth(z, e)
                tile_at, lane_at = (slot * 2 + beyond, 96 if outside < 0 else 0)
            elif 0 <= z + outside <= 3:
                slot, code = nth(z + outside, e)
                tile_at, lane_at = (slot * 2 + (1 if outside < 0 else 0), 96 if outside < 0 else 0)
            elif outside < 0:
                q = downs[0][e]
                code = jnp.where(q >= 24, q - 24, -1)
                tile_at, lane_at = (8 + (3 + e) // 2, 64 * ((3 + e) % 2) + 32)
            else:
                q = ups[0][e]
                code = jnp.where((q >= 0) & (q < 8), q, -1)
                tile_at, lane_at = (8 + e // 2, 64 * (e % 2))
            codes.append(code)
            for k in range(2):
                tile = turned[tile_at * 2 + k]
                shift = (32 * e - lane_at) % 128
                if shift:
                    tile = pltpu.roll(tile, shift, 1)
                beside[k] = jnp.where(y_block == e, tile, beside[k])
        for e, code in enumerate(codes):
            beside[0] = jnp.where(lane == 96 + e, (code + 1).astype(F32), beside[0])
        for k in range(2):
            chunks[d * 8 + 6 + k] = beside[k]


def filter_kernel(parts, planes, across, spot, meta, received, swapped, out, grid, once):
    member = spot[0]
    depth = planes + 4
    wide = parts // across
    lane = lanes()
    row = rows()
    group_lane = lane // 16
    zeros = jnp.zeros((8, 128), F32)

    def clear(index, carry):
        grid[index] = zeros
        return carry

    lax.fori_loop(0, depth * 8 * wide, clear, 0, unroll=8)
    begin = member * planes
    half = begin % 16 // 8
    side = jnp.where(begin % 8 == 0, 0, planes + 2) if planes < 8 else half * (planes + 2)

    def place_plane(tile, lane_at, window, code, k, column, tile_x):
        at = (column * 2 + code % 2) % 8
        moved = pltpu.roll(tile, (at * 16 - lane_at + 256) % 128, 1)
        where_to = (window * 8 + code // 2 * 2 + k) * wide + tile_x
        grid[where_to] = jnp.where(group_lane == at, moved, grid[where_to])

    def from_device(column, carry):
        tile_x = column // across
        for e in range(3):
            code = meta[column, 0, 0, 96 + e].astype(I32) - 1

            @pl.when(code >= 0)
            def _(e=e, code=code):
                for k in range(2):
                    tile = received[column * 8 + 2 * e + k]
                    if planes == 8:
                        for p in range(8):
                            place_plane(tile, 16 * p, p + 2, code, k, column, tile_x)
                        other = swapped[column * 8 + 2 * e + k]
                        for p in range(2):
                            place_plane(
                                other,
                                jnp.where(half == 0, 16 * p, 96 + 16 * p),
                                jnp.where(half == 0, 10 + p, p),
                                code,
                                k,
                                column,
                                tile_x,
                            )
                    else:
                        for window in range(depth):
                            p = begin % 8 + window - 2

                            @pl.when((p >= 0) & (p < 8))
                            def _(tile=tile, p=p, window=window, k=k):
                                place_plane(tile, 16 * p, window, code, k, column, tile_x)

        for e in range(3):
            code = meta[column, 0, 0, 99 + e].astype(I32) - 1

            @pl.when(code >= 0)
            def _(e=e, code=code):
                for k in range(2):
                    tile = received[column * 8 + 6 + k]
                    for p in range(2):
                        place_plane(
                            tile, 32 * e + 16 * p, side + p, code, k, column, tile_x
                        )

        return carry

    lax.fori_loop(0, parts, from_device, 0)

    def relax(ref, window, y, x):
        here = (window * 8 + y) * wide + x
        tile = ref[here]
        north = ref[here + wide] if y < 7 else zeros
        south = ref[here - wide] if y > 0 else zeros
        east = ref[here + 1] if x < wide - 1 else zeros
        west = ref[here - 1] if x > 0 else zeros
        near = ref[here + 8 * wide] + ref[here - 8 * wide]
        near = near + pltpu.roll(jnp.where(row == 0, north, tile), 7, 0)
        near = near + pltpu.roll(jnp.where(row == 7, south, tile), 1, 0)
        near = near + pltpu.roll(jnp.where(lane == 0, east, tile), 127, 1)
        near = near + pltpu.roll(jnp.where(lane == 127, west, tile), 1, 1)
        return (grid[here] + 2.0 * near) * (1.0 / 13.0)

    first = spot[1] == 0
    last = spot[1] == spot[2] - 1

    def sweep_once(window, carry):
        gone = (first & (window < 2)) | (last & (window >= planes + 2))
        keep = jnp.where(gone, 0.0, 1.0).astype(F32)
        for y in range(8):
            for x in range(wide):
                once[(window * 8 + y) * wide + x] = relax(grid, window, y, x) * keep
        return carry

    lax.fori_loop(1, depth - 1, sweep_once, 0)

    def sweep_again(window, carry):
        for y in range(8):
            for x in range(wide):
                out[window - 2, 8 * y : 8 * y + 8, 128 * x : 128 * x + 128] = relax(
                    once, window, y, x
                )
        return carry

    lax.fori_loop(2, depth - 2, sweep_again, 0)


VMEM = pl.BlockSpec(memory_space=pltpu.VMEM)
SMEM = pl.BlockSpec(memory_space=pltpu.SMEM)
ANY = pl.BlockSpec(memory_space=pl.ANY)
BIG = 48 * 1024 * 1024


def meta_of(index):
    return pl.BlockSpec((1, 8, 128), lambda i: (index, 0, 0), memory_space=pltpu.SMEM)


def params():
    return pltpu.CompilerParams(vmem_limit_bytes=BIG)


def tiles(count):
    return jax.ShapeDtypeStruct((count, 8, 128), F32)


def per_device(
    material_fraction, primal_heat_solution, dual_load, dual_prior_design, holder_cube_location
):
    parts = lax.axis_size("ba")
    groups = lax.axis_size("gz")
    member = lax.axis_index("ba")
    group = lax.axis_index("gz")
    planes = 64 // parts
    parity = (member % 2).reshape(1).astype(I32)
    place = holder_cube_location
    fields = [
        field.reshape(128, 1024)
        for field in (material_fraction, primal_heat_solution, dual_load, dual_prior_design)
    ]
    near, far, up, down = pl.pallas_call(
        pack_kernel,
        out_shape=(tiles(X_TILES), tiles(X_TILES), tiles(Z_TILES), tiles(Z_TILES)),
        in_specs=[SMEM, SMEM, VMEM, VMEM, VMEM, VMEM],
        out_specs=(VMEM, VMEM, VMEM, VMEM),
        compiler_params=params(),
        name="pack",
    )(place, parity, *fields)
    inner = [(i, i ^ 1) for i in range(parts)]
    outer = [(i, i + 1 if i % 2 else i - 1) for i in range(1, parts - 1)]
    near = lax.ppermute(near, "ba", inner)
    far = lax.ppermute(far, "ba", outer)
    up, down = pl.pallas_call(
        corner_kernel,
        out_shape=(tiles(Z_TILES), tiles(Z_TILES)),
        in_specs=[SMEM, meta_of(X_TILES - 1), meta_of(X_TILES - 1), ANY, ANY, ANY, ANY],
        out_specs=(ANY, ANY),
        input_output_aliases={5: 0, 6: 1},
        scratch_shapes=[pltpu.VMEM((8, 128), F32), pltpu.SemaphoreType.DMA((38,))],
        grid=(1,),
        compiler_params=params(),
        name="corners",
    )(place, near, far, near, far, up, down)
    rising = [(i, i + 1) for i in range(groups - 1)]
    falling = [(i + 1, i) for i in range(groups - 1)]
    from_below = lax.ppermute(up, "gz", rising)
    from_above = lax.ppermute(down, "gz", falling)
    meta_z = meta_of(Z_TILES - 1)
    meta_x = meta_of(X_TILES - 1)
    field_tiles = pltpu.VMEM((TILES, 8, 128), F32)
    dual, chunks = pl.pallas_call(
        functools.partial(main_kernel, parts),
        out_shape=(jax.ShapeDtypeStruct((128, 1024), F32), tiles(8 * parts)),
        in_specs=[SMEM, SMEM, meta_x, meta_x, meta_z, meta_z] + [VMEM] * 8,
        out_specs=(VMEM, VMEM),
        scratch_shapes=[
            pltpu.SMEM((145,), I32),
            pltpu.SMEM((22 * 8,), I32),
            pltpu.SMEM((44 * 8,), I32),
            field_tiles,
            field_tiles,
            field_tiles,
            field_tiles,
            field_tiles,
            field_tiles,
            pltpu.VMEM((6 * TILES, 8, 128), F32),
            field_tiles,
            pltpu.VMEM((176, 1024), F32),
            pltpu.VMEM((176, 128), F32),
            pltpu.VMEM((22, 8, 128), F32),
        ],
        grid=(1,),
        compiler_params=params(),
        name="sweeps",
    )(
        place,
        parity,
        near,
        far,
        from_above,
        from_below,
        *fields,
        near,
        far,
        from_above,
        from_below,
    )
    received = lax.all_to_all(chunks, "ba", split_axis=0, concat_axis=0, tiled=True)
    swapped = lax.ppermute(received, "ba", inner) if planes == 8 else received
    spot = jnp.stack([member, group * parts + member, jnp.int32(groups * parts)]).astype(I32)
    wide = 32 * parts // 128
    filtered = pl.pallas_call(
        functools.partial(filter_kernel, parts, planes, 4),
        out_shape=jax.ShapeDtypeStruct((planes, 64, 32 * parts), F32),
        in_specs=[
            SMEM,
            pl.BlockSpec(
                (parts, 1, 8, 128), lambda i: (0, 6, 0, 0), memory_space=pltpu.SMEM
            ),
            VMEM,
            VMEM,
        ],
        out_specs=VMEM,
        scratch_shapes=[
            pltpu.VMEM(((planes + 4) * 8 * wide, 8, 128), F32),
            pltpu.VMEM(((planes + 4) * 8 * wide, 8, 128), F32),
        ],
        grid=(1,),
        compiler_params=params(),
        name="smooth",
    )(spot, received.reshape(parts, 8, 8, 128), received, swapped)
    return (dual.reshape(material_fraction.shape), filtered)


def solution(mesh):
    spec = P(("gz", "ba"), None, None)
    return jax.shard_map(
        per_device,
        mesh=mesh,
        in_specs=(spec, spec, spec, spec, P(("gz", "ba"))),
        out_specs=(spec, spec),
        check_vma=False,
    )
```

time: 288 us -> 87.9 us (0.31)
  local copies, waits for them, and re-layouts: 140 us -> 4.82 us
  starting transfers between devices: 43.9 us -> 6.62 us
  Pallas kernels: 0 us -> 34.3 us
  other arithmetic: 33.2 us -> 0.08 us
  matrix products: 27.2 us -> 0 us
    gather x87 -> x0, local copies, waits for them, and re-layouts: 79.1 us -> none  [the longest x30 45.9 us: trade_boundary_layers(): tables[direction][plans[direction]]]
    ppermute x16 -> x5, starting transfers between devices: 43.9 us -> 6.62 us  [the longest x1 3.34 us: per_device(): from_above = lax.ppermute(down, 'gz', falling)]
    pallas_call x0 -> x4, Pallas kernels: none -> 34.3 us  [the longest x1 23.9 us: per_device(): pl.pallas_call(functools.partial(main_kernel, parts), out_shape=(jax.Shap...]
    slice x40 -> x0, local copies, waits for them, and re-layouts: 27.8 us -> none  [the longest x5 5.5 us: adjacent_holder(): field_data[:, :, 1:]]
    dot_general x21 -> x0, matrix products: 27.2 us -> none  [lane_product(): jnp.einsum('szc,ch->szh', field_data, table, precision=lax.Precision.HIGH...]
    another operation x30 -> x0, local copies, waits for them, and re-layouts: 15.2 us -> none  [the longest x5 6.2 us: trade_boundary_layers(): x_prev = moved_x[channel, 0].reshape(BZ * BY, brick_edge, brick_edge)]
    reshape x12 -> x0, local copies, waits for them, and re-layouts: 9.74 us -> none  [the longest x1 3.71 us: brick_grid(): shaped.reshape(BZ * depth_cells, BY * height_cells, TBX * width_cells)]
    select_n x18 -> x0, other arithmetic: 9.64 us -> none  [the longest x10 8.4 us: select_rows(): return jnp.where((slot_rows >= 0)[:, None, None], picked, 0.0)]
  transfers between devices with their start and end apart: 16 -> 5, of which waited for: 3 -> 4; matrix products, arithmetic and copies ran while one was open for 34% -> 0% of each run, Pallas kernels for 0% -> 0%
where the time goes in v1:
time: 87.9 us; the launch traced here: 86.9 us
  Pallas kernels  34.3 us (39%)
  blocking collectives  24.5 us (28%)
  waiting for transfers between devices  15.9 us (18%)
  starting transfers between devices  6.62 us (8%)
  local copies, waits for them, and re-layouts  4.82 us (5%)
    all_to_all x1, blocking collectives, per_device(): lax.all_to_all(chunks, 'ba', split_axis=0, concat_axis=0, tiled=True)  24.5 us
    pallas_call x1, Pallas kernels, per_device(): pl.pallas_call(functools.partial(main_kernel, parts), out_shape=(jax.Shap...  23.9 us
    ppermute x1, waiting for transfers between devices, per_device(): from_below = lax.ppermute(up, 'gz', rising)  9.1 us
    pallas_call x1, Pallas kernels, per_device(): pl.pallas_call(functools.partial(filter_kernel, parts, planes, 4), out_sh...  5.96 us
    unnamed x14, local copies, waits for them, and re-layouts  4.82 us
    ppermute x1, waiting for transfers between devices, per_device(): from_above = lax.ppermute(down, 'gz', falling)  4.62 us
    ppermute x1, starting transfers between devices, per_device(): from_above = lax.ppermute(down, 'gz', falling)  3.34 us
    pallas_call x1, Pallas kernels, per_device(): pl.pallas_call(pack_kernel, out_shape=(tiles(X_TILES), tiles(X_TILES), ti...  3.11 us
  transfers between devices with their start and end apart: 5, of which 4 were waited for; matrix products, arithmetic and copies ran while one was open for 0% of the time, Pallas kernels for 0%

profile of v1, /device:TPU:4, one launch (start us, length us, event | category | flops | bytes accessed | tf_op | source)
XLA Modules:
  0.0 86.9 jit_solution(11085446044767455962)
XLA Ops:
  0.6 0.0 copy-start.6
  0.7 0.6 copy-done.6
  1.3 0.0 copy-start
  1.3 1.0 %copy-done = f32[4,32,1024]{2,1,0:T(8,128)S(1)} copy-done((f32[4,32,1024]{2,1,0:T(8,128)S(1)}, f32[4,32,1024]{2,1,0:T(8,128)}, u32[]{:S(2)}) %copy-start) | copy-done | bytes 524312
  2.3 0.0 copy-start.2
  2.3 1.0 %copy-done.2 = f32[4,32,1024]{2,1,0:T(8,128)S(1)} copy-done((f32[4,32,1024]{2,1,0:T(8,128)S(1)}, f32[4,32,1024]{2,1,0:T(8,128)}, u32[]{:S(2)}) %copy-start.2) | copy-done | bytes 524312
  3.4 0.0 copy-start.4
  3.4 1.0 %copy-done.4 = f32[4,32,1024]{2,1,0:T(8,128)S(1)} copy-done((f32[4,32,1024]{2,1,0:T(8,128)S(1)}, f32[4,32,1024]{2,1,0:T(8,128)}, u32[]{:S(2)}) %copy-start.4) | copy-done | bytes 524312
  4.4 0.0 copy-start.5
  4.4 1.0 %copy-done.5 = f32[4,32,1024]{2,1,0:T(8,128)S(1)} copy-done((f32[4,32,1024]{2,1,0:T(8,128)S(1)}, f32[4,32,1024]{2,1,0:T(8,128)}, u32[]{:S(2)}) %copy-start.5) | copy-done | bytes 524312
  5.5 3.1 %pack.1 = (f32[49,8,128]{2,1,0:T(8,128)S(1)}, f32[49,8,128]{2,1,0:T(8,128)S(1)}, f32[115,8,128]{2,1,0:T(8,128)S(1)}, f32[115,8,128]{2,1,0:T(8,128)S(1)}) custom-call(s32[4]{0:T(128)S(1)} %copy-done.6, s32[1]{0:T(128)} %bitcast.parity_ref, f32[128,1024]{1,0:T(8,128)S(1)} %bitcast.10, f32[128,1024]{1,0:T(8,128)S(1)} %bitcast.12, f32[128,1024]{1,0:T(8,128)S(1)} %bitcast.14, ...), custom_call_target="tpu_custom_call" | custom-call | tf_op jit(solution)/shard_map/pack/pallas_call | solution.py:723
  8.6 0.1 collective-permute-start
  8.7 0.7 collective-permute-start.1
  9.3 0.8 collective-permute-done.near_meta.near
  10.1 0.0 collective-permute-done.1.far_meta.far
  10.1 0.0 copy-start.1
  10.1 0.0 copy-start.3
  10.1 1.3 %corners.1 = (f32[115,8,128]{2,1,0:T(8,128)S(1)}, f32[115,8,128]{2,1,0:T(8,128)S(1)}) custom-call(s32[4]{0:T(128)S(1)} %copy-done.6, f32[49,8,128]{2,1,0:T(8,128)S(1)} %collective-permute-done.near_meta.near, f32[49,8,128]{2,1,0:T(8,128)S(1)} %collective-permute-done.1.far_meta.far, ...), custom_call_target="tpu_custom_call", output_to_operand_aliasing={{0}: (5, {}), {1}: (6, {})} | custom-call | tf_op jit(solution)/shard_map/corners/pallas_call | solution.py:735
  11.4 3.3 %collective-permute-start.2 = (f32[115,8,128]{2,1,0:T(8,128)S(1)}, f32[115,8,128]{2,1,0:T(8,128)S(1)}, u32[]{:S(2)}, u32[]{:S(2)}) collective-permute-start(f32[115,8,128]{2,1,0:T(8,128)S(1)} %get-tuple-element.14), channel_id=1, source_target_pairs={{8,0},{16,8},{24,16},{9,1},{17,9},{25,17},{10,2},{18,10},{26,18},{... | collective-permute-start | bytes 1413128 | tf_op jit(solution)/shard_map/ppermute | solution.py:749
  14.8 2.5 %collective-permute-start.3 = (f32[115,8,128]{2,1,0:T(8,128)S(1)}, f32[115,8,128]{2,1,0:T(8,128)S(1)}, u32[]{:S(2)}, u32[]{:S(2)}) collective-permute-start(f32[115,8,128]{2,1,0:T(8,128)S(1)} %get-tuple-element.15), channel_id=1, source_target_pairs={{0,8},{8,16},{16,24},{1,9},{9,17},{17,25},{2,10},{10,18},{18,26},{... | collective-permute-start | bytes 1413128 | tf_op jit(solution)/shard_map/ppermute | solution.py:748
  17.3 4.6 %collective-permute-done.2.up_meta.z_up = f32[115,8,128]{2,1,0:T(8,128)S(1)} collective-permute-done((f32[115,8,128]{2,1,0:T(8,128)S(1)}, f32[115,8,128]{2,1,0:T(8,128)S(1)}, u32[]{:S(2)}, u32[]{:S(2)}) %collective-permute-start.2) | collective-permute-done | bytes 471072 | tf_op jit(solution)/shard_map/ppermute | solution.py:749
  21.9 9.1 %collective-permute-done.3.down_meta.z_down = f32[115,8,128]{2,1,0:T(8,128)S(1)} collective-permute-done((f32[115,8,128]{2,1,0:T(8,128)S(1)}, f32[115,8,128]{2,1,0:T(8,128)S(1)}, u32[]{:S(2)}, u32[]{:S(2)}) %collective-permute-start.3) | collective-permute-done | bytes 471072 | tf_op jit(solution)/shard_map/ppermute | solution.py:748
  31.0 0.0 copy-done.1
  31.0 0.0 copy-done.3
  31.0 23.9 %sweeps.1 = (f32[128,1024]{1,0:T(8,128)}, f32[64,8,128]{2,1,0:T(8,128)S(1)}) custom-call(s32[4]{0:T(128)S(1)} %copy-done.6, s32[1]{0:T(128)} %bitcast.parity_ref, f32[49,8,128]{2,1,0:T(8,128)S(1)} %collective-permute-done.near_meta.near, f32[49,8,128]{2,1,0:T(8,128)S(1)} %collective-permute-done.1.far_meta.far, ...), custom_call_target="tpu_custom_call" | custom-call | tf_op jit(solution)/shard_map/sweeps/pallas_call | solution.py:753
  55.0 24.5 %all_to_all.5.received = f32[64,8,128]{2,1,0:T(8,128)S(1)} all-to-all(f32[64,8,128]{2,1,0:T(8,128)S(1)} %get-tuple-element.17), channel_id=1, replica_groups=mesh['gz'=4,'ba'=8] {'ba'}, dimensions={0} | all-to-all | bytes 524288 | tf_op jit(solution)/shard_map/all_to_all | solution.py:790
  79.4 0.0 collective-permute-start.4
  79.4 0.1 pad_add_fusion.spot
  79.5 1.5 %collective-permute-done.4.swapped = f32[64,8,128]{2,1,0:T(8,128)S(1)} collective-permute-done((f32[64,8,128]{2,1,0:T(8,128)S(1)}, f32[64,8,128]{2,1,0:T(8,128)S(1)}, u32[]{:S(2)}, u32[]{:S(2)}) %collective-permute-start.4) | collective-permute-done | bytes 262176 | tf_op jit(solution)/shard_map/ppermute | solution.py:791
  81.0 6.0 %smooth.1 = f32[8,64,256]{2,1,0:T(8,128)} custom-call(s32[3]{0:T(128)S(1)} %pad_add_fusion.spot, f32[8,8,8,128]{3,2,1,0:T(8,128)S(1)} %bitcast.9, f32[64,8,128]{2,1,0:T(8,128)S(1)} %all_to_all.5.received, f32[64,8,128]{2,1,0:T(8,128)S(1)} %collective-permute-done.4.swapped), custom_call_target="tpu_custom_call" | custom-call | tf_op jit(solution)/shard_map/smooth/pallas_call | solution.py:794
Async XLA Ops:
  0.6 0.7 copy-start.6
  1.3 1.0 %copy-start = (f32[4,32,1024]{2,1,0:T(8,128)S(1)}, f32[4,32,1024]{2,1,0:T(8,128)}, u32[]{:S(2)}) copy-start(f32[4,32,1024]{2,1,0:T(8,128)} %param.5) | copy-start | bytes 1572868
  2.3 1.0 %copy-start.2 = (f32[4,32,1024]{2,1,0:T(8,128)S(1)}, f32[4,32,1024]{2,1,0:T(8,128)}, u32[]{:S(2)}) copy-start(f32[4,32,1024]{2,1,0:T(8,128)} %param.6) | copy-start | bytes 1572868
  3.4 1.0 %copy-start.4 = (f32[4,32,1024]{2,1,0:T(8,128)S(1)}, f32[4,32,1024]{2,1,0:T(8,128)}, u32[]{:S(2)}) copy-start(f32[4,32,1024]{2,1,0:T(8,128)} %param.7) | copy-start | bytes 1572868
  4.4 1.0 %copy-start.5 = (f32[4,32,1024]{2,1,0:T(8,128)S(1)}, f32[4,32,1024]{2,1,0:T(8,128)}, u32[]{:S(2)}) copy-start(f32[4,32,1024]{2,1,0:T(8,128)} %param.8) | copy-start | bytes 1572868
  8.6 1.5 %collective-permute-start = (f32[49,8,128]{2,1,0:T(8,128)S(1)}, f32[49,8,128]{2,1,0:T(8,128)S(1)}, u32[]{:S(2)}, u32[]{:S(2)}) collective-permute-start(f32[49,8,128]{2,1,0:T(8,128)S(1)} %get-tuple-element.10), channel_id=1, source_target_pairs={{0,1},{1,0},{2,3},{3,2},{4,5},{5,4},{6,7},{7,6},{8,9},{9,8},{10,11... | collective-permute-start | bytes 602120 | tf_op jit(solution)/shard_map/ppermute | solution.py:733
  8.7 1.4 %collective-permute-start.1 = (f32[49,8,128]{2,1,0:T(8,128)S(1)}, f32[49,8,128]{2,1,0:T(8,128)S(1)}, u32[]{:S(2)}, u32[]{:S(2)}) collective-permute-start(f32[49,8,128]{2,1,0:T(8,128)S(1)} %get-tuple-element.11), channel_id=1, source_target_pairs={{1,2},{2,1},{3,4},{4,3},{5,6},{6,5},{9,10},{10,9},{11,12},{12,11},... | collective-permute-start | bytes 602120 | tf_op jit(solution)/shard_map/ppermute | solution.py:734
  10.1 20.9 %copy-start.1 = (f32[4,32,1024]{2,1,0:T(8,128)S(1)}, f32[4,32,1024]{2,1,0:T(8,128)}, u32[]{:S(2)}) copy-start(f32[4,32,1024]{2,1,0:T(8,128)} %param.5) | copy-start | bytes 1572868
  10.1 20.9 %copy-start.3 = (f32[4,32,1024]{2,1,0:T(8,128)S(1)}, f32[4,32,1024]{2,1,0:T(8,128)}, u32[]{:S(2)}) copy-start(f32[4,32,1024]{2,1,0:T(8,128)} %param.6) | copy-start | bytes 1572868
  11.4 10.5 %collective-permute-start.2 = (f32[115,8,128]{2,1,0:T(8,128)S(1)}, f32[115,8,128]{2,1,0:T(8,128)S(1)}, u32[]{:S(2)}, u32[]{:S(2)}) collective-permute-start(f32[115,8,128]{2,1,0:T(8,128)S(1)} %get-tuple-element.14), channel_id=1, source_target_pairs={{8,0},{16,8},{24,16},{9,1},{17,9},{25,17},{10,2},{18,10},{26,18},{... | collective-permute-start | bytes 1413128 | tf_op jit(solution)/shard_map/ppermute | solution.py:749
  14.8 16.3 %collective-permute-start.3 = (f32[115,8,128]{2,1,0:T(8,128)S(1)}, f32[115,8,128]{2,1,0:T(8,128)S(1)}, u32[]{:S(2)}, u32[]{:S(2)}) collective-permute-start(f32[115,8,128]{2,1,0:T(8,128)S(1)} %get-tuple-element.15), channel_id=1, source_target_pairs={{0,8},{8,16},{16,24},{1,9},{9,17},{17,25},{2,10},{10,18},{18,26},{... | collective-permute-start | bytes 1413128 | tf_op jit(solution)/shard_map/ppermute | solution.py:748
  79.4 1.5 %collective-permute-start.4 = (f32[64,8,128]{2,1,0:T(8,128)S(1)}, f32[64,8,128]{2,1,0:T(8,128)S(1)}, u32[]{:S(2)}, u32[]{:S(2)}) collective-permute-start(f32[64,8,128]{2,1,0:T(8,128)S(1)} %all_to_all.5.received), channel_id=1, source_target_pairs={{0,1},{1,0},{2,3},{3,2},{4,5},{5,4},{6,7},{7,6},{8,9},{9,8},{10,11... | collective-permute-start | bytes 786440 | tf_op jit(solution)/shard_map/ppermute | solution.py:791

commit v2 on v1

v2 whole, which is shorter than its diff:
```python
import functools

import jax
import jax.numpy as jnp
from jax import lax
from jax.experimental import pallas as pl
from jax.experimental.pallas import tpu as pltpu
from jax.sharding import PartitionSpec as P

SLOTS = 4
KMIN = 0.01
HEAT = 0.05
F32 = jnp.float32
I32 = jnp.int32

E_SLAB = 128
E_ZERO = 160
E_TILES = 192
L_INNER = 32
L_UP = 64
L_DOWN = 88
L_SLAB = 112
L_ZERO = 140
L_TILES = 148
X_TILES = 33
Z_SLABS = 72
Z_TILES = 85
DUMMY = 29


def lanes():
    return lax.broadcasted_iota(I32, (8, 128), 1)


def rows():
    return lax.broadcasted_iota(I32, (8, 128), 0)


def take(tile, index):
    return jnp.take_along_axis(tile, index, axis=1)


def row_of(values):
    lane = lanes()
    result = jnp.zeros((8, 128), F32)
    for index, value in enumerate(values):
        result = jnp.where(lane == index, (value + 1).astype(F32), result)
    return result


def position_at(meta, index):
    return meta[0, 0, index].astype(I32) - 1


def as_int(flag):
    return jnp.where(flag, 1, 0).astype(I32)


def pack_kernel(
    place,
    parity_ref,
    mat_in,
    heat_in,
    load_in,
    prior_in,
    near,
    far,
    mat,
    heat,
    load,
    prior,
    sems,
):
    pairs = ((mat_in, mat), (prior_in, prior), (load_in, load), (heat_in, heat))
    fetches = [
        [
            pltpu.make_async_copy(
                source.at[pl.ds(32 * s, 32)], target.at[pl.ds(32 * s, 32)], sems.at[k, s]
            )
            for k, (source, target) in enumerate(pairs)
        ]
        for s in range(SLOTS)
    ]
    for slot_fetches in fetches:
        for fetch in slot_fetches:
            fetch.start()
    parity = parity_ref[0]
    lane = lanes()
    depth = lane // 32
    inside = 32 * (lane % 4)
    pick = (lane % 32) // 4
    mirror = parity == 0
    sides = []
    for out, flip in ((near, mirror), (far, jnp.logical_not(mirror))):
        base = jnp.where(flip, inside + 31, inside)
        sign = jnp.where(flip, -1, 1)
        sides.append(
            (
                out,
                base + sign * depth,
                base,
                base + sign * jnp.maximum(depth - 2, 0),
            )
        )

    def slab(unit, carry):
        row = pl.multiple_of(unit * 8, 8)

        def gather(ref, index):
            tile = take(ref[pl.ds(row, 8), 0:128], index)
            for j in range(1, 8):
                got = take(ref[pl.ds(row, 8), 128 * j : 128 * j + 128], index)
                tile = jnp.where(pick == j, got, tile)
            return tile

        for out, at_depth, at_face, at_load in sides:
            fraction = gather(mat, at_depth)
            warm = gather(heat, at_face)
            dual = gather(prior, at_depth)
            given = gather(load, at_load)
            own = conductivity(fraction)
            third = conduct(own, pltpu.roll(own, 96, 1)) * pltpu.roll(dual, 96, 1)
            given = given + jnp.where(depth == 3, pltpu.roll(third, 64, 1), 0.0)
            out[unit] = jnp.where(depth == 3, warm, fraction)
            out[16 + unit] = jnp.where(depth < 2, dual, given)
        return carry

    for s in range(SLOTS):
        for fetch in fetches[s]:
            fetch.wait()
        lax.fori_loop(4 * s, 4 * s + 4, slab, 0, unroll=2)
    meta = row_of([place[s] for s in range(SLOTS)])
    near[X_TILES - 1] = meta
    far[X_TILES - 1] = meta


def corner_kernel(
    place, near_meta, far_meta, mat, heat, load, prior, near, far, up, down
):
    values = [place[s] for s in range(SLOTS)]
    start = as_int(values[SLOTS - 1] >= 0)
    row = rows()

    def layer(out, to, at, j, rising):
        fraction, warm, given, dual = (
            ref[pl.ds(at, 8), 128 * j : 128 * j + 128] for ref in (mat, heat, load, prior)
        )
        step = 1 if rising else 7
        own = conductivity(fraction)
        beyond = conduct(own, pltpu.roll(own, step, 0)) * pltpu.roll(dual, step, 0)
        given = given + jnp.where(row == (2 if rising else 5), beyond, 0.0)
        spare, two = ((row == 0, row < 2) if rising else (row == 7, row > 5))
        a, b, c = ((5, 4, 2) if rising else (7, 5, 3))
        out[to] = jnp.where(spare, pltpu.roll(warm, a, 0), fraction)
        out[to + 24] = jnp.where(two, pltpu.roll(warm, b, 0), dual)
        out[to + 48] = jnp.where(two, pltpu.roll(warm, c, 0), given)

    for i in range(3):
        top = pl.multiple_of((start + i) * 32 + 24, 8)
        for j in range(8):
            layer(up, 8 * i + j, top, j, True)
            layer(down, 8 * i + j, 32 * i, j, False)
    for b, (meta, source) in enumerate(((near_meta, near), (far_meta, far))):
        listed = [position_at(meta, s) for s in range(SLOTS)]
        values = values + listed
        start = as_int(listed[SLOTS - 1] >= 0)
        for field in range(2):
            for i in range(3):
                to = Z_SLABS + b * 6 + field * 3 + i
                up[to] = source[field * 16 + (start + i) * 4 + 3]
                down[to] = source[field * 16 + i * 4]
    meta_tile = row_of(values)
    up[Z_TILES - 1] = meta_tile
    down[Z_TILES - 1] = meta_tile


def conduct(own, beside):
    return (2.0 * own) * beside / jnp.maximum(own + beside, KMIN)


def conductivity(fraction):
    return KMIN + (1.0 - KMIN) * fraction * fraction * fraction


def cell_of(x, y, z):
    return ((z + 1) * 6 + y + 1) * 4 + x + 1


def clear_cells(cells, zero):
    def clear(index, carry):
        cells[index] = zero
        return carry

    lax.fori_loop(0, 144, clear, 0, unroll=16)


def enter(cells, position, wanted, x, z, tile):
    here = jnp.where(wanted, cell_of(x, position // 2 % 4, z), 144)
    cells[here] = tile
    return jnp.where(wanted, here, DUMMY)


def fill(table, unit, values):
    for k, value in enumerate(values):
        table[unit * 8 + k] = value


class Stencil:
    def __init__(self, weights, stride):
        self.lane = lanes()
        row = rows()
        self.top_row = row == 0
        self.last_row = row == 7
        self.x_cell = self.lane % 32
        self.y_block = self.lane // 32
        self.face_block = self.lane // 4
        self.face_lane = 32 * (self.lane % 4)
        self.weights = weights
        self.stride = stride

    def above(self, tile, other):
        return pltpu.roll(jnp.where(self.top_row, other, tile), 7, 0)

    def below(self, tile, other):
        return pltpu.roll(jnp.where(self.last_row, other, tile), 1, 0)

    def brick(self, table, unit):
        base, up, down, north, south, east, west, px = (table[unit * 8 + k] for k in range(8))
        lane, x_cell = (self.lane, self.x_cell)
        inner = 1 - px
        east_index = jnp.where(px == 1, self.y_block, jnp.maximum(lane - 31, 0))
        west_index = jnp.where(px == 0, self.y_block, jnp.minimum(lane + 31, 127))

        def around(ref, j):
            tile = ref[base + j]
            after = ref[base + j + 1] if j < 7 else ref[north]
            before = ref[base + j - 1] if j > 0 else ref[south + 7]
            over = take(ref[east + inner * j], east_index + 4 * j * px)
            under = take(ref[west + px * j], west_index + 4 * j * inner)
            return tile, (
                jnp.where(x_cell == 31, over, pltpu.roll(tile, 127, 1)),
                jnp.where(x_cell == 0, under, pltpu.roll(tile, 1, 1)),
                pltpu.roll(jnp.where(lane < 32, after, tile), 96, 1),
                pltpu.roll(jnp.where(lane >= 96, before, tile), 32, 1),
                self.above(tile, ref[up + j]),
                self.below(tile, ref[down + j]),
            )

        return base, around

    def slab(self, table, unit):
        at, up, down, north, south, face, column = (table[unit * 8 + k] for k in range(7))
        lane, x_cell = (self.lane, self.x_cell)
        index = self.face_lane + column

        def around(ref):
            tile = ref[at]
            edge = take(ref[face], index)
            for j in range(1, 8):
                edge = jnp.where(self.face_block == j, take(ref[face + j], index), edge)
            return tile, (
                pltpu.roll(tile, 96, 1),
                jnp.where(lane < 32, edge, pltpu.roll(tile, 32, 1)),
                jnp.where(x_cell == 31, pltpu.roll(ref[north], 31, 1), pltpu.roll(tile, 127, 1)),
                jnp.where(x_cell == 0, pltpu.roll(ref[south], 97, 1), pltpu.roll(tile, 1, 1)),
                self.above(tile, ref[up]),
                self.below(tile, ref[down]),
            )

        return at, around

    def first(self, t, source, inverse, dual1, own_kappa, beside_kappa, beside):
        total = jnp.full((8, 128), HEAT, F32)
        flux = source[t]
        for k in range(6):
            weight = conduct(own_kappa, beside_kappa[k])
            self.weights[k * self.stride + t] = weight
            total = total + weight
            flux = flux + weight * beside[k]
        scale = 1.0 / total
        inverse[t] = scale
        dual1[t] = flux * scale

    def later(self, t, source, inverse, beside):
        flux = source[t]
        for k in range(6):
            flux = flux + self.weights[k * self.stride + t] * beside[k]
        return flux * inverse[t]

    def sensitivity(self, t, warm, warms, dual, duals):
        total = jnp.zeros((8, 128), F32)
        for k in range(6):
            total = total + jnp.where(
                self.weights[k * self.stride + t] > 0,
                (warms[k] - warm) * (duals[k] - dual),
                0.0,
            )
        return total


def factor_of(fraction):
    return (-1.5 * (1.0 - KMIN)) * fraction * fraction


def spread(to, first, second, kappa, temperature, source, dual0):
    kappa[to] = conductivity(first)
    dual0[to] = jnp.where(lanes() < 64, second, 0.0)
    source[to] = pltpu.roll(second, 64, 1)
    temperature[to] = pltpu.roll(first, 32, 1)


def shrink_table():
    cell = lax.broadcasted_iota(I32, (512, 128), 0)
    coarse = lax.broadcasted_iota(I32, (512, 128), 1)
    matches = (cell // 64 == coarse // 16) & (cell % 32 // 2 == coarse % 16)
    return jnp.where(matches, 0.125, 0.0).astype(F32)


def restrict(sens, summed, out, count):
    shrink = shrink_table()
    for half in range(2):
        summed[...] = jnp.dot(
            sens[:, 512 * half : 512 * half + 512],
            shrink,
            precision=lax.Precision.HIGHEST,
            preferred_element_type=F32,
        )
        for r in range(count):
            out[half, 8 * r : 8 * r + 8, :] = (
                summed[pl.ds(16 * r, 8, stride=2), :] + summed[pl.ds(16 * r + 1, 8, stride=2), :]
            )


def early_kernel(
    place,
    parity_ref,
    near_meta,
    far_meta,
    mat,
    heat,
    load,
    prior,
    near,
    far,
    dual1,
    dual2,
    coarse,
    cells,
    brick_table,
    slab_table,
    kappa,
    temperature,
    source,
    dual0,
    weights,
    inverse,
    sens,
    summed,
):
    parity = parity_ref[0]
    clear_cells(cells, E_ZERO)
    own = [place[s] for s in range(SLOTS)]
    own_cell = [enter(cells, q, q >= 0, q % 2, q // 8, 32 * s) for s, q in enumerate(own)]
    slab_cell = []
    slab_live = []
    for b, meta in enumerate((near_meta, far_meta)):
        east = parity == b
        column = jnp.where(east, 0, 1)
        x = jnp.where(east, 2, -1)
        for s in range(SLOTS):
            q = position_at(meta, s)
            wanted = (q >= 0) & (q % 2 == column)
            slab_live.append((wanted, q))
            slab_cell.append(
                enter(cells, q, wanted, x, q // 8, E_SLAB + 16 * b + 4 * s)
            )
    for s in range(SLOTS):
        here = own_cell[s]
        px = jnp.where(own[s] >= 0, own[s] % 2, 0)
        lift = jnp.where(own[s] >= 8, 24, 0)
        north, south = (cells[here + 4], cells[here - 4])
        east, west = (cells[here + 1], cells[here - 1])
        above, below = (cells[here + 24], cells[here - 24] + lift)
        for c in range(4):
            base = s * 32 + c * 8
            fill(
                brick_table,
                s * 4 + c,
                (
                    base,
                    base + 8 if c < 3 else above,
                    base - 8 if c > 0 else below,
                    north + 8 * c,
                    south + 8 * c,
                    east + jnp.where(px == 1, c, 8 * c),
                    west + jnp.where(px == 0, c, 8 * c),
                    px,
                ),
            )
    for b in range(2):
        inward = jnp.where(parity == b, -1, 1)
        column = jnp.where(parity == b, 31, 0)
        for s in range(SLOTS):
            here = slab_cell[4 * b + s]
            wanted, q = slab_live[4 * b + s]
            lift = jnp.where(q >= 8, 3, 0)
            north, south = (cells[here + 4], cells[here - 4])
            above, below = (cells[here + 24], cells[here - 24] + lift)
            face = cells[here + inward]
            live = as_int(wanted)
            for c in range(4):
                unit = 16 * b + 4 * s + c
                fill(
                    slab_table,
                    unit,
                    (
                        E_SLAB + unit,
                        E_SLAB + unit + 1 if c < 3 else above,
                        E_SLAB + unit - 1 if c > 0 else below,
                        north + c,
                        south + c,
                        face + 8 * c,
                        column,
                        live,
                    ),
                )

    zeros = jnp.zeros((8, 128), F32)
    for ref in (kappa, temperature, dual0, dual1, dual2):
        for t in range(32):
            ref[E_ZERO + t] = zeros

    def own_unit(unit, carry):
        at = pl.multiple_of(unit * 8, 8)
        active = place[unit // 4] >= 0
        for j in range(8):
            span = slice(128 * j, 128 * j + 128)
            t = unit * 8 + j
            kappa[t] = jnp.where(active, conductivity(mat[pl.ds(at, 8), span]), 0.0)
            source[t] = jnp.where(active, load[pl.ds(at, 8), span], 0.0)
            dual0[t] = prior[pl.ds(at, 8), span]
            temperature[t] = heat[pl.ds(at, 8), span]
        return carry

    lax.fori_loop(0, 16, own_unit, 0)
    for b, message in enumerate((near, far)):
        for t in range(16):
            to = E_SLAB + 16 * b + t
            spread(to, message[t], message[t + 16], kappa, temperature, source, dual0)

    stencil = Stencil(weights, E_TILES)

    def slabs(body):
        def slot(index, carry):
            @pl.when(slab_table[index * 32 + 7] > 0)
            def _():
                for c in range(4):
                    body(*stencil.slab(slab_table, index * 4 + c))

            return carry

        lax.fori_loop(0, 8, slot, 0)

    def bricks(body):
        def two(step, carry):
            for k in range(2):
                unit = 2 * step + k
                base, around = stencil.brick(brick_table, unit)
                for j in range(8):
                    body(unit, base, around, j)
            return carry

        lax.fori_loop(0, 8, two, 0)

    def brick_first(unit, base, around, j):
        own_kappa, beside_kappa = around(kappa, j)
        stencil.first(
            base + j, source, inverse, dual1, own_kappa, beside_kappa, around(dual0, j)[1]
        )

    def slab_first(t, around):
        own_kappa, beside_kappa = around(kappa)
        stencil.first(t, source, inverse, dual1, own_kappa, beside_kappa, around(dual0)[1])

    def brick_second(unit, base, around, j):
        dual2[base + j] = stencil.later(base + j, source, inverse, around(dual1, j)[1])

    def slab_second(t, around):
        dual2[t] = stencil.later(t, source, inverse, around(dual1)[1])

    def brick_third(unit, base, around, j):
        at = pl.multiple_of(unit * 8, 8)
        dual, duals = around(dual2, j)
        warm, warms = around(temperature, j)
        total = stencil.sensitivity(base + j, warm, warms, dual, duals)
        span = slice(128 * j, 128 * j + 128)
        sens[pl.ds(at, 8), span] = factor_of(mat[pl.ds(at, 8), span]) * total

    bricks(brick_first)
    slabs(slab_first)
    bricks(brick_second)
    slabs(slab_second)
    bricks(brick_third)
    restrict(sens, summed, coarse, 8)


def late_kernel(
    parts,
    place,
    parity_ref,
    near_meta,
    far_meta,
    up_meta,
    down_meta,
    mat,
    heat,
    load,
    prior,
    near,
    far,
    z_up,
    z_down,
    early1,
    early2,
    coarse,
    dual_out,
    chunks,
    dual_rows,
    dual_sem,
    cells,
    brick_table,
    slab_table,
    brick_list,
    slab_list,
    kappa,
    temperature,
    source,
    dual0,
    dual1,
    dual2,
    weights,
    inverse,
    factor,
    sens,
    summed,
    edge,
    whole,
    turned,
):
    parity = parity_ref[0]
    lane = lanes()
    row = rows()
    clear_cells(cells, L_ZERO)
    own = [place[s] for s in range(SLOTS)]

    def at_edge(q):
        return ((q >= 0) & (q < 8)) | (q >= 24)

    own_cell = [
        enter(cells, q, at_edge(q), q % 2, q // 8, 8 * s) for s, q in enumerate(own)
    ]
    lists_up = [[position_at(up_meta, 4 * k + s) for s in range(SLOTS)] for k in range(3)]
    lists_down = [[position_at(down_meta, 4 * k + s) for s in range(SLOTS)] for k in range(3)]

    def shifted(listed):
        full = listed[SLOTS - 1] >= 0
        return [jnp.where(full, listed[i + 1], listed[i]) for i in range(3)]

    ups = [listed[:3] for listed in lists_up]
    downs = [shifted(listed) for listed in lists_down]
    brick_live = [at_edge(q) for q in own]
    brick_live += [(q >= 0) & (q < 8) for q in ups[0]]
    brick_live += [q >= 24 for q in downs[0]]
    halo_cell = [
        enter(cells, q, brick_live[4 + i], q % 2, 4, L_UP + 8 * i) for i, q in enumerate(ups[0])
    ]
    halo_cell += [
        enter(cells, q, brick_live[7 + i], q % 2, -1, L_DOWN + 8 * i)
        for i, q in enumerate(downs[0])
    ]
    slab_cell = []
    slab_live = []
    slab_own = []
    for b, meta in enumerate((near_meta, far_meta)):
        east = parity == b
        column = jnp.where(east, 0, 1)
        x = jnp.where(east, 2, -1)
        base = L_SLAB + 14 * b
        mine = [position_at(meta, s) for s in range(SLOTS)]
        slab_own.append(mine)
        tests = [at_edge(q) & (q % 2 == column) for q in mine]
        tests += [(q >= 0) & (q < 8) & (q % 2 == column) for q in ups[1 + b]]
        tests += [(q >= 24) & (q % 2 == column) for q in downs[1 + b]]
        slab_live += tests
        for k, q in enumerate(mine + ups[1 + b] + downs[1 + b]):
            z = q // 8 if k < 4 else 4 if k < 7 else -1
            slab_cell.append(enter(cells, q, tests[k], x, z, base + (k if k < 4 else 4 + k)))

    high = [as_int(q >= 24) for q in own]
    for s in range(SLOTS):
        here = own_cell[s]
        px = jnp.where(own[s] >= 0, own[s] % 2, 0)
        inner = L_INNER + 8 * s
        fill(
            brick_table,
            s,
            (
                jnp.int32(8 * s),
                jnp.where(high[s] == 1, cells[here + 24], inner),
                jnp.where(high[s] == 1, inner, cells[here - 24]),
                cells[here + 4],
                cells[here - 4],
                cells[here + 1],
                cells[here - 1],
                px,
            ),
        )
    for i in range(6):
        here = halo_cell[i]
        q = (ups[0] + downs[0])[i]
        px = jnp.where(q >= 0, q % 2, 0)
        fill(
            brick_table,
            4 + i,
            (
                jnp.int32(L_UP + 8 * i),
                jnp.int32(L_ZERO) if i < 3 else cells[here + 24],
                cells[here - 24] if i < 3 else jnp.int32(L_ZERO),
                cells[here + 4],
                cells[here - 4],
                cells[here + 1],
                cells[here - 1],
                px,
            ),
        )
    for b in range(2):
        inward = jnp.where(parity == b, -1, 1)
        column = jnp.where(parity == b, 31, 0)
        base = L_SLAB + 14 * b
        for k in range(10):
            here = slab_cell[10 * b + k]
            above, below = (cells[here + 24], cells[here - 24])
            if k < 4:
                top = slab_own[b][k] >= 24
                inner = base + 4 + k
                above, below = (jnp.where(top, above, inner), jnp.where(top, inner, below))
            elif k < 7:
                above = jnp.int32(L_ZERO)
            else:
                below = jnp.int32(L_ZERO)
            fill(
                slab_table,
                10 * b + k,
                (
                    jnp.int32(base + (k if k < 4 else 4 + k)),
                    above,
                    below,
                    cells[here + 4],
                    cells[here - 4],
                    cells[here + inward],
                    column,
                ),
            )

    def listed(target, flags):
        count = jnp.int32(0)
        for index, flag in enumerate(flags):
            target[count] = index
            count = count + as_int(flag)
        last = target[jnp.maximum(count - 1, 0)]
        for k in range(3):
            target[count + k] = last
        return count

    brick_count = listed(brick_list, brick_live)
    slab_count = listed(slab_list, slab_live)

    zeros = jnp.zeros((8, 128), F32)
    for ref in (kappa, temperature, dual0, dual1, dual2):
        for t in range(8):
            ref[L_ZERO + t] = zeros

    for s in range(SLOTS):
        active = own[s] >= 0
        for to, chunk in ((8 * s, 3 * high[s]), (L_INNER + 8 * s, 1 + high[s])):
            at = pl.multiple_of(s * 32 + 8 * chunk, 8)
            for j in range(8):
                span = slice(128 * j, 128 * j + 128)
                fraction = mat[pl.ds(at, 8), span]
                kappa[to + j] = jnp.where(active, conductivity(fraction), 0.0)
                dual0[to + j] = prior[pl.ds(at, 8), span]
                temperature[to + j] = heat[pl.ds(at, 8), span]
                if to < L_INNER:
                    source[to + j] = load[pl.ds(at, 8), span]
                    factor[to + j] = factor_of(fraction)
                else:
                    dual1[to + j] = early1[32 * s + 8 * chunk + j]
                    dual2[to + j] = early2[32 * s + 8 * chunk + j]

    for k, message in enumerate((z_up, z_down)):
        for i in range(3):

            @pl.when(brick_live[4 + 3 * k + i])
            def _(k=k, i=i, message=message):
                for j in range(8):
                    t = 8 * i + j
                    to = L_UP + 24 * k + t
                    one, two, three = (message[t], message[24 + t], message[48 + t])
                    a, b, c = ((3, 4, 6) if k else (1, 3, 5))
                    kappa[to] = conductivity(one)
                    dual0[to] = jnp.where(row >= 2 if k else row < 6, two, 0.0)
                    source[to] = three
                    temperature[to] = jnp.where(
                        row == 3 if k else row == 0,
                        pltpu.roll(one, a, 0),
                        jnp.where(
                            row < 6 if k else row < 3,
                            pltpu.roll(two, b, 0),
                            pltpu.roll(three, c, 0),
                        ),
                    )
                    factor[to] = factor_of(one)

    def slab_tile(to, message, at, step):
        spread(to, message[at], message[at + step], kappa, temperature, source, dual0)

    for b, message in enumerate((near, far)):
        base = L_SLAB + 14 * b
        for s in range(SLOTS):
            top = as_int(slab_own[b][s] >= 24)
            slab_tile(base + s, message, 4 * s + 3 * top, 16)
            inner = 4 * s + 1 + top
            slab_tile(base + 4 + s, message, inner, 16)
            dual1[base + 4 + s] = early1[E_SLAB + 16 * b + inner]
            dual2[base + 4 + s] = early2[E_SLAB + 16 * b + inner]
        for i in range(3):
            slab_tile(base + 8 + i, z_up, Z_SLABS + 6 * b + i, 3)
            slab_tile(base + 11 + i, z_down, Z_SLABS + 6 * b + i, 3)

    stencil = Stencil(weights, L_TILES)

    def bricks(body):
        def two(step, carry):
            for k in range(2):
                unit = brick_list[2 * step + k]
                base, around = stencil.brick(brick_table, unit)
                for j in range(8):
                    body(base, around, j)
            return carry

        lax.fori_loop(0, (brick_count + 1) // 2, two, 0)

    def slabs(body):
        def four(step, carry):
            for k in range(4):
                body(*stencil.slab(slab_table, slab_list[4 * step + k]))
            return carry

        lax.fori_loop(0, (slab_count + 3) // 4, four, 0)

    def brick_first(base, around, j):
        own_kappa, beside_kappa = around(kappa, j)
        stencil.first(
            base + j, source, inverse, dual1, own_kappa, beside_kappa, around(dual0, j)[1]
        )

    def slab_first(t, around):
        own_kappa, beside_kappa = around(kappa)
        stencil.first(t, source, inverse, dual1, own_kappa, beside_kappa, around(dual0)[1])

    def brick_second(base, around, j):
        dual2[base + j] = stencil.later(base + j, source, inverse, around(dual1, j)[1])

    def slab_second(t, around):
        dual2[t] = stencil.later(t, source, inverse, around(dual1)[1])

    def brick_third(base, around, j):
        dual, duals = around(dual2, j)
        warm, warms = around(temperature, j)
        total = stencil.sensitivity(base + j, warm, warms, dual, duals)
        at = jnp.where(base < L_INNER, base, base - 32)
        sens[pl.ds(pl.multiple_of(at, 8), 8), 128 * j : 128 * j + 128] = factor[base + j] * total

    bricks(brick_first)
    slabs(slab_first)
    bricks(brick_second)
    slabs(slab_second)
    for s in range(SLOTS):
        for c in range(4):
            for j in range(8):
                dual_rows[32 * s + 8 * c : 32 * s + 8 * c + 8, 128 * j : 128 * j + 128] = early2[
                    32 * s + 8 * c + j
                ]

        @pl.when(brick_live[s])
        def _(s=s):
            at = pl.multiple_of(32 * s + 24 * high[s], 8)
            for j in range(8):
                dual_rows[pl.ds(at, 8), 128 * j : 128 * j + 128] = dual2[8 * s + j]

    writing = pltpu.make_async_copy(dual_rows, dual_out, dual_sem)
    writing.start()
    bricks(brick_third)

    restrict(sens, summed, edge, 5)
    for half in range(2):
        whole[...] = coarse[half]
        for s in range(SLOTS):

            @pl.when(brick_live[s])
            def _(s=s):
                whole[pl.ds(16 * s + 12 * high[s], 4), :] = edge[half, 4 * s : 4 * s + 4, :]

        for r in range(11):
            if r < 8:
                tile = whole[8 * r : 8 * r + 8, :]
            else:
                tile = edge[half, 8 * r - 48 : 8 * r - 40, :]
            for bit in (1, 2, 4):
                low_row = (row & bit) == 0
                low_lane = (lane & (16 * bit)) == 0
                swap_a = pltpu.roll(pltpu.roll(tile, 8 - bit, 0), 16 * bit, 1)
                swap_b = pltpu.roll(pltpu.roll(tile, bit, 0), 128 - 16 * bit, 1)
                tile = jnp.where(low_row == low_lane, tile, jnp.where(low_row, swap_a, swap_b))
            turned[2 * r + half] = tile

    y_block = lane // 32

    planes = 64 // parts
    level = [jnp.where(q >= 0, q // 8, 9) for q in own]

    def count(test):
        return functools.reduce(lambda a, b: a + b, [as_int(test(v)) for v in level])

    before = [count(lambda v, z=z: v < z) for z in range(5)]

    def nth(z, e):
        index = before[z] + e
        valid = index < before[z + 1]
        slot = jnp.minimum(index, SLOTS - 1)
        code = jnp.where(valid, place[slot] - 8 * z, -1)
        return slot, code

    for d in range(parts):
        z = d * planes // 16
        half = d * planes % 16 // 8
        codes = []
        for e in range(3):
            slot, code = nth(z, e)
            codes.append(code)
            for k in range(2):
                chunks[d * 8 + 2 * e + k] = turned[(slot * 2 + half) * 2 + k]
        start = d * planes % 8 == 0
        end = (d + 1) * planes % 8 == 0
        if planes >= 8:
            outside = -1 if half == 0 else 1
        else:
            outside = -1 if start else 1 if end else 0
        beyond = half + outside
        beside = [zeros, zeros]
        for e in range(3):
            if outside == 0:
                tile_at, lane_at, code = (0, 0, jnp.int32(-1))
            elif beyond in (0, 1):
                slot, code = nth(z, e)
                tile_at, lane_at = (slot * 2 + beyond, 96 if outside < 0 else 0)
            elif 0 <= z + outside <= 3:
                slot, code = nth(z + outside, e)
                tile_at, lane_at = (slot * 2 + (1 if outside < 0 else 0), 96 if outside < 0 else 0)
            elif outside < 0:
                q = downs[0][e]
                code = jnp.where(q >= 24, q - 24, -1)
                tile_at, lane_at = (8 + (3 + e) // 2, 64 * ((3 + e) % 2) + 32)
            else:
                q = ups[0][e]
                code = jnp.where((q >= 0) & (q < 8), q, -1)
                tile_at, lane_at = (8 + e // 2, 64 * (e % 2))
            codes.append(code)
            for k in range(2):
                tile = turned[tile_at * 2 + k]
                shift = (32 * e - lane_at) % 128
                if shift:
                    tile = pltpu.roll(tile, shift, 1)
                beside[k] = jnp.where(y_block == e, tile, beside[k])
        for e, code in enumerate(codes):
            beside[0] = jnp.where(lane == 96 + e, (code + 1).astype(F32), beside[0])
        for k in range(2):
            chunks[d * 8 + 6 + k] = beside[k]
    writing.wait()


def filter_kernel(parts, planes, across, spot, meta, received, swapped, out, grid, once):
    member = spot[0]
    depth = planes + 4
    wide = parts // across
    lane = lanes()
    row = rows()
    group_lane = lane // 16
    zeros = jnp.zeros((8, 128), F32)

    def clear(index, carry):
        grid[index] = zeros
        return carry

    lax.fori_loop(0, depth * 8 * wide, clear, 0, unroll=8)
    begin = member * planes
    half = begin % 16 // 8
    side = jnp.where(begin % 8 == 0, 0, planes + 2) if planes < 8 else half * (planes + 2)

    def place_plane(tile, lane_at, window, code, k, column, tile_x):
        at = (column * 2 + code % 2) % 8
        moved = pltpu.roll(tile, (at * 16 - lane_at + 256) % 128, 1)
        where_to = (window * 8 + code // 2 * 2 + k) * wide + tile_x
        grid[where_to] = jnp.where(group_lane == at, moved, grid[where_to])

    def from_device(column, carry):
        tile_x = column // across
        for e in range(3):
            code = meta[column, 0, 0, 96 + e].astype(I32) - 1

            @pl.when(code >= 0)
            def _(e=e, code=code):
                for k in range(2):
                    tile = received[column * 8 + 2 * e + k]
                    if planes == 8:
                        for p in range(8):
                            place_plane(tile, 16 * p, p + 2, code, k, column, tile_x)
                        other = swapped[column * 8 + 2 * e + k]
                        for p in range(2):
                            place_plane(
                                other,
                                jnp.where(half == 0, 16 * p, 96 + 16 * p),
                                jnp.where(half == 0, 10 + p, p),
                                code,
                                k,
                                column,
                                tile_x,
                            )
                    else:
                        for window in range(depth):
                            p = begin % 8 + window - 2

                            @pl.when((p >= 0) & (p < 8))
                            def _(tile=tile, p=p, window=window, k=k):
                                place_plane(tile, 16 * p, window, code, k, column, tile_x)

        for e in range(3):
            code = meta[column, 0, 0, 99 + e].astype(I32) - 1

            @pl.when(code >= 0)
            def _(e=e, code=code):
                for k in range(2):
                    tile = received[column * 8 + 6 + k]
                    for p in range(2):
                        place_plane(
                            tile, 32 * e + 16 * p, side + p, code, k, column, tile_x
                        )

        return carry

    lax.fori_loop(0, parts, from_device, 0)

    def relax(ref, window, y, x):
        here = (window * 8 + y) * wide + x
        tile = ref[here]
        north = ref[here + wide] if y < 7 else zeros
        south = ref[here - wide] if y > 0 else zeros
        east = ref[here + 1] if x < wide - 1 else zeros
        west = ref[here - 1] if x > 0 else zeros
        near = ref[here + 8 * wide] + ref[here - 8 * wide]
        near = near + pltpu.roll(jnp.where(row == 0, north, tile), 7, 0)
        near = near + pltpu.roll(jnp.where(row == 7, south, tile), 1, 0)
        near = near + pltpu.roll(jnp.where(lane == 0, east, tile), 127, 1)
        near = near + pltpu.roll(jnp.where(lane == 127, west, tile), 1, 1)
        return (grid[here] + 2.0 * near) * (1.0 / 13.0)

    first = spot[1] == 0
    last = spot[1] == spot[2] - 1

    def sweep_once(window, carry):
        gone = (first & (window < 2)) | (last & (window >= planes + 2))
        keep = jnp.where(gone, 0.0, 1.0).astype(F32)
        for y in range(8):
            for x in range(wide):
                once[(window * 8 + y) * wide + x] = relax(grid, window, y, x) * keep
        return carry

    lax.fori_loop(1, depth - 1, sweep_once, 0)

    def sweep_again(window, carry):
        for y in range(8):
            for x in range(wide):
                out[window - 2, 8 * y : 8 * y + 8, 128 * x : 128 * x + 128] = relax(
                    once, window, y, x
                )
        return carry

    lax.fori_loop(2, depth - 2, sweep_again, 0)


VMEM = pl.BlockSpec(memory_space=pltpu.VMEM)
SMEM = pl.BlockSpec(memory_space=pltpu.SMEM)
HBM = pl.BlockSpec(memory_space=pltpu.HBM)
BIG = 32 * 1024 * 1024
WHOLE = 60 * 1024 * 1024


def meta_of(index):
    return pl.BlockSpec((1, 8, 128), lambda i: (index, 0, 0), memory_space=pltpu.SMEM)


def params(limit=BIG):
    return pltpu.CompilerParams(vmem_limit_bytes=limit)


def tiles(count):
    return jax.ShapeDtypeStruct((count, 8, 128), F32)


def per_device(
    material_fraction, primal_heat_solution, dual_load, dual_prior_design, holder_cube_location
):
    parts = lax.axis_size("ba")
    groups = lax.axis_size("gz")
    member = lax.axis_index("ba")
    group = lax.axis_index("gz")
    planes = 64 // parts
    parity = (member % 2).reshape(1).astype(I32)
    place = holder_cube_location
    fields = [
        field.reshape(128, 1024)
        for field in (material_fraction, primal_heat_solution, dual_load, dual_prior_design)
    ]
    near, far = pl.pallas_call(
        pack_kernel,
        out_shape=(tiles(X_TILES), tiles(X_TILES)),
        in_specs=[SMEM, SMEM, HBM, HBM, HBM, HBM],
        out_specs=(VMEM, VMEM),
        scratch_shapes=[pltpu.VMEM((128, 1024), F32)] * 4 + [pltpu.SemaphoreType.DMA((4, 4))],
        compiler_params=params(WHOLE),
        name="pack",
    )(place, parity, *fields)
    inner = [(i, i ^ 1) for i in range(parts)]
    outer = [(i, i + 1 if i % 2 else i - 1) for i in range(1, parts - 1)]
    near = lax.ppermute(near, "ba", inner)
    far = lax.ppermute(far, "ba", outer)
    up, down = pl.pallas_call(
        corner_kernel,
        out_shape=(tiles(Z_TILES), tiles(Z_TILES)),
        in_specs=[SMEM, meta_of(X_TILES - 1), meta_of(X_TILES - 1)] + [VMEM] * 6,
        out_specs=(VMEM, VMEM),
        grid=(1,),
        compiler_params=params(),
        name="corners",
    )(place, near, far, *fields, near, far)
    rising = [(i, i + 1) for i in range(groups - 1)]
    falling = [(i + 1, i) for i in range(groups - 1)]
    from_below = lax.ppermute(up, "gz", rising)
    from_above = lax.ppermute(down, "gz", falling)
    meta_z = meta_of(Z_TILES - 1)
    meta_x = meta_of(X_TILES - 1)
    early = pltpu.VMEM((E_TILES, 8, 128), F32)
    dual1, dual2, coarse = pl.pallas_call(
        early_kernel,
        out_shape=(tiles(E_TILES), tiles(E_TILES), jax.ShapeDtypeStruct((2, 64, 128), F32)),
        in_specs=[SMEM, SMEM, meta_x, meta_x] + [VMEM] * 6,
        out_specs=(VMEM, VMEM, VMEM),
        scratch_shapes=[
            pltpu.SMEM((145,), I32),
            pltpu.SMEM((16 * 8,), I32),
            pltpu.SMEM((32 * 8,), I32),
            early,
            early,
            early,
            early,
            pltpu.VMEM((6 * E_TILES, 8, 128), F32),
            early,
            pltpu.VMEM((128, 1024), F32),
            pltpu.VMEM((128, 128), F32),
        ],
        grid=(1,),
        cost_estimate=pl.CostEstimate(flops=10**9, bytes_accessed=3 * 10**7, transcendentals=0),
        compiler_params=params(),
        name="early",
    )(place, parity, near, far, *fields, near, far)
    late = pltpu.VMEM((L_TILES, 8, 128), F32)
    dual, chunks = pl.pallas_call(
        functools.partial(late_kernel, parts),
        out_shape=(jax.ShapeDtypeStruct((128, 1024), F32), tiles(8 * parts)),
        in_specs=[SMEM, SMEM, meta_x, meta_x, meta_z, meta_z] + [VMEM] * 11,
        out_specs=(HBM, VMEM),
        scratch_shapes=[
            pltpu.VMEM((128, 1024), F32),
            pltpu.SemaphoreType.DMA,
            pltpu.SMEM((145,), I32),
            pltpu.SMEM((10 * 8,), I32),
            pltpu.SMEM((20 * 8,), I32),
            pltpu.SMEM((16,), I32),
            pltpu.SMEM((24,), I32),
            late,
            late,
            late,
            late,
            late,
            late,
            pltpu.VMEM((6 * L_TILES, 8, 128), F32),
            late,
            pltpu.VMEM((L_SLAB, 8, 128), F32),
            pltpu.VMEM((80, 1024), F32),
            pltpu.VMEM((80, 128), F32),
            pltpu.VMEM((2, 40, 128), F32),
            pltpu.VMEM((64, 128), F32),
            pltpu.VMEM((22, 8, 128), F32),
        ],
        grid=(1,),
        compiler_params=params(),
        name="late",
    )(
        place,
        parity,
        near,
        far,
        from_above,
        from_below,
        *fields,
        near,
        far,
        from_above,
        from_below,
        dual1,
        dual2,
        coarse,
    )
    received = lax.all_to_all(chunks, "ba", split_axis=0, concat_axis=0, tiled=True)
    swapped = lax.ppermute(received, "ba", inner) if planes == 8 else received
    spot = jnp.stack([member, group * parts + member, jnp.int32(groups * parts)]).astype(I32)
    wide = 32 * parts // 128
    filtered = pl.pallas_call(
        functools.partial(filter_kernel, parts, planes, 4),
        out_shape=jax.ShapeDtypeStruct((planes, 64, 32 * parts), F32),
        in_specs=[
            SMEM,
            pl.BlockSpec(
                (parts, 1, 8, 128), lambda i: (0, 6, 0, 0), memory_space=pltpu.SMEM
            ),
            VMEM,
            VMEM,
        ],
        out_specs=VMEM,
        scratch_shapes=[
            pltpu.VMEM(((planes + 4) * 8 * wide, 8, 128), F32),
            pltpu.VMEM(((planes + 4) * 8 * wide, 8, 128), F32),
        ],
        grid=(1,),
        compiler_params=params(),
        name="smooth",
    )(spot, received.reshape(parts, 8, 8, 128), received, swapped)
    return (dual.reshape(material_fraction.shape), filtered)


def solution(mesh):
    spec = P(("gz", "ba"), None, None)
    return jax.shard_map(
        per_device,
        mesh=mesh,
        in_specs=(spec, spec, spec, spec, P(("gz", "ba"))),
        out_specs=(spec, spec),
        check_vma=False,
    )
```

time: 87.9 us -> 63.3 us (0.72)
  waiting for transfers between devices: 15.9 us -> 2.34 us
  local copies, waits for them, and re-layouts: 4.82 us -> 0.02 us
  blocking collectives: 24.5 us -> 20.4 us
  Pallas kernels: 34.3 us -> 32.3 us
    ppermute x1, waiting for transfers between devices: 9.1 us -> 0.01 us  [per_device(): from_below = lax.ppermute(up, 'gz', rising)]
    unnamed x14 -> x10, local copies, waits for them, and re-layouts: 4.82 us -> 0.02 us
    ppermute x1, waiting for transfers between devices: 4.62 us -> 0.01 us  [per_device(): from_above = lax.ppermute(down, 'gz', falling)]
    all_to_all x1, blocking collectives: 24.5 us -> 20.4 us  [per_device(): lax.all_to_all(chunks, 'ba', split_axis=0, concat_axis=0, tiled=True)]
    pallas_call x2 -> x3, Pallas kernels: 27 us -> 25 us  [the longest x1 12.3 us: per_device(): pl.pallas_call(early_kernel, out_shape=(tiles(E_TILES), tiles(E_TILES), j...]
  transfers between devices with their start and end apart: 5 -> 5, of which waited for: 4 -> 2; matrix products, arithmetic and copies ran while one was open for 0% -> 0% of each run, Pallas kernels for 0% -> 20%
where the time goes in v2:
time: 63.3 us; the launch traced here: 62.5 us
  Pallas kernels  32.3 us (51%)
  blocking collectives  20.4 us (32%)
  starting transfers between devices  6.6 us (10%)
  waiting for transfers between devices  2.34 us (4%)
  between operations  0.78 us (1%)
    all_to_all x1, blocking collectives, per_device(): lax.all_to_all(chunks, 'ba', split_axis=0, concat_axis=0, tiled=True)  20.4 us
    pallas_call x1, Pallas kernels, per_device(): pl.pallas_call(early_kernel, out_shape=(tiles(E_TILES), tiles(E_TILES), j...  12.3 us
    pallas_call x1, Pallas kernels, per_device(): pl.pallas_call(functools.partial(late_kernel, parts), out_shape=(jax.Shap...  6.77 us
    pallas_call x1, Pallas kernels, per_device(): pl.pallas_call(functools.partial(filter_kernel, parts, planes, 4), out_sh...  6.46 us
    pallas_call x1, Pallas kernels, per_device(): pl.pallas_call(pack_kernel, out_shape=(tiles(X_TILES), tiles(X_TILES)), i...  5.96 us
    ppermute x1, starting transfers between devices, per_device(): from_above = lax.ppermute(down, 'gz', falling)  3.34 us
    ppermute x1, starting transfers between devices, per_device(): from_below = lax.ppermute(up, 'gz', rising)  2.52 us
    ppermute x1, waiting for transfers between devices, per_device(): swapped = lax.ppermute(received, 'ba', inner) if planes == 8 else received  1.46 us
  transfers between devices with their start and end apart: 5, of which 2 were waited for; matrix products, arithmetic and copies ran while one was open for 0% of the time, Pallas kernels for 20%

profile of v2, /device:TPU:4, one launch (start us, length us, event | category | flops | bytes accessed | tf_op | source)
XLA Modules:
  0.0 62.5 jit_solution(10666414380506955704)
XLA Ops:
  0.6 0.0 copy-start
  0.7 0.0 copy-start.1
  0.7 0.0 copy-start.2
  0.7 0.0 copy-start.3
  0.7 6.0 %pack.1 = (f32[33,8,128]{2,1,0:T(8,128)}, f32[33,8,128]{2,1,0:T(8,128)}) custom-call(s32[4]{0:T(128)} %place.7, s32[1]{0:T(128)} %bitcast.parity_ref, f32[128,1024]{1,0:T(8,128)} %bitcast.9, f32[128,1024]{1,0:T(8,128)} %bitcast.13, f32[128,1024]{1,0:T(8,128)} %bitcast.17, f32[128,1024]{1,0:T(8,128)} %bitcast.21), custom_call_target="tpu_custom_call" | custom-call | tf_op jit(solution)/shard_map/pack/pallas_call | solution.py:1034
  6.7 0.0 copy-start.4
  6.7 0.1 collective-permute-start
  6.7 0.7 %collective-permute-start.1 = (f32[33,8,128]{2,1,0:T(8,128)}, f32[33,8,128]{2,1,0:T(8,128)S(1)}, u32[]{:S(2)}, u32[]{:S(2)}) collective-permute-start(f32[33,8,128]{2,1,0:T(8,128)} %get-tuple-element.12), channel_id=1, source_target_pairs={{1,2},{2,1},{3,4},{4,3},{5,6},{6,5},{9,10},{10,9},{11,12},{12,11},... | collective-permute-start | bytes 405512 | tf_op jit(solution)/shard_map/ppermute | solution.py:1046
  7.4 0.9 %collective-permute-done.near_meta.near = f32[33,8,128]{2,1,0:T(8,128)S(1)} collective-permute-done((f32[33,8,128]{2,1,0:T(8,128)}, f32[33,8,128]{2,1,0:T(8,128)S(1)}, u32[]{:S(2)}, u32[]{:S(2)}) %collective-permute-start) | collective-permute-done | bytes 135200 | tf_op jit(solution)/shard_map/ppermute | solution.py:1045
  8.3 0.0 collective-permute-done.1.far_meta.far
  8.3 0.0 copy-done
  8.3 0.0 copy-done.1
  8.3 0.0 copy-done.2
  8.3 0.0 copy-done.3
  8.3 0.0 copy-done.4
  8.3 0.8 %corners.1 = (f32[85,8,128]{2,1,0:T(8,128)S(1)}, f32[85,8,128]{2,1,0:T(8,128)S(1)}) custom-call(s32[4]{0:T(128)S(1)} %copy-done.4, f32[33,8,128]{2,1,0:T(8,128)S(1)} %collective-permute-done.near_meta.near, f32[33,8,128]{2,1,0:T(8,128)S(1)} %collective-permute-done.1.far_meta.far, f32[128,1024]{1,0:T(8,128)S(1)} %bitcast.10, f32[128,1024]{1,0:T(8,128)S(1)} %bitcast.14, ...), custom_call_target="tpu_custom_call" | custom-call | tf_op jit(solution)/shard_map/corners/pallas_call | solution.py:1047
  9.2 3.3 %collective-permute-start.2 = (f32[85,8,128]{2,1,0:T(8,128)S(1)}, f32[85,8,128]{2,1,0:T(8,128)S(1)}, u32[]{:S(2)}, u32[]{:S(2)}) collective-permute-start(f32[85,8,128]{2,1,0:T(8,128)S(1)} %get-tuple-element.13), channel_id=1, source_target_pairs={{8,0},{16,8},{24,16},{9,1},{17,9},{25,17},{10,2},{18,10},{26,18},{... | collective-permute-start | bytes 1044488 | tf_op jit(solution)/shard_map/ppermute | solution.py:1059
  12.5 2.5 %collective-permute-start.3 = (f32[85,8,128]{2,1,0:T(8,128)S(1)}, f32[85,8,128]{2,1,0:T(8,128)S(1)}, u32[]{:S(2)}, u32[]{:S(2)}) collective-permute-start(f32[85,8,128]{2,1,0:T(8,128)S(1)} %get-tuple-element.14), channel_id=1, source_target_pairs={{0,8},{8,16},{16,24},{1,9},{9,17},{17,25},{2,10},{10,18},{18,26},{... | collective-permute-start | bytes 1044488 | tf_op jit(solution)/shard_map/ppermute | solution.py:1058
  15.0 12.3 %early.1 = (f32[192,8,128]{2,1,0:T(8,128)S(1)}, f32[192,8,128]{2,1,0:T(8,128)S(1)}, f32[2,64,128]{2,1,0:T(8,128)S(1)}) custom-call(s32[4]{0:T(128)S(1)} %copy-done.4, s32[1]{0:T(128)} %bitcast.parity_ref, f32[33,8,128]{2,1,0:T(8,128)S(1)} %collective-permute-done.near_meta.near, f32[33,8,128]{2,1,0:T(8,128)S(1)} %collective-permute-done.1.far_meta.far, ...), custom_call_target="tpu_custom_call" | custom-call | flops 1000000000 | bytes 30000000 | tf_op jit(solution)/shard_map/early/pallas_call | solution.py:1063
  27.3 0.0 collective-permute-done.2.up_meta.z_up
  27.3 0.0 collective-permute-done.3.down_meta.z_down
  27.3 6.8 %late.1 = (f32[128,1024]{1,0:T(8,128)}, f32[64,8,128]{2,1,0:T(8,128)S(1)}) custom-call(s32[4]{0:T(128)S(1)} %copy-done.4, s32[1]{0:T(128)} %bitcast.parity_ref, f32[33,8,128]{2,1,0:T(8,128)S(1)} %collective-permute-done.near_meta.near, f32[33,8,128]{2,1,0:T(8,128)S(1)} %collective-permute-done.1.far_meta.far, ...), custom_call_target="tpu_custom_call" | custom-call | tf_op jit(solution)/shard_map/late/pallas_call | solution.py:1087
  34.1 20.4 %all_to_all.5.received = f32[64,8,128]{2,1,0:T(8,128)S(1)} all-to-all(f32[64,8,128]{2,1,0:T(8,128)S(1)} %get-tuple-element.19), channel_id=1, replica_groups=mesh['gz'=4,'ba'=8] {'ba'}, dimensions={0} | all-to-all | bytes 524288 | tf_op jit(solution)/shard_map/all_to_all | solution.py:1134
  54.5 0.0 collective-permute-start.4
  54.5 0.1 pad_add_fusion.spot
  54.6 1.5 %collective-permute-done.4.swapped = f32[64,8,128]{2,1,0:T(8,128)S(1)} collective-permute-done((f32[64,8,128]{2,1,0:T(8,128)S(1)}, f32[64,8,128]{2,1,0:T(8,128)S(1)}, u32[]{:S(2)}, u32[]{:S(2)}) %collective-permute-start.4) | collective-permute-done | bytes 262176 | tf_op jit(solution)/shard_map/ppermute | solution.py:1135
  56.0 6.5 %smooth.1 = f32[8,64,256]{2,1,0:T(8,128)} custom-call(s32[3]{0:T(128)S(1)} %pad_add_fusion.spot, f32[8,8,8,128]{3,2,1,0:T(8,128)S(1)} %bitcast.25, f32[64,8,128]{2,1,0:T(8,128)S(1)} %all_to_all.5.received, f32[64,8,128]{2,1,0:T(8,128)S(1)} %collective-permute-done.4.swapped), custom_call_target="tpu_custom_call" | custom-call | tf_op jit(solution)/shard_map/smooth/pallas_call | solution.py:1138
Async XLA Ops:
  0.6 7.7 %copy-start = (f32[4,32,1024]{2,1,0:T(8,128)S(1)}, f32[4,32,1024]{2,1,0:T(8,128)}, u32[]{:S(2)}) copy-start(f32[4,32,1024]{2,1,0:T(8,128)} %param.5) | copy-start | bytes 1572868
  0.7 7.6 %copy-start.1 = (f32[4,32,1024]{2,1,0:T(8,128)S(1)}, f32[4,32,1024]{2,1,0:T(8,128)}, u32[]{:S(2)}) copy-start(f32[4,32,1024]{2,1,0:T(8,128)} %param.6) | copy-start | bytes 1572868
  0.7 7.6 %copy-start.2 = (f32[4,32,1024]{2,1,0:T(8,128)S(1)}, f32[4,32,1024]{2,1,0:T(8,128)}, u32[]{:S(2)}) copy-start(f32[4,32,1024]{2,1,0:T(8,128)} %param.7) | copy-start | bytes 1572868
  0.7 7.6 %copy-start.3 = (f32[4,32,1024]{2,1,0:T(8,128)S(1)}, f32[4,32,1024]{2,1,0:T(8,128)}, u32[]{:S(2)}) copy-start(f32[4,32,1024]{2,1,0:T(8,128)} %param.8) | copy-start | bytes 1572868
  6.7 1.7 %copy-start.4 = (s32[4]{0:T(128)S(1)}, s32[4]{0:T(128)}, u32[]{:S(2)}) copy-start(s32[4]{0:T(128)} %place.7) | copy-start | bytes 52
  6.7 1.6 %collective-permute-start = (f32[33,8,128]{2,1,0:T(8,128)}, f32[33,8,128]{2,1,0:T(8,128)S(1)}, u32[]{:S(2)}, u32[]{:S(2)}) collective-permute-start(f32[33,8,128]{2,1,0:T(8,128)} %get-tuple-element.11), channel_id=1, source_target_pairs={{0,1},{1,0},{2,3},{3,2},{4,5},{5,4},{6,7},{7,6},{8,9},{9,8},{10,11... | collective-permute-start | bytes 405512 | tf_op jit(solution)/shard_map/ppermute | solution.py:1045
  6.7 1.6 %collective-permute-start.1 = (f32[33,8,128]{2,1,0:T(8,128)}, f32[33,8,128]{2,1,0:T(8,128)S(1)}, u32[]{:S(2)}, u32[]{:S(2)}) collective-permute-start(f32[33,8,128]{2,1,0:T(8,128)} %get-tuple-element.12), channel_id=1, source_target_pairs={{1,2},{2,1},{3,4},{4,3},{5,6},{6,5},{9,10},{10,9},{11,12},{12,11},... | collective-permute-start | bytes 405512 | tf_op jit(solution)/shard_map/ppermute | solution.py:1046
  9.2 18.1 %collective-permute-start.2 = (f32[85,8,128]{2,1,0:T(8,128)S(1)}, f32[85,8,128]{2,1,0:T(8,128)S(1)}, u32[]{:S(2)}, u32[]{:S(2)}) collective-permute-start(f32[85,8,128]{2,1,0:T(8,128)S(1)} %get-tuple-element.13), channel_id=1, source_target_pairs={{8,0},{16,8},{24,16},{9,1},{17,9},{25,17},{10,2},{18,10},{26,18},{... | collective-permute-start | bytes 1044488 | tf_op jit(solution)/shard_map/ppermute | solution.py:1059
  12.5 14.8 %collective-permute-start.3 = (f32[85,8,128]{2,1,0:T(8,128)S(1)}, f32[85,8,128]{2,1,0:T(8,128)S(1)}, u32[]{:S(2)}, u32[]{:S(2)}) collective-permute-start(f32[85,8,128]{2,1,0:T(8,128)S(1)} %get-tuple-element.14), channel_id=1, source_target_pairs={{0,8},{8,16},{16,24},{1,9},{9,17},{17,25},{2,10},{10,18},{18,26},{... | collective-permute-start | bytes 1044488 | tf_op jit(solution)/shard_map/ppermute | solution.py:1058
  54.5 1.5 %collective-permute-start.4 = (f32[64,8,128]{2,1,0:T(8,128)S(1)}, f32[64,8,128]{2,1,0:T(8,128)S(1)}, u32[]{:S(2)}, u32[]{:S(2)}) collective-permute-start(f32[64,8,128]{2,1,0:T(8,128)S(1)} %all_to_all.5.received), channel_id=1, source_target_pairs={{0,1},{1,0},{2,3},{3,2},{4,5},{5,4},{6,7},{7,6},{8,9},{9,8},{10,11... | collective-permute-start | bytes 786440 | tf_op jit(solution)/shard_map/ppermute | solution.py:1135

commit v3 on v2

--- a/solution.py
+++ b/solution.py
@@ -69,9 +69,10 @@
     heat,
     load,
     prior,
+    parts,
     sems,
 ):
-    pairs = ((mat_in, mat), (prior_in, prior), (load_in, load), (heat_in, heat))
+    pairs = ((mat_in, mat), (heat_in, heat), (prior_in, prior), (load_in, load))
     fetches = [
         [
             pltpu.make_async_copy(
@@ -84,51 +85,44 @@
     for slot_fetches in fetches:
         for fetch in slot_fetches:
             fetch.start()
-    parity = parity_ref[0]
-    lane = lanes()
-    depth = lane // 32
-    inside = 32 * (lane % 4)
-    pick = (lane % 32) // 4
-    mirror = parity == 0
-    sides = []
-    for out, flip in ((near, mirror), (far, jnp.logical_not(mirror))):
-        base = jnp.where(flip, inside + 31, inside)
-        sign = jnp.where(flip, -1, 1)
-        sides.append(
-            (
-                out,
-                base + sign * depth,
-                base,
-                base + sign * jnp.maximum(depth - 2, 0),
-            )
-        )
-
-    def slab(unit, carry):
-        row = pl.multiple_of(unit * 8, 8)
-
-        def gather(ref, index):
-            tile = take(ref[pl.ds(row, 8), 0:128], index)
-            for j in range(1, 8):
-                got = take(ref[pl.ds(row, 8), 128 * j : 128 * j + 128], index)
-                tile = jnp.where(pick == j, got, tile)
-            return tile
-
-        for out, at_depth, at_face, at_load in sides:
-            fraction = gather(mat, at_depth)
-            warm = gather(heat, at_face)
-            dual = gather(prior, at_depth)
-            given = gather(load, at_load)
-            own = conductivity(fraction)
-            third = conduct(own, pltpu.roll(own, 96, 1)) * pltpu.roll(dual, 96, 1)
-            given = given + jnp.where(depth == 3, pltpu.roll(third, 64, 1), 0.0)
-            out[unit] = jnp.where(depth == 3, warm, fraction)
-            out[16 + unit] = jnp.where(depth < 2, dual, given)
-        return carry
-
+    cell = lax.broadcasted_iota(I32, (1024, 256), 0)
+    column = lax.broadcasted_iota(I32, (1024, 256), 1)
+    deep = column % 128 // 32
+    flipped = (column // 128) != parity_ref[0]
+    wanted = 32 * (column % 32) + jnp.where(flipped, deep, 31 - deep)
+    pick = jnp.where(cell == wanted, 1.0, 0.0).astype(jnp.bfloat16)
+    depth = lanes() // 32
     for s in range(SLOTS):
         for fetch in fetches[s]:
             fetch.wait()
-        lax.fori_loop(4 * s, 4 * s + 4, slab, 0, unroll=2)
+        for k, ref in enumerate((mat, heat, prior, load)):
+            rest = ref[32 * s : 32 * s + 32, :]
+            for third in range(3):
+                part = rest.astype(jnp.bfloat16)
+                at = (3 * k + third) * 32
+                parts[at : at + 32, :] = part
+                rest = rest - part.astype(F32)
+        moved = jnp.dot(parts[...], pick, preferred_element_type=F32)
+        for side, out in enumerate((near, far)):
+            for c in range(4):
+
+                def field(k):
+                    high, mid, low = (
+                        moved[
+                            (3 * k + third) * 32 + 8 * c : (3 * k + third) * 32 + 8 * c + 8,
+                            128 * side : 128 * side + 128,
+                        ]
+                        for third in range(3)
+                    )
+                    return (high + mid) + low
+
+                fraction, warm, dual, given = (field(k) for k in range(4))
+                own = conductivity(fraction)
+                beyond = conduct(own, pltpu.roll(own, 96, 1)) * pltpu.roll(dual, 96, 1)
+                given = pltpu.roll(given + jnp.where(depth == 1, beyond, 0.0), 64, 1)
+                unit = 4 * s + c
+                out[unit] = jnp.where(depth == 3, pltpu.roll(warm, 96, 1), fraction)
+                out[16 + unit] = jnp.where(depth < 2, dual, given)
     meta = row_of([place[s] for s in range(SLOTS)])
     near[X_TILES - 1] = meta
     far[X_TILES - 1] = meta
@@ -227,19 +221,29 @@
     def brick(self, table, unit):
         base, up, down, north, south, east, west, px = (table[unit * 8 + k] for k in range(8))
         lane, x_cell = (self.lane, self.x_cell)
-        inner = 1 - px
-        east_index = jnp.where(px == 1, self.y_block, jnp.maximum(lane - 31, 0))
-        west_index = jnp.where(px == 0, self.y_block, jnp.minimum(lane + 31, 127))
+        own_lane = 31 * px
+        brick_at = jnp.where(px == 1, west, east)
+        slab_at = jnp.where(px == 1, east, west)
+        from_brick = x_cell == own_lane
+        to_brick = x_cell == 31 - own_lane
+        index = jnp.where(to_brick, 32 * self.y_block + own_lane, self.y_block)
+        step = jnp.where(to_brick, 0, 4)
 
         def around(ref, j):
             tile = ref[base + j]
             after = ref[base + j + 1] if j < 7 else ref[north]
             before = ref[base + j - 1] if j > 0 else ref[south + 7]
-            over = take(ref[east + inner * j], east_index + 4 * j * px)
-            under = take(ref[west + px * j], west_index + 4 * j * inner)
+            beside = ref[slab_at]
+            moved = 0
+            if j == 0:
+                beside, moved = (pltpu.roll(beside, 4, 1), 1)
+            elif j == 7:
+                beside, moved = (jnp.where(px == 1, pltpu.roll(beside, 4, 1), beside), px)
+            both = jnp.where(from_brick, ref[brick_at + j], beside)
+            edge = take(both, index + step * (j + moved))
             return tile, (
-                jnp.where(x_cell == 31, over, pltpu.roll(tile, 127, 1)),
-                jnp.where(x_cell == 0, under, pltpu.roll(tile, 1, 1)),
+                jnp.where(x_cell == 31, edge, pltpu.roll(tile, 127, 1)),
+                jnp.where(x_cell == 0, edge, pltpu.roll(tile, 1, 1)),
                 pltpu.roll(jnp.where(lane < 32, after, tile), 96, 1),
                 pltpu.roll(jnp.where(lane >= 96, before, tile), 32, 1),
                 self.above(tile, ref[up + j]),
@@ -462,15 +466,15 @@
         lax.fori_loop(0, 8, slot, 0)
 
     def bricks(body):
-        def two(step, carry):
-            for k in range(2):
-                unit = 2 * step + k
+        def four(step, carry):
+            for k in range(4):
+                unit = 4 * step + k
                 base, around = stencil.brick(brick_table, unit)
                 for j in range(8):
                     body(unit, base, around, j)
             return carry
 
-        lax.fori_loop(0, 8, two, 0)
+        lax.fori_loop(0, 4, four, 0)
 
     def brick_first(unit, base, around, j):
         own_kappa, beside_kappa = around(kappa, j)
@@ -985,7 +989,7 @@
                 once[(window * 8 + y) * wide + x] = relax(grid, window, y, x) * keep
         return carry
 
-    lax.fori_loop(1, depth - 1, sweep_once, 0)
+    lax.fori_loop(1, depth - 1, sweep_once, 0, unroll=2)
 
     def sweep_again(window, carry):
         for y in range(8):
@@ -995,7 +999,7 @@
                 )
         return carry
 
-    lax.fori_loop(2, depth - 2, sweep_again, 0)
+    lax.fori_loop(2, depth - 2, sweep_again, 0, unroll=2)
 
 
 VMEM = pl.BlockSpec(memory_space=pltpu.VMEM)
@@ -1036,7 +1040,8 @@
         out_shape=(tiles(X_TILES), tiles(X_TILES)),
         in_specs=[SMEM, SMEM, HBM, HBM, HBM, HBM],
         out_specs=(VMEM, VMEM),
-        scratch_shapes=[pltpu.VMEM((128, 1024), F32)] * 4 + [pltpu.SemaphoreType.DMA((4, 4))],
+        scratch_shapes=[pltpu.VMEM((128, 1024), F32)] * 4
+        + [pltpu.VMEM((384, 1024), jnp.bfloat16), pltpu.SemaphoreType.DMA((4, 4))],
         compiler_params=params(WHOLE),
         name="pack",
     )(place, parity, *fields)

time: 63.3 us -> 60.6 us (0.957); the launches traced: 62.5 us -> 61 us
  Pallas kernels: 32.3 us -> 28.8 us
  waiting for transfers between devices: 2.34 us -> 3.66 us
    pallas_call x1, Pallas kernels: 12.3 us -> 9.96 us  [per_device(): pl.pallas_call(early_kernel, out_shape=(tiles(E_TILES), tiles(E_TILES), j...]
    ppermute x1, waiting for transfers between devices: 0.01 us -> 1.33 us  [per_device(): from_below = lax.ppermute(up, 'gz', rising)]
    pallas_call x1, Pallas kernels: 6.46 us -> 5.69 us  [per_device(): pl.pallas_call(functools.partial(filter_kernel, parts, planes, 4), out_sh...]
  transfers between devices with their start and end apart: 5 -> 5, of which waited for: 2 -> 3; matrix products, arithmetic and copies ran while one was open for 0% -> 0% of each run, Pallas kernels for 20% -> 16%
where the time goes in v3:
time: 60.6 us; the launch traced here: 61 us
  Pallas kernels  28.8 us (48%)
  blocking collectives  21 us (35%)
  starting transfers between devices  6.6 us (11%)
  waiting for transfers between devices  3.66 us (6%)
  between operations  0.77 us (1%)
    all_to_all x1, blocking collectives, per_device(): lax.all_to_all(chunks, 'ba', split_axis=0, concat_axis=0, tiled=True)  21 us
    pallas_call x1, Pallas kernels, per_device(): pl.pallas_call(early_kernel, out_shape=(tiles(E_TILES), tiles(E_TILES), j...  9.96 us
    pallas_call x1, Pallas kernels, per_device(): pl.pallas_call(functools.partial(late_kernel, parts), out_shape=(jax.Shap...  6.87 us
    pallas_call x1, Pallas kernels, per_device(): pl.pallas_call(functools.partial(filter_kernel, parts, planes, 4), out_sh...  5.69 us
    pallas_call x1, Pallas kernels, per_device(): pl.pallas_call(pack_kernel, out_shape=(tiles(X_TILES), tiles(X_TILES)), i...  5.45 us
    ppermute x1, starting transfers between devices, per_device(): from_above = lax.ppermute(down, 'gz', falling)  3.34 us
    ppermute x1, starting transfers between devices, per_device(): from_below = lax.ppermute(up, 'gz', rising)  2.52 us
    ppermute x1, waiting for transfers between devices, per_device(): swapped = lax.ppermute(received, 'ba', inner) if planes == 8 else received  1.46 us
  transfers between devices with their start and end apart: 5, of which 3 were waited for; matrix products, arithmetic and copies ran while one was open for 0% of the time, Pallas kernels for 16%

profile of v3, /device:TPU:4, one launch (start us, length us, event | category | flops | bytes accessed | tf_op | source)
XLA Modules:
  0.0 61.0 jit_solution(4315514441749317841)
XLA Ops:
  0.6 0.0 copy-start
  0.7 0.0 copy-start.1
  0.7 0.0 copy-start.2
  0.7 0.0 copy-start.3
  0.7 5.5 %pack.1 = (f32[33,8,128]{2,1,0:T(8,128)}, f32[33,8,128]{2,1,0:T(8,128)}) custom-call(s32[4]{0:T(128)} %place.7, s32[1]{0:T(128)} %bitcast.parity_ref, f32[128,1024]{1,0:T(8,128)} %bitcast.9, f32[128,1024]{1,0:T(8,128)} %bitcast.13, f32[128,1024]{1,0:T(8,128)} %bitcast.17, f32[128,1024]{1,0:T(8,128)} %bitcast.21), custom_call_target="tpu_custom_call" | custom-call | tf_op jit(solution)/shard_map/pack/pallas_call | solution.py:1038
  6.1 0.0 copy-start.4
  6.2 0.1 collective-permute-start
  6.2 0.7 %collective-permute-start.1 = (f32[33,8,128]{2,1,0:T(8,128)}, f32[33,8,128]{2,1,0:T(8,128)S(1)}, u32[]{:S(2)}, u32[]{:S(2)}) collective-permute-start(f32[33,8,128]{2,1,0:T(8,128)} %get-tuple-element.12), channel_id=1, source_target_pairs={{1,2},{2,1},{3,4},{4,3},{5,6},{6,5},{9,10},{10,9},{11,12},{12,11},... | collective-permute-start | bytes 405512 | tf_op jit(solution)/shard_map/ppermute | solution.py:1051
  6.9 0.9 %collective-permute-done.near_meta.near = f32[33,8,128]{2,1,0:T(8,128)S(1)} collective-permute-done((f32[33,8,128]{2,1,0:T(8,128)}, f32[33,8,128]{2,1,0:T(8,128)S(1)}, u32[]{:S(2)}, u32[]{:S(2)}) %collective-permute-start) | collective-permute-done | bytes 135200 | tf_op jit(solution)/shard_map/ppermute | solution.py:1050
  7.8 0.0 collective-permute-done.1.far_meta.far
  7.8 0.0 copy-done
  7.8 0.0 copy-done.1
  7.8 0.0 copy-done.2
  7.8 0.0 copy-done.3
  7.8 0.0 copy-done.4
  7.8 0.8 %corners.1 = (f32[85,8,128]{2,1,0:T(8,128)S(1)}, f32[85,8,128]{2,1,0:T(8,128)S(1)}) custom-call(s32[4]{0:T(128)S(1)} %copy-done.4, f32[33,8,128]{2,1,0:T(8,128)S(1)} %collective-permute-done.near_meta.near, f32[33,8,128]{2,1,0:T(8,128)S(1)} %collective-permute-done.1.far_meta.far, f32[128,1024]{1,0:T(8,128)S(1)} %bitcast.10, f32[128,1024]{1,0:T(8,128)S(1)} %bitcast.14, ...), custom_call_target="tpu_custom_call" | custom-call | tf_op jit(solution)/shard_map/corners/pallas_call | solution.py:1052
  8.7 3.3 %collective-permute-start.2 = (f32[85,8,128]{2,1,0:T(8,128)S(1)}, f32[85,8,128]{2,1,0:T(8,128)S(1)}, u32[]{:S(2)}, u32[]{:S(2)}) collective-permute-start(f32[85,8,128]{2,1,0:T(8,128)S(1)} %get-tuple-element.13), channel_id=1, source_target_pairs={{8,0},{16,8},{24,16},{9,1},{17,9},{25,17},{10,2},{18,10},{26,18},{... | collective-permute-start | bytes 1044488 | tf_op jit(solution)/shard_map/ppermute | solution.py:1064
  12.0 2.5 %collective-permute-start.3 = (f32[85,8,128]{2,1,0:T(8,128)S(1)}, f32[85,8,128]{2,1,0:T(8,128)S(1)}, u32[]{:S(2)}, u32[]{:S(2)}) collective-permute-start(f32[85,8,128]{2,1,0:T(8,128)S(1)} %get-tuple-element.14), channel_id=1, source_target_pairs={{0,8},{8,16},{16,24},{1,9},{9,17},{17,25},{2,10},{10,18},{18,26},{... | collective-permute-start | bytes 1044488 | tf_op jit(solution)/shard_map/ppermute | solution.py:1063
  14.5 10.0 %early.1 = (f32[192,8,128]{2,1,0:T(8,128)S(1)}, f32[192,8,128]{2,1,0:T(8,128)S(1)}, f32[2,64,128]{2,1,0:T(8,128)S(1)}) custom-call(s32[4]{0:T(128)S(1)} %copy-done.4, s32[1]{0:T(128)} %bitcast.parity_ref, f32[33,8,128]{2,1,0:T(8,128)S(1)} %collective-permute-done.near_meta.near, f32[33,8,128]{2,1,0:T(8,128)S(1)} %collective-permute-done.1.far_meta.far, ...), custom_call_target="tpu_custom_call" | custom-call | flops 1000000000 | bytes 30000000 | tf_op jit(solution)/shard_map/early/pallas_call | solution.py:1068
  24.5 0.0 collective-permute-done.2.up_meta.z_up
  24.5 1.3 %collective-permute-done.3.down_meta.z_down = f32[85,8,128]{2,1,0:T(8,128)S(1)} collective-permute-done((f32[85,8,128]{2,1,0:T(8,128)S(1)}, f32[85,8,128]{2,1,0:T(8,128)S(1)}, u32[]{:S(2)}, u32[]{:S(2)}) %collective-permute-start.3) | collective-permute-done | bytes 348192 | tf_op jit(solution)/shard_map/ppermute | solution.py:1063
  25.8 6.9 %late.1 = (f32[128,1024]{1,0:T(8,128)}, f32[64,8,128]{2,1,0:T(8,128)S(1)}) custom-call(s32[4]{0:T(128)S(1)} %copy-done.4, s32[1]{0:T(128)} %bitcast.parity_ref, f32[33,8,128]{2,1,0:T(8,128)S(1)} %collective-permute-done.near_meta.near, f32[33,8,128]{2,1,0:T(8,128)S(1)} %collective-permute-done.1.far_meta.far, ...), custom_call_target="tpu_custom_call" | custom-call | tf_op jit(solution)/shard_map/late/pallas_call | solution.py:1092
  32.7 21.0 %all_to_all.5.received = f32[64,8,128]{2,1,0:T(8,128)S(1)} all-to-all(f32[64,8,128]{2,1,0:T(8,128)S(1)} %get-tuple-element.19), channel_id=1, replica_groups=mesh['gz'=4,'ba'=8] {'ba'}, dimensions={0} | all-to-all | bytes 524288 | tf_op jit(solution)/shard_map/all_to_all | solution.py:1139
  53.7 0.0 collective-permute-start.4
  53.8 0.1 pad_add_fusion.spot
  53.8 1.5 %collective-permute-done.4.swapped = f32[64,8,128]{2,1,0:T(8,128)S(1)} collective-permute-done((f32[64,8,128]{2,1,0:T(8,128)S(1)}, f32[64,8,128]{2,1,0:T(8,128)S(1)}, u32[]{:S(2)}, u32[]{:S(2)}) %collective-permute-start.4) | collective-permute-done | bytes 262176 | tf_op jit(solution)/shard_map/ppermute | solution.py:1140
  55.3 5.7 %smooth.1 = f32[8,64,256]{2,1,0:T(8,128)} custom-call(s32[3]{0:T(128)S(1)} %pad_add_fusion.spot, f32[8,8,8,128]{3,2,1,0:T(8,128)S(1)} %bitcast.25, f32[64,8,128]{2,1,0:T(8,128)S(1)} %all_to_all.5.received, f32[64,8,128]{2,1,0:T(8,128)S(1)} %collective-permute-done.4.swapped), custom_call_target="tpu_custom_call" | custom-call | tf_op jit(solution)/shard_map/smooth/pallas_call | solution.py:1143
Async XLA Ops:
  0.6 7.1 %copy-start = (f32[4,32,1024]{2,1,0:T(8,128)S(1)}, f32[4,32,1024]{2,1,0:T(8,128)}, u32[]{:S(2)}) copy-start(f32[4,32,1024]{2,1,0:T(8,128)} %param.5) | copy-start | bytes 1572868
  0.7 7.1 %copy-start.1 = (f32[4,32,1024]{2,1,0:T(8,128)S(1)}, f32[4,32,1024]{2,1,0:T(8,128)}, u32[]{:S(2)}) copy-start(f32[4,32,1024]{2,1,0:T(8,128)} %param.6) | copy-start | bytes 1572868
  0.7 7.1 %copy-start.2 = (f32[4,32,1024]{2,1,0:T(8,128)S(1)}, f32[4,32,1024]{2,1,0:T(8,128)}, u32[]{:S(2)}) copy-start(f32[4,32,1024]{2,1,0:T(8,128)} %param.7) | copy-start | bytes 1572868
  0.7 7.1 %copy-start.3 = (f32[4,32,1024]{2,1,0:T(8,128)S(1)}, f32[4,32,1024]{2,1,0:T(8,128)}, u32[]{:S(2)}) copy-start(f32[4,32,1024]{2,1,0:T(8,128)} %param.8) | copy-start | bytes 1572868
  6.1 1.7 %copy-start.4 = (s32[4]{0:T(128)S(1)}, s32[4]{0:T(128)}, u32[]{:S(2)}) copy-start(s32[4]{0:T(128)} %place.7) | copy-start | bytes 52
  6.2 1.6 %collective-permute-start = (f32[33,8,128]{2,1,0:T(8,128)}, f32[33,8,128]{2,1,0:T(8,128)S(1)}, u32[]{:S(2)}, u32[]{:S(2)}) collective-permute-start(f32[33,8,128]{2,1,0:T(8,128)} %get-tuple-element.11), channel_id=1, source_target_pairs={{0,1},{1,0},{2,3},{3,2},{4,5},{5,4},{6,7},{7,6},{8,9},{9,8},{10,11... | collective-permute-start | bytes 405512 | tf_op jit(solution)/shard_map/ppermute | solution.py:1050
  6.2 1.6 %collective-permute-start.1 = (f32[33,8,128]{2,1,0:T(8,128)}, f32[33,8,128]{2,1,0:T(8,128)S(1)}, u32[]{:S(2)}, u32[]{:S(2)}) collective-permute-start(f32[33,8,128]{2,1,0:T(8,128)} %get-tuple-element.12), channel_id=1, source_target_pairs={{1,2},{2,1},{3,4},{4,3},{5,6},{6,5},{9,10},{10,9},{11,12},{12,11},... | collective-permute-start | bytes 405512 | tf_op jit(solution)/shard_map/ppermute | solution.py:1051
  8.7 15.8 %collective-permute-start.2 = (f32[85,8,128]{2,1,0:T(8,128)S(1)}, f32[85,8,128]{2,1,0:T(8,128)S(1)}, u32[]{:S(2)}, u32[]{:S(2)}) collective-permute-start(f32[85,8,128]{2,1,0:T(8,128)S(1)} %get-tuple-element.13), channel_id=1, source_target_pairs={{8,0},{16,8},{24,16},{9,1},{17,9},{25,17},{10,2},{18,10},{26,18},{... | collective-permute-start | bytes 1044488 | tf_op jit(solution)/shard_map/ppermute | solution.py:1064
  12.0 13.8 %collective-permute-start.3 = (f32[85,8,128]{2,1,0:T(8,128)S(1)}, f32[85,8,128]{2,1,0:T(8,128)S(1)}, u32[]{:S(2)}, u32[]{:S(2)}) collective-permute-start(f32[85,8,128]{2,1,0:T(8,128)S(1)} %get-tuple-element.14), channel_id=1, source_target_pairs={{0,8},{8,16},{16,24},{1,9},{9,17},{17,25},{2,10},{10,18},{18,26},{... | collective-permute-start | bytes 1044488 | tf_op jit(solution)/shard_map/ppermute | solution.py:1063
  53.7 1.5 %collective-permute-start.4 = (f32[64,8,128]{2,1,0:T(8,128)S(1)}, f32[64,8,128]{2,1,0:T(8,128)S(1)}, u32[]{:S(2)}, u32[]{:S(2)}) collective-permute-start(f32[64,8,128]{2,1,0:T(8,128)S(1)} %all_to_all.5.received), channel_id=1, source_target_pairs={{0,1},{1,0},{2,3},{3,2},{4,5},{5,4},{6,7},{7,6},{8,9},{9,8},{10,11... | collective-permute-start | bytes 786440 | tf_op jit(solution)/shard_map/ppermute | solution.py:1140

commit v4 on v3

--- a/solution.py
+++ b/solution.py
@@ -26,6 +26,7 @@
 Z_SLABS = 72
 Z_TILES = 85
 DUMMY = 29
+GROUP = 4
 
 
 def lanes():
@@ -92,37 +93,43 @@
     wanted = 32 * (column % 32) + jnp.where(flipped, deep, 31 - deep)
     pick = jnp.where(cell == wanted, 1.0, 0.0).astype(jnp.bfloat16)
     depth = lanes() // 32
+    def field(moved, k, lead, c, side):
+        high, mid, low = (
+            moved[
+                384 * lead + (3 * k + third) * 32 + 8 * c : 384 * lead + (3 * k + third) * 32 + 8 * c + 8,
+                128 * side : 128 * side + 128,
+            ]
+            for third in range(3)
+        )
+        return (high + mid) + low
+
     for s in range(SLOTS):
         for fetch in fetches[s]:
             fetch.wait()
+        lead = s % GROUP
         for k, ref in enumerate((mat, heat, prior, load)):
             rest = ref[32 * s : 32 * s + 32, :]
             for third in range(3):
                 part = rest.astype(jnp.bfloat16)
-                at = (3 * k + third) * 32
+                at = 384 * lead + (3 * k + third) * 32
                 parts[at : at + 32, :] = part
                 rest = rest - part.astype(F32)
+        if lead < GROUP - 1:
+            continue
         moved = jnp.dot(parts[...], pick, preferred_element_type=F32)
-        for side, out in enumerate((near, far)):
-            for c in range(4):
-
-                def field(k):
-                    high, mid, low = (
-                        moved[
-                            (3 * k + third) * 32 + 8 * c : (3 * k + third) * 32 + 8 * c + 8,
-                            128 * side : 128 * side + 128,
-                        ]
-                        for third in range(3)
+        for lead in range(GROUP):
+            slot = s - GROUP + 1 + lead
+            for side, out in enumerate((near, far)):
+                for c in range(4):
+                    fraction, warm, dual, given = (
+                        field(moved, k, lead, c, side) for k in range(4)
                     )
-                    return (high + mid) + low
-
-                fraction, warm, dual, given = (field(k) for k in range(4))
-                own = conductivity(fraction)
-                beyond = conduct(own, pltpu.roll(own, 96, 1)) * pltpu.roll(dual, 96, 1)
-                given = pltpu.roll(given + jnp.where(depth == 1, beyond, 0.0), 64, 1)
-                unit = 4 * s + c
-                out[unit] = jnp.where(depth == 3, pltpu.roll(warm, 96, 1), fraction)
-                out[16 + unit] = jnp.where(depth < 2, dual, given)
+                    own = conductivity(fraction)
+                    beyond = conduct(own, pltpu.roll(own, 96, 1)) * pltpu.roll(dual, 96, 1)
+                    given = pltpu.roll(given + jnp.where(depth == 1, beyond, 0.0), 64, 1)
+                    unit = 4 * slot + c
+                    out[unit] = jnp.where(depth == 3, pltpu.roll(warm, 96, 1), fraction)
+                    out[16 + unit] = jnp.where(depth < 2, dual, given)
     meta = row_of([place[s] for s in range(SLOTS)])
     near[X_TILES - 1] = meta
     far[X_TILES - 1] = meta
@@ -893,73 +900,88 @@
     writing.wait()
 
 
+class Placer:
+    def __init__(self, grid, size, wide, across, code, column):
+        self.grid = grid
+        self.stride = 8 * wide
+        self.wide = wide
+        self.to = jnp.where(code >= 0, 0, size) + lax.div(column, across)
+        code = jnp.maximum(code, 0)
+        self.to = self.to + (code >> 1) * (2 * wide)
+        self.at = (column * 2 + (code & 1)) & 7
+        self.here = lanes() // 16 == self.at
+
+    def planes(self, tile, k, windows, first, moved=0):
+        found = []
+        for p, window in enumerate(windows):
+            shift = (self.at * 16 + moved + (-first - 16 * p) % 128) & 127
+            to = self.to + k * self.wide + window * self.stride
+            found.append((to, pltpu.roll(tile, shift, 1)))
+        return found
+
+    def put(self, planes):
+        old = [self.grid[to] for to, _ in planes]
+        for (to, moved), before in zip(planes, old):
+            self.grid[to] = jnp.where(self.here, moved, before)
+
+
+def code_of(meta, column, index):
+    return meta[column, 0, 0, 96 + index].astype(I32) - 1
+
+
 def filter_kernel(parts, planes, across, spot, meta, received, swapped, out, grid, once):
-    member = spot[0]
     depth = planes + 4
     wide = parts // across
     lane = lanes()
     row = rows()
-    group_lane = lane // 16
     zeros = jnp.zeros((8, 128), F32)
 
     def clear(index, carry):
         grid[index] = zeros
         return carry
 
-    lax.fori_loop(0, depth * 8 * wide, clear, 0, unroll=8)
-    begin = member * planes
+    lax.fori_loop(0, depth * 8 * wide, clear, 0, unroll=16)
+    begin = spot[0] * planes
     half = begin % 16 // 8
     side = jnp.where(begin % 8 == 0, 0, planes + 2) if planes < 8 else half * (planes + 2)
 
-    def place_plane(tile, lane_at, window, code, k, column, tile_x):
-        at = (column * 2 + code % 2) % 8
-        moved = pltpu.roll(tile, (at * 16 - lane_at + 256) % 128, 1)
-        where_to = (window * 8 + code // 2 * 2 + k) * wide + tile_x
-        grid[where_to] = jnp.where(group_lane == at, moved, grid[where_to])
-
     def from_device(column, carry):
-        tile_x = column // across
+        work = []
         for e in range(3):
-            code = meta[column, 0, 0, 96 + e].astype(I32) - 1
-
-            @pl.when(code >= 0)
-            def _(e=e, code=code):
+            placer = Placer(grid, depth * 8 * wide, wide, across, code_of(meta, column, e), column)
+            pair = [received[column * 8 + 2 * e + k] for k in range(2)]
+            if planes == 8:
+                found = []
                 for k in range(2):
-                    tile = received[column * 8 + 2 * e + k]
-                    if planes == 8:
-                        for p in range(8):
-                            place_plane(tile, 16 * p, p + 2, code, k, column, tile_x)
-                        other = swapped[column * 8 + 2 * e + k]
-                        for p in range(2):
-                            place_plane(
-                                other,
-                                jnp.where(half == 0, 16 * p, 96 + 16 * p),
-                                jnp.where(half == 0, 10 + p, p),
-                                code,
-                                k,
-                                column,
-                                tile_x,
-                            )
-                    else:
-                        for window in range(depth):
-                            p = begin % 8 + window - 2
-
-                            @pl.when((p >= 0) & (p < 8))
-                            def _(tile=tile, p=p, window=window, k=k):
-                                place_plane(tile, 16 * p, window, code, k, column, tile_x)
+                    found += placer.planes(pair[k], k, range(2, 10), 0)
+                    found += placer.planes(
+                        swapped[column * 8 + 2 * e + k],
+                        k,
+                        [jnp.where(half == 0, 10 + p, p) for p in range(2)],
+                        0,
+                        jnp.where(half == 0, 0, 32),
+                    )
+                work.append((placer, found))
+            else:
+                for window in range(depth):
+                    p = begin % 8 + window - 2
+
+                    @pl.when((p >= 0) & (p < 8))
+                    def _(p=p, window=window, pair=pair, placer=placer):
+                        found = []
+                        for k in range(2):
+                            found += placer.planes(pair[k], k, [window], 0, 128 - 16 * p)
+                        placer.put(found)
 
         for e in range(3):
-            code = meta[column, 0, 0, 99 + e].astype(I32) - 1
-
-            @pl.when(code >= 0)
-            def _(e=e, code=code):
-                for k in range(2):
-                    tile = received[column * 8 + 6 + k]
-                    for p in range(2):
-                        place_plane(
-                            tile, 32 * e + 16 * p, side + p, code, k, column, tile_x
-                        )
-
+            code = code_of(meta, column, 3 + e)
+            placer = Placer(grid, depth * 8 * wide, wide, across, code, column)
+            found = []
+            for k in range(2):
+                found += placer.planes(received[column * 8 + 6 + k], k, [side, side + 1], 32 * e)
+            work.append((placer, found))
+        for placer, found in work:
+            placer.put(found)
         return carry
 
     lax.fori_loop(0, parts, from_device, 0)
@@ -989,7 +1011,7 @@
                 once[(window * 8 + y) * wide + x] = relax(grid, window, y, x) * keep
         return carry
 
-    lax.fori_loop(1, depth - 1, sweep_once, 0, unroll=2)
+    lax.fori_loop(1, depth - 1, sweep_once, 0, unroll=5)
 
     def sweep_again(window, carry):
         for y in range(8):
@@ -999,7 +1021,7 @@
                 )
         return carry
 
-    lax.fori_loop(2, depth - 2, sweep_again, 0, unroll=2)
+    lax.fori_loop(2, depth - 2, sweep_again, 0, unroll=4)
 
 
 VMEM = pl.BlockSpec(memory_space=pltpu.VMEM)
@@ -1041,7 +1063,7 @@
         in_specs=[SMEM, SMEM, HBM, HBM, HBM, HBM],
         out_specs=(VMEM, VMEM),
         scratch_shapes=[pltpu.VMEM((128, 1024), F32)] * 4
-        + [pltpu.VMEM((384, 1024), jnp.bfloat16), pltpu.SemaphoreType.DMA((4, 4))],
+        + [pltpu.VMEM((384 * GROUP, 1024), jnp.bfloat16), pltpu.SemaphoreType.DMA((4, 4))],
         compiler_params=params(WHOLE),
         name="pack",
     )(place, parity, *fields)
@@ -1140,26 +1162,19 @@
     swapped = lax.ppermute(received, "ba", inner) if planes == 8 else received
     spot = jnp.stack([member, group * parts + member, jnp.int32(groups * parts)]).astype(I32)
     wide = 32 * parts // 128
+    codes = received.reshape(parts, 8, 8, 128)
+    codes_spec = pl.BlockSpec((parts, 1, 8, 128), lambda i: (0, 6, 0, 0), memory_space=pltpu.SMEM)
+    window = (planes + 4) * 8 * wide
     filtered = pl.pallas_call(
         functools.partial(filter_kernel, parts, planes, 4),
         out_shape=jax.ShapeDtypeStruct((planes, 64, 32 * parts), F32),
-        in_specs=[
-            SMEM,
-            pl.BlockSpec(
-                (parts, 1, 8, 128), lambda i: (0, 6, 0, 0), memory_space=pltpu.SMEM
-            ),
-            VMEM,
-            VMEM,
-        ],
+        in_specs=[SMEM, codes_spec, VMEM, VMEM],
         out_specs=VMEM,
-        scratch_shapes=[
-            pltpu.VMEM(((planes + 4) * 8 * wide, 8, 128), F32),
-            pltpu.VMEM(((planes + 4) * 8 * wide, 8, 128), F32),
-        ],
+        scratch_shapes=[pltpu.VMEM((2 * window, 8, 128), F32), pltpu.VMEM((window, 8, 128), F32)],
         grid=(1,),
         compiler_params=params(),
         name="smooth",
-    )(spot, received.reshape(parts, 8, 8, 128), received, swapped)
+    )(spot, codes, received, swapped)
     return (dual.reshape(material_fraction.shape), filtered)
 
 

time: 60.6 us -> 58.6 us (0.967); the launches traced: 61 us -> 58.3 us
  Pallas kernels: 28.8 us -> 26.7 us
  waiting for transfers between devices: 3.66 us -> 2.96 us
    pallas_call x1, Pallas kernels: 5.69 us -> 4.08 us  [per_device(): pl.pallas_call(functools.partial(filter_kernel, parts, planes, 4), out_sh...]
    pallas_call x1, Pallas kernels: 5.45 us -> 4.32 us  [per_device(): pl.pallas_call(pack_kernel, out_shape=(tiles(X_TILES), tiles(X_TILES)), i...]
    ppermute x1, waiting for transfers between devices: 1.33 us -> 0.63 us  [per_device(): from_below = lax.ppermute(up, 'gz', rising)]
    pallas_call x1, Pallas kernels: 9.96 us -> 10.7 us  [per_device(): pl.pallas_call(early_kernel, out_shape=(tiles(E_TILES), tiles(E_TILES), j...]
  transfers between devices with their start and end apart: 5 -> 5, of which waited for: 3 -> 3; matrix products, arithmetic and copies ran while one was open for 0% -> 0% of each run, Pallas kernels for 16% -> 18%
where the time goes in v4:
time: 58.6 us; the launch traced here: 58.3 us
  Pallas kernels  26.7 us (46%)
  blocking collectives  21.1 us (36%)
  starting transfers between devices  6.6 us (11%)
  waiting for transfers between devices  2.96 us (5%)
  between operations  0.77 us (1%)
    all_to_all x1, blocking collectives, per_device(): lax.all_to_all(chunks, 'ba', split_axis=0, concat_axis=0, tiled=True)  21.1 us
    pallas_call x1, Pallas kernels, per_device(): pl.pallas_call(early_kernel, out_shape=(tiles(E_TILES), tiles(E_TILES), j...  10.7 us
    pallas_call x1, Pallas kernels, per_device(): pl.pallas_call(functools.partial(late_kernel, parts), out_shape=(jax.Shap...  6.86 us
    pallas_call x1, Pallas kernels, per_device(): pl.pallas_call(pack_kernel, out_shape=(tiles(X_TILES), tiles(X_TILES)), i...  4.32 us
    pallas_call x1, Pallas kernels, per_device(): pl.pallas_call(functools.partial(filter_kernel, parts, planes, 4), out_sh...  4.08 us
    ppermute x1, starting transfers between devices, per_device(): from_above = lax.ppermute(down, 'gz', falling)  3.34 us
    ppermute x1, starting transfers between devices, per_device(): from_below = lax.ppermute(up, 'gz', rising)  2.52 us
    ppermute x1, waiting for transfers between devices, per_device(): swapped = lax.ppermute(received, 'ba', inner) if planes == 8 else received  1.46 us
  transfers between devices with their start and end apart: 5, of which 3 were waited for; matrix products, arithmetic and copies ran while one was open for 0% of the time, Pallas kernels for 18%

profile of v4, /device:TPU:4, one launch (start us, length us, event | category | flops | bytes accessed | tf_op | source)
XLA Modules:
  0.0 58.3 jit_solution(2490022663201873889)
XLA Ops:
  0.6 0.0 copy-start
  0.7 0.0 copy-start.1
  0.7 0.0 copy-start.2
  0.7 0.0 copy-start.3
  0.7 4.3 %pack.1 = (f32[33,8,128]{2,1,0:T(8,128)}, f32[33,8,128]{2,1,0:T(8,128)}) custom-call(s32[4]{0:T(128)} %place.7, s32[1]{0:T(128)} %bitcast.parity_ref, f32[128,1024]{1,0:T(8,128)} %bitcast.9, f32[128,1024]{1,0:T(8,128)} %bitcast.13, f32[128,1024]{1,0:T(8,128)} %bitcast.17, f32[128,1024]{1,0:T(8,128)} %bitcast.21), custom_call_target="tpu_custom_call" | custom-call | tf_op jit(solution)/shard_map/pack/pallas_call | solution.py:1060
  5.0 0.0 copy-start.4
  5.0 0.1 collective-permute-start
  5.1 0.7 %collective-permute-start.1 = (f32[33,8,128]{2,1,0:T(8,128)}, f32[33,8,128]{2,1,0:T(8,128)S(1)}, u32[]{:S(2)}, u32[]{:S(2)}) collective-permute-start(f32[33,8,128]{2,1,0:T(8,128)} %get-tuple-element.12), channel_id=1, source_target_pairs={{1,2},{2,1},{3,4},{4,3},{5,6},{6,5},{9,10},{10,9},{11,12},{12,11},... | collective-permute-start | bytes 405512 | tf_op jit(solution)/shard_map/ppermute | solution.py:1073
  5.8 0.9 %collective-permute-done.near_meta.near = f32[33,8,128]{2,1,0:T(8,128)S(1)} collective-permute-done((f32[33,8,128]{2,1,0:T(8,128)}, f32[33,8,128]{2,1,0:T(8,128)S(1)}, u32[]{:S(2)}, u32[]{:S(2)}) %collective-permute-start) | collective-permute-done | bytes 135200 | tf_op jit(solution)/shard_map/ppermute | solution.py:1072
  6.6 0.0 collective-permute-done.1.far_meta.far
  6.7 0.0 copy-done
  6.7 0.0 copy-done.1
  6.7 0.0 copy-done.2
  6.7 0.0 copy-done.3
  6.7 0.0 copy-done.4
  6.7 0.8 %corners.1 = (f32[85,8,128]{2,1,0:T(8,128)S(1)}, f32[85,8,128]{2,1,0:T(8,128)S(1)}) custom-call(s32[4]{0:T(128)S(1)} %copy-done.4, f32[33,8,128]{2,1,0:T(8,128)S(1)} %collective-permute-done.near_meta.near, f32[33,8,128]{2,1,0:T(8,128)S(1)} %collective-permute-done.1.far_meta.far, f32[128,1024]{1,0:T(8,128)S(1)} %bitcast.10, f32[128,1024]{1,0:T(8,128)S(1)} %bitcast.14, ...), custom_call_target="tpu_custom_call" | custom-call | tf_op jit(solution)/shard_map/corners/pallas_call | solution.py:1074
  7.5 3.3 %collective-permute-start.2 = (f32[85,8,128]{2,1,0:T(8,128)S(1)}, f32[85,8,128]{2,1,0:T(8,128)S(1)}, u32[]{:S(2)}, u32[]{:S(2)}) collective-permute-start(f32[85,8,128]{2,1,0:T(8,128)S(1)} %get-tuple-element.13), channel_id=1, source_target_pairs={{8,0},{16,8},{24,16},{9,1},{17,9},{25,17},{10,2},{18,10},{26,18},{... | collective-permute-start | bytes 1044488 | tf_op jit(solution)/shard_map/ppermute | solution.py:1086
  10.9 2.5 %collective-permute-start.3 = (f32[85,8,128]{2,1,0:T(8,128)S(1)}, f32[85,8,128]{2,1,0:T(8,128)S(1)}, u32[]{:S(2)}, u32[]{:S(2)}) collective-permute-start(f32[85,8,128]{2,1,0:T(8,128)S(1)} %get-tuple-element.14), channel_id=1, source_target_pairs={{0,8},{8,16},{16,24},{1,9},{9,17},{17,25},{2,10},{10,18},{18,26},{... | collective-permute-start | bytes 1044488 | tf_op jit(solution)/shard_map/ppermute | solution.py:1085
  13.4 10.7 %early.1 = (f32[192,8,128]{2,1,0:T(8,128)S(1)}, f32[192,8,128]{2,1,0:T(8,128)S(1)}, f32[2,64,128]{2,1,0:T(8,128)S(1)}) custom-call(s32[4]{0:T(128)S(1)} %copy-done.4, s32[1]{0:T(128)} %bitcast.parity_ref, f32[33,8,128]{2,1,0:T(8,128)S(1)} %collective-permute-done.near_meta.near, f32[33,8,128]{2,1,0:T(8,128)S(1)} %collective-permute-done.1.far_meta.far, ...), custom_call_target="tpu_custom_call" | custom-call | flops 1000000000 | bytes 30000000 | tf_op jit(solution)/shard_map/early/pallas_call | solution.py:1090
  24.0 0.0 collective-permute-done.2.up_meta.z_up
  24.1 0.6 %collective-permute-done.3.down_meta.z_down = f32[85,8,128]{2,1,0:T(8,128)S(1)} collective-permute-done((f32[85,8,128]{2,1,0:T(8,128)S(1)}, f32[85,8,128]{2,1,0:T(8,128)S(1)}, u32[]{:S(2)}, u32[]{:S(2)}) %collective-permute-start.3) | collective-permute-done | bytes 348192 | tf_op jit(solution)/shard_map/ppermute | solution.py:1085
  24.7 6.9 %late.1 = (f32[128,1024]{1,0:T(8,128)}, f32[64,8,128]{2,1,0:T(8,128)S(1)}) custom-call(s32[4]{0:T(128)S(1)} %copy-done.4, s32[1]{0:T(128)} %bitcast.parity_ref, f32[33,8,128]{2,1,0:T(8,128)S(1)} %collective-permute-done.near_meta.near, f32[33,8,128]{2,1,0:T(8,128)S(1)} %collective-permute-done.1.far_meta.far, ...), custom_call_target="tpu_custom_call" | custom-call | tf_op jit(solution)/shard_map/late/pallas_call | solution.py:1114
  31.5 21.1 %all_to_all.5.received = f32[64,8,128]{2,1,0:T(8,128)S(1)} all-to-all(f32[64,8,128]{2,1,0:T(8,128)S(1)} %get-tuple-element.19), channel_id=1, replica_groups=mesh['gz'=4,'ba'=8] {'ba'}, dimensions={0} | all-to-all | bytes 524288 | tf_op jit(solution)/shard_map/all_to_all | solution.py:1161
  52.6 0.0 collective-permute-start.4
  52.7 0.1 pad_add_fusion.spot
  52.7 1.5 %collective-permute-done.4.swapped = f32[64,8,128]{2,1,0:T(8,128)S(1)} collective-permute-done((f32[64,8,128]{2,1,0:T(8,128)S(1)}, f32[64,8,128]{2,1,0:T(8,128)S(1)}, u32[]{:S(2)}, u32[]{:S(2)}) %collective-permute-start.4) | collective-permute-done | bytes 262176 | tf_op jit(solution)/shard_map/ppermute | solution.py:1162
  54.2 4.1 %smooth.1 = f32[8,64,256]{2,1,0:T(8,128)} custom-call(s32[3]{0:T(128)S(1)} %pad_add_fusion.spot, f32[8,8,8,128]{3,2,1,0:T(8,128)S(1)} %bitcast.25, f32[64,8,128]{2,1,0:T(8,128)S(1)} %all_to_all.5.received, f32[64,8,128]{2,1,0:T(8,128)S(1)} %collective-permute-done.4.swapped), custom_call_target="tpu_custom_call" | custom-call | tf_op jit(solution)/shard_map/smooth/pallas_call | solution.py:1168
Async XLA Ops:
  0.6 6.0 %copy-start = (f32[4,32,1024]{2,1,0:T(8,128)S(1)}, f32[4,32,1024]{2,1,0:T(8,128)}, u32[]{:S(2)}) copy-start(f32[4,32,1024]{2,1,0:T(8,128)} %param.5) | copy-start | bytes 1572868
  0.7 6.0 %copy-start.1 = (f32[4,32,1024]{2,1,0:T(8,128)S(1)}, f32[4,32,1024]{2,1,0:T(8,128)}, u32[]{:S(2)}) copy-start(f32[4,32,1024]{2,1,0:T(8,128)} %param.6) | copy-start | bytes 1572868
  0.7 6.0 %copy-start.2 = (f32[4,32,1024]{2,1,0:T(8,128)S(1)}, f32[4,32,1024]{2,1,0:T(8,128)}, u32[]{:S(2)}) copy-start(f32[4,32,1024]{2,1,0:T(8,128)} %param.7) | copy-start | bytes 1572868
  0.7 6.0 %copy-start.3 = (f32[4,32,1024]{2,1,0:T(8,128)S(1)}, f32[4,32,1024]{2,1,0:T(8,128)}, u32[]{:S(2)}) copy-start(f32[4,32,1024]{2,1,0:T(8,128)} %param.8) | copy-start | bytes 1572868
  5.0 1.7 %copy-start.4 = (s32[4]{0:T(128)S(1)}, s32[4]{0:T(128)}, u32[]{:S(2)}) copy-start(s32[4]{0:T(128)} %place.7) | copy-start | bytes 52
  5.0 1.6 %collective-permute-start = (f32[33,8,128]{2,1,0:T(8,128)}, f32[33,8,128]{2,1,0:T(8,128)S(1)}, u32[]{:S(2)}, u32[]{:S(2)}) collective-permute-start(f32[33,8,128]{2,1,0:T(8,128)} %get-tuple-element.11), channel_id=1, source_target_pairs={{0,1},{1,0},{2,3},{3,2},{4,5},{5,4},{6,7},{7,6},{8,9},{9,8},{10,11... | collective-permute-start | bytes 405512 | tf_op jit(solution)/shard_map/ppermute | solution.py:1072
  5.1 1.6 %collective-permute-start.1 = (f32[33,8,128]{2,1,0:T(8,128)}, f32[33,8,128]{2,1,0:T(8,128)S(1)}, u32[]{:S(2)}, u32[]{:S(2)}) collective-permute-start(f32[33,8,128]{2,1,0:T(8,128)} %get-tuple-element.12), channel_id=1, source_target_pairs={{1,2},{2,1},{3,4},{4,3},{5,6},{6,5},{9,10},{10,9},{11,12},{12,11},... | collective-permute-start | bytes 405512 | tf_op jit(solution)/shard_map/ppermute | solution.py:1073
  7.5 16.5 %collective-permute-start.2 = (f32[85,8,128]{2,1,0:T(8,128)S(1)}, f32[85,8,128]{2,1,0:T(8,128)S(1)}, u32[]{:S(2)}, u32[]{:S(2)}) collective-permute-start(f32[85,8,128]{2,1,0:T(8,128)S(1)} %get-tuple-element.13), channel_id=1, source_target_pairs={{8,0},{16,8},{24,16},{9,1},{17,9},{25,17},{10,2},{18,10},{26,18},{... | collective-permute-start | bytes 1044488 | tf_op jit(solution)/shard_map/ppermute | solution.py:1086
  10.9 13.8 %collective-permute-start.3 = (f32[85,8,128]{2,1,0:T(8,128)S(1)}, f32[85,8,128]{2,1,0:T(8,128)S(1)}, u32[]{:S(2)}, u32[]{:S(2)}) collective-permute-start(f32[85,8,128]{2,1,0:T(8,128)S(1)} %get-tuple-element.14), channel_id=1, source_target_pairs={{0,8},{8,16},{16,24},{1,9},{9,17},{17,25},{2,10},{10,18},{18,26},{... | collective-permute-start | bytes 1044488 | tf_op jit(solution)/shard_map/ppermute | solution.py:1085
  52.6 1.5 %collective-permute-start.4 = (f32[64,8,128]{2,1,0:T(8,128)S(1)}, f32[64,8,128]{2,1,0:T(8,128)S(1)}, u32[]{:S(2)}, u32[]{:S(2)}) collective-permute-start(f32[64,8,128]{2,1,0:T(8,128)S(1)} %all_to_all.5.received), channel_id=1, source_target_pairs={{0,1},{1,0},{2,3},{3,2},{4,5},{5,4},{6,7},{7,6},{8,9},{9,8},{10,11... | collective-permute-start | bytes 786440 | tf_op jit(solution)/shard_map/ppermute | solution.py:1162

commit v5 on v4

--- a/solution.py
+++ b/solution.py
@@ -709,28 +709,23 @@
                     dual2[to + j] = early2[32 * s + 8 * chunk + j]
 
     for k, message in enumerate((z_up, z_down)):
-        for i in range(3):
-
-            @pl.when(brick_live[4 + 3 * k + i])
-            def _(k=k, i=i, message=message):
-                for j in range(8):
-                    t = 8 * i + j
-                    to = L_UP + 24 * k + t
-                    one, two, three = (message[t], message[24 + t], message[48 + t])
-                    a, b, c = ((3, 4, 6) if k else (1, 3, 5))
-                    kappa[to] = conductivity(one)
-                    dual0[to] = jnp.where(row >= 2 if k else row < 6, two, 0.0)
-                    source[to] = three
-                    temperature[to] = jnp.where(
-                        row == 3 if k else row == 0,
-                        pltpu.roll(one, a, 0),
-                        jnp.where(
-                            row < 6 if k else row < 3,
-                            pltpu.roll(two, b, 0),
-                            pltpu.roll(three, c, 0),
-                        ),
-                    )
-                    factor[to] = factor_of(one)
+        for t in range(24):
+            to = L_UP + 24 * k + t
+            one, two, three = (message[t], message[24 + t], message[48 + t])
+            a, b, c = ((3, 4, 6) if k else (1, 3, 5))
+            kappa[to] = conductivity(one)
+            dual0[to] = jnp.where(row >= 2 if k else row < 6, two, 0.0)
+            source[to] = three
+            temperature[to] = jnp.where(
+                row == 3 if k else row == 0,
+                pltpu.roll(one, a, 0),
+                jnp.where(
+                    row < 6 if k else row < 3,
+                    pltpu.roll(two, b, 0),
+                    pltpu.roll(three, c, 0),
+                ),
+            )
+            factor[to] = factor_of(one)
 
     def slab_tile(to, message, at, step):
         spread(to, message[at], message[at + step], kappa, temperature, source, dual0)
@@ -802,12 +797,11 @@
                 dual_rows[32 * s + 8 * c : 32 * s + 8 * c + 8, 128 * j : 128 * j + 128] = early2[
                     32 * s + 8 * c + j
                 ]
-
-        @pl.when(brick_live[s])
-        def _(s=s):
-            at = pl.multiple_of(32 * s + 24 * high[s], 8)
-            for j in range(8):
-                dual_rows[pl.ds(at, 8), 128 * j : 128 * j + 128] = dual2[8 * s + j]
+        at = pl.multiple_of(32 * s + 24 * high[s], 8)
+        for j in range(8):
+            dual_rows[pl.ds(at, 8), 128 * j : 128 * j + 128] = jnp.where(
+                brick_live[s], dual2[8 * s + j], early2[32 * s + 24 * high[s] + j]
+            )
 
     writing = pltpu.make_async_copy(dual_rows, dual_out, dual_sem)
     writing.start()
@@ -817,10 +811,10 @@
     for half in range(2):
         whole[...] = coarse[half]
         for s in range(SLOTS):
-
-            @pl.when(brick_live[s])
-            def _(s=s):
-                whole[pl.ds(16 * s + 12 * high[s], 4), :] = edge[half, 4 * s : 4 * s + 4, :]
+            at = 16 * s + 12 * high[s]
+            whole[pl.ds(at, 4), :] = jnp.where(
+                brick_live[s], edge[half, 4 * s : 4 * s + 4, :], coarse[half, pl.ds(at, 4), :]
+            )
 
         for r in range(11):
             if r < 8:

time: 58.6 us -> 57.7 us (0.985)
  blocking collectives: 21.1 us -> 20.1 us
  waiting for transfers between devices: 2.96 us -> 3.66 us
    all_to_all x1, blocking collectives: 21.1 us -> 20.1 us  [per_device(): lax.all_to_all(chunks, 'ba', split_axis=0, concat_axis=0, tiled=True)]
    ppermute x1, waiting for transfers between devices: 0.63 us -> 1.32 us  [per_device(): from_below = lax.ppermute(up, 'gz', rising)]
    pallas_call x1, Pallas kernels: 10.7 us -> 9.96 us  [per_device(): pl.pallas_call(early_kernel, out_shape=(tiles(E_TILES), tiles(E_TILES), j...]
  transfers between devices with their start and end apart: 5 -> 5, of which waited for: 3 -> 3; matrix products, arithmetic and copies ran while one was open for 0% -> 0% of each run, Pallas kernels for 18% -> 17%
where the time goes in v5:
time: 57.7 us; the launch traced here: 57.5 us
  Pallas kernels  26.3 us (46%)
  blocking collectives  20.1 us (35%)
  starting transfers between devices  6.6 us (11%)
  waiting for transfers between devices  3.66 us (6%)
  between operations  0.77 us (1%)
    all_to_all x1, blocking collectives, per_device(): lax.all_to_all(chunks, 'ba', split_axis=0, concat_axis=0, tiled=True)  20.1 us
    pallas_call x1, Pallas kernels, per_device(): pl.pallas_call(early_kernel, out_shape=(tiles(E_TILES), tiles(E_TILES), j...  9.96 us
    pallas_call x1, Pallas kernels, per_device(): pl.pallas_call(functools.partial(late_kernel, parts), out_shape=(jax.Shap...  7.11 us
    pallas_call x1, Pallas kernels, per_device(): pl.pallas_call(pack_kernel, out_shape=(tiles(X_TILES), tiles(X_TILES)), i...  4.32 us
    pallas_call x1, Pallas kernels, per_device(): pl.pallas_call(functools.partial(filter_kernel, parts, planes, 4), out_sh...  4.08 us
    ppermute x1, starting transfers between devices, per_device(): from_above = lax.ppermute(down, 'gz', falling)  3.34 us
    ppermute x1, starting transfers between devices, per_device(): from_below = lax.ppermute(up, 'gz', rising)  2.52 us
    ppermute x1, waiting for transfers between devices, per_device(): swapped = lax.ppermute(received, 'ba', inner) if planes == 8 else received  1.46 us
  transfers between devices with their start and end apart: 5, of which 3 were waited for; matrix products, arithmetic and copies ran while one was open for 0% of the time, Pallas kernels for 17%

profile of v5, /device:TPU:4, one launch (start us, length us, event | category | flops | bytes accessed | tf_op | source)
XLA Modules:
  0.0 57.5 jit_solution(14955611319983338176)
XLA Ops:
  0.6 0.0 copy-start
  0.7 0.0 copy-start.1
  0.7 0.0 copy-start.2
  0.7 0.0 copy-start.3
  0.7 4.3 %pack.1 = (f32[33,8,128]{2,1,0:T(8,128)}, f32[33,8,128]{2,1,0:T(8,128)}) custom-call(s32[4]{0:T(128)} %place.7, s32[1]{0:T(128)} %bitcast.parity_ref, f32[128,1024]{1,0:T(8,128)} %bitcast.9, f32[128,1024]{1,0:T(8,128)} %bitcast.13, f32[128,1024]{1,0:T(8,128)} %bitcast.17, f32[128,1024]{1,0:T(8,128)} %bitcast.21), custom_call_target="tpu_custom_call" | custom-call | tf_op jit(solution)/shard_map/pack/pallas_call | solution.py:1054
  5.0 0.0 copy-start.4
  5.0 0.1 collective-permute-start
  5.1 0.7 %collective-permute-start.1 = (f32[33,8,128]{2,1,0:T(8,128)}, f32[33,8,128]{2,1,0:T(8,128)S(1)}, u32[]{:S(2)}, u32[]{:S(2)}) collective-permute-start(f32[33,8,128]{2,1,0:T(8,128)} %get-tuple-element.12), channel_id=1, source_target_pairs={{1,2},{2,1},{3,4},{4,3},{5,6},{6,5},{9,10},{10,9},{11,12},{12,11},... | collective-permute-start | bytes 405512 | tf_op jit(solution)/shard_map/ppermute | solution.py:1067
  5.8 0.9 %collective-permute-done.near_meta.near = f32[33,8,128]{2,1,0:T(8,128)S(1)} collective-permute-done((f32[33,8,128]{2,1,0:T(8,128)}, f32[33,8,128]{2,1,0:T(8,128)S(1)}, u32[]{:S(2)}, u32[]{:S(2)}) %collective-permute-start) | collective-permute-done | bytes 135200 | tf_op jit(solution)/shard_map/ppermute | solution.py:1066
  6.6 0.0 collective-permute-done.1.far_meta.far
  6.7 0.0 copy-done
  6.7 0.0 copy-done.1
  6.7 0.0 copy-done.2
  6.7 0.0 copy-done.3
  6.7 0.0 copy-done.4
  6.7 0.8 %corners.1 = (f32[85,8,128]{2,1,0:T(8,128)S(1)}, f32[85,8,128]{2,1,0:T(8,128)S(1)}) custom-call(s32[4]{0:T(128)S(1)} %copy-done.4, f32[33,8,128]{2,1,0:T(8,128)S(1)} %collective-permute-done.near_meta.near, f32[33,8,128]{2,1,0:T(8,128)S(1)} %collective-permute-done.1.far_meta.far, f32[128,1024]{1,0:T(8,128)S(1)} %bitcast.10, f32[128,1024]{1,0:T(8,128)S(1)} %bitcast.14, ...), custom_call_target="tpu_custom_call" | custom-call | tf_op jit(solution)/shard_map/corners/pallas_call | solution.py:1068
  7.5 3.3 %collective-permute-start.2 = (f32[85,8,128]{2,1,0:T(8,128)S(1)}, f32[85,8,128]{2,1,0:T(8,128)S(1)}, u32[]{:S(2)}, u32[]{:S(2)}) collective-permute-start(f32[85,8,128]{2,1,0:T(8,128)S(1)} %get-tuple-element.13), channel_id=1, source_target_pairs={{8,0},{16,8},{24,16},{9,1},{17,9},{25,17},{10,2},{18,10},{26,18},{... | collective-permute-start | bytes 1044488 | tf_op jit(solution)/shard_map/ppermute | solution.py:1080
  10.9 2.5 %collective-permute-start.3 = (f32[85,8,128]{2,1,0:T(8,128)S(1)}, f32[85,8,128]{2,1,0:T(8,128)S(1)}, u32[]{:S(2)}, u32[]{:S(2)}) collective-permute-start(f32[85,8,128]{2,1,0:T(8,128)S(1)} %get-tuple-element.14), channel_id=1, source_target_pairs={{0,8},{8,16},{16,24},{1,9},{9,17},{17,25},{2,10},{10,18},{18,26},{... | collective-permute-start | bytes 1044488 | tf_op jit(solution)/shard_map/ppermute | solution.py:1079
  13.4 10.0 %early.1 = (f32[192,8,128]{2,1,0:T(8,128)S(1)}, f32[192,8,128]{2,1,0:T(8,128)S(1)}, f32[2,64,128]{2,1,0:T(8,128)S(1)}) custom-call(s32[4]{0:T(128)S(1)} %copy-done.4, s32[1]{0:T(128)} %bitcast.parity_ref, f32[33,8,128]{2,1,0:T(8,128)S(1)} %collective-permute-done.near_meta.near, f32[33,8,128]{2,1,0:T(8,128)S(1)} %collective-permute-done.1.far_meta.far, ...), custom_call_target="tpu_custom_call" | custom-call | flops 1000000000 | bytes 30000000 | tf_op jit(solution)/shard_map/early/pallas_call | solution.py:1084
  23.3 0.0 collective-permute-done.2.up_meta.z_up
  23.4 1.3 %collective-permute-done.3.down_meta.z_down = f32[85,8,128]{2,1,0:T(8,128)S(1)} collective-permute-done((f32[85,8,128]{2,1,0:T(8,128)S(1)}, f32[85,8,128]{2,1,0:T(8,128)S(1)}, u32[]{:S(2)}, u32[]{:S(2)}) %collective-permute-start.3) | collective-permute-done | bytes 348192 | tf_op jit(solution)/shard_map/ppermute | solution.py:1079
  24.7 7.1 %late.1 = (f32[128,1024]{1,0:T(8,128)}, f32[64,8,128]{2,1,0:T(8,128)S(1)}) custom-call(s32[4]{0:T(128)S(1)} %copy-done.4, s32[1]{0:T(128)} %bitcast.parity_ref, f32[33,8,128]{2,1,0:T(8,128)S(1)} %collective-permute-done.near_meta.near, f32[33,8,128]{2,1,0:T(8,128)S(1)} %collective-permute-done.1.far_meta.far, ...), custom_call_target="tpu_custom_call" | custom-call | tf_op jit(solution)/shard_map/late/pallas_call | solution.py:1108
  31.8 20.1 %all_to_all.5.received = f32[64,8,128]{2,1,0:T(8,128)S(1)} all-to-all(f32[64,8,128]{2,1,0:T(8,128)S(1)} %get-tuple-element.19), channel_id=1, replica_groups=mesh['gz'=4,'ba'=8] {'ba'}, dimensions={0} | all-to-all | bytes 524288 | tf_op jit(solution)/shard_map/all_to_all | solution.py:1155
  51.9 0.0 collective-permute-start.4
  51.9 0.1 pad_add_fusion.spot
  52.0 1.5 %collective-permute-done.4.swapped = f32[64,8,128]{2,1,0:T(8,128)S(1)} collective-permute-done((f32[64,8,128]{2,1,0:T(8,128)S(1)}, f32[64,8,128]{2,1,0:T(8,128)S(1)}, u32[]{:S(2)}, u32[]{:S(2)}) %collective-permute-start.4) | collective-permute-done | bytes 262176 | tf_op jit(solution)/shard_map/ppermute | solution.py:1156
  53.4 4.1 %smooth.1 = f32[8,64,256]{2,1,0:T(8,128)} custom-call(s32[3]{0:T(128)S(1)} %pad_add_fusion.spot, f32[8,8,8,128]{3,2,1,0:T(8,128)S(1)} %bitcast.25, f32[64,8,128]{2,1,0:T(8,128)S(1)} %all_to_all.5.received, f32[64,8,128]{2,1,0:T(8,128)S(1)} %collective-permute-done.4.swapped), custom_call_target="tpu_custom_call" | custom-call | tf_op jit(solution)/shard_map/smooth/pallas_call | solution.py:1162
Async XLA Ops:
  0.6 6.0 %copy-start = (f32[4,32,1024]{2,1,0:T(8,128)S(1)}, f32[4,32,1024]{2,1,0:T(8,128)}, u32[]{:S(2)}) copy-start(f32[4,32,1024]{2,1,0:T(8,128)} %param.5) | copy-start | bytes 1572868
  0.7 6.0 %copy-start.1 = (f32[4,32,1024]{2,1,0:T(8,128)S(1)}, f32[4,32,1024]{2,1,0:T(8,128)}, u32[]{:S(2)}) copy-start(f32[4,32,1024]{2,1,0:T(8,128)} %param.6) | copy-start | bytes 1572868
  0.7 6.0 %copy-start.2 = (f32[4,32,1024]{2,1,0:T(8,128)S(1)}, f32[4,32,1024]{2,1,0:T(8,128)}, u32[]{:S(2)}) copy-start(f32[4,32,1024]{2,1,0:T(8,128)} %param.7) | copy-start | bytes 1572868
  0.7 6.0 %copy-start.3 = (f32[4,32,1024]{2,1,0:T(8,128)S(1)}, f32[4,32,1024]{2,1,0:T(8,128)}, u32[]{:S(2)}) copy-start(f32[4,32,1024]{2,1,0:T(8,128)} %param.8) | copy-start | bytes 1572868
  5.0 1.7 %copy-start.4 = (s32[4]{0:T(128)S(1)}, s32[4]{0:T(128)}, u32[]{:S(2)}) copy-start(s32[4]{0:T(128)} %place.7) | copy-start | bytes 52
  5.0 1.6 %collective-permute-start = (f32[33,8,128]{2,1,0:T(8,128)}, f32[33,8,128]{2,1,0:T(8,128)S(1)}, u32[]{:S(2)}, u32[]{:S(2)}) collective-permute-start(f32[33,8,128]{2,1,0:T(8,128)} %get-tuple-element.11), channel_id=1, source_target_pairs={{0,1},{1,0},{2,3},{3,2},{4,5},{5,4},{6,7},{7,6},{8,9},{9,8},{10,11... | collective-permute-start | bytes 405512 | tf_op jit(solution)/shard_map/ppermute | solution.py:1066
  5.1 1.6 %collective-permute-start.1 = (f32[33,8,128]{2,1,0:T(8,128)}, f32[33,8,128]{2,1,0:T(8,128)S(1)}, u32[]{:S(2)}, u32[]{:S(2)}) collective-permute-start(f32[33,8,128]{2,1,0:T(8,128)} %get-tuple-element.12), channel_id=1, source_target_pairs={{1,2},{2,1},{3,4},{4,3},{5,6},{6,5},{9,10},{10,9},{11,12},{12,11},... | collective-permute-start | bytes 405512 | tf_op jit(solution)/shard_map/ppermute | solution.py:1067
  7.5 15.8 %collective-permute-start.2 = (f32[85,8,128]{2,1,0:T(8,128)S(1)}, f32[85,8,128]{2,1,0:T(8,128)S(1)}, u32[]{:S(2)}, u32[]{:S(2)}) collective-permute-start(f32[85,8,128]{2,1,0:T(8,128)S(1)} %get-tuple-element.13), channel_id=1, source_target_pairs={{8,0},{16,8},{24,16},{9,1},{17,9},{25,17},{10,2},{18,10},{26,18},{... | collective-permute-start | bytes 1044488 | tf_op jit(solution)/shard_map/ppermute | solution.py:1080
  10.9 13.8 %collective-permute-start.3 = (f32[85,8,128]{2,1,0:T(8,128)S(1)}, f32[85,8,128]{2,1,0:T(8,128)S(1)}, u32[]{:S(2)}, u32[]{:S(2)}) collective-permute-start(f32[85,8,128]{2,1,0:T(8,128)S(1)} %get-tuple-element.14), channel_id=1, source_target_pairs={{0,8},{8,16},{16,24},{1,9},{9,17},{17,25},{2,10},{10,18},{18,26},{... | collective-permute-start | bytes 1044488 | tf_op jit(solution)/shard_map/ppermute | solution.py:1079
  51.9 1.5 %collective-permute-start.4 = (f32[64,8,128]{2,1,0:T(8,128)S(1)}, f32[64,8,128]{2,1,0:T(8,128)S(1)}, u32[]{:S(2)}, u32[]{:S(2)}) collective-permute-start(f32[64,8,128]{2,1,0:T(8,128)S(1)} %all_to_all.5.received), channel_id=1, source_target_pairs={{0,1},{1,0},{2,3},{3,2},{4,5},{5,4},{6,7},{7,6},{8,9},{9,8},{10,11... | collective-permute-start | bytes 786440 | tf_op jit(solution)/shard_map/ppermute | solution.py:1156

commit v6 on v5

--- a/solution.py
+++ b/solution.py
@@ -650,15 +650,12 @@
         base = L_SLAB + 14 * b
         for k in range(10):
             here = slab_cell[10 * b + k]
-            above, below = (cells[here + 24], cells[here - 24])
+            above = jnp.int32(L_ZERO) if 4 <= k < 7 else cells[here + 24]
+            below = jnp.int32(L_ZERO) if k >= 7 else cells[here - 24]
             if k < 4:
                 top = slab_own[b][k] >= 24
                 inner = base + 4 + k
                 above, below = (jnp.where(top, above, inner), jnp.where(top, inner, below))
-            elif k < 7:
-                above = jnp.int32(L_ZERO)
-            else:
-                below = jnp.int32(L_ZERO)
             fill(
                 slab_table,
                 10 * b + k,

time: 57.7 us -> 58.4 us (1.012); the launches traced: 57.5 us -> 57.5 us
  Pallas kernels: 26.3 us -> 25.3 us
  blocking collectives: 20.1 us -> 21.1 us
    pallas_call x1, Pallas kernels: 7.11 us -> 6.11 us  [per_device(): pl.pallas_call(functools.partial(late_kernel, parts), out_shape=(jax.Shap...]
    all_to_all x1, blocking collectives: 20.1 us -> 21.1 us  [per_device(): lax.all_to_all(chunks, 'ba', split_axis=0, concat_axis=0, tiled=True)]
where the time goes in v6:
time: 58.4 us; the launch traced here: 57.5 us
  Pallas kernels  25.3 us (43%)
  blocking collectives  21.1 us (36%)
  starting transfers between devices  6.6 us (11%)
  waiting for transfers between devices  3.66 us (6%)
  between operations  0.77 us (1%)
    all_to_all x1, blocking collectives, per_device(): lax.all_to_all(chunks, 'ba', split_axis=0, concat_axis=0, tiled=True)  21.1 us
    pallas_call x1, Pallas kernels, per_device(): pl.pallas_call(early_kernel, out_shape=(tiles(E_TILES), tiles(E_TILES), j...  9.96 us
    pallas_call x1, Pallas kernels, per_device(): pl.pallas_call(functools.partial(late_kernel, parts), out_shape=(jax.Shap...  6.11 us
    pallas_call x1, Pallas kernels, per_device(): pl.pallas_call(pack_kernel, out_shape=(tiles(X_TILES), tiles(X_TILES)), i...  4.32 us
    pallas_call x1, Pallas kernels, per_device(): pl.pallas_call(functools.partial(filter_kernel, parts, planes, 4), out_sh...  4.08 us
    ppermute x1, starting transfers between devices, per_device(): from_above = lax.ppermute(down, 'gz', falling)  3.34 us
    ppermute x1, starting transfers between devices, per_device(): from_below = lax.ppermute(up, 'gz', rising)  2.52 us
    ppermute x1, waiting for transfers between devices, per_device(): swapped = lax.ppermute(received, 'ba', inner) if planes == 8 else received  1.46 us
  transfers between devices with their start and end apart: 5, of which 3 were waited for; matrix products, arithmetic and copies ran while one was open for 0% of the time, Pallas kernels for 17%

profile of v6, /device:TPU:4, one launch (start us, length us, event | category | flops | bytes accessed | tf_op | source)
XLA Modules:
  0.0 57.5 jit_solution(14955611319983338176)
XLA Ops:
  0.6 0.0 copy-start
  0.7 0.0 copy-start.1
  0.7 0.0 copy-start.2
  0.7 0.0 copy-start.3
  0.7 4.3 %pack.1 = (f32[33,8,128]{2,1,0:T(8,128)}, f32[33,8,128]{2,1,0:T(8,128)}) custom-call(s32[4]{0:T(128)} %place.7, s32[1]{0:T(128)} %bitcast.parity_ref, f32[128,1024]{1,0:T(8,128)} %bitcast.9, f32[128,1024]{1,0:T(8,128)} %bitcast.13, f32[128,1024]{1,0:T(8,128)} %bitcast.17, f32[128,1024]{1,0:T(8,128)} %bitcast.21), custom_call_target="tpu_custom_call" | custom-call | tf_op jit(solution)/shard_map/pack/pallas_call | solution.py:1051
  5.0 0.0 copy-start.4
  5.0 0.1 collective-permute-start
  5.1 0.7 %collective-permute-start.1 = (f32[33,8,128]{2,1,0:T(8,128)}, f32[33,8,128]{2,1,0:T(8,128)S(1)}, u32[]{:S(2)}, u32[]{:S(2)}) collective-permute-start(f32[33,8,128]{2,1,0:T(8,128)} %get-tuple-element.12), channel_id=1, source_target_pairs={{1,2},{2,1},{3,4},{4,3},{5,6},{6,5},{9,10},{10,9},{11,12},{12,11},... | collective-permute-start | bytes 405512 | tf_op jit(solution)/shard_map/ppermute | solution.py:1064
  5.8 0.9 %collective-permute-done.near_meta.near = f32[33,8,128]{2,1,0:T(8,128)S(1)} collective-permute-done((f32[33,8,128]{2,1,0:T(8,128)}, f32[33,8,128]{2,1,0:T(8,128)S(1)}, u32[]{:S(2)}, u32[]{:S(2)}) %collective-permute-start) | collective-permute-done | bytes 135200 | tf_op jit(solution)/shard_map/ppermute | solution.py:1063
  6.6 0.0 collective-permute-done.1.far_meta.far
  6.7 0.0 copy-done
  6.7 0.0 copy-done.1
  6.7 0.0 copy-done.2
  6.7 0.0 copy-done.3
  6.7 0.0 copy-done.4
  6.7 0.8 %corners.1 = (f32[85,8,128]{2,1,0:T(8,128)S(1)}, f32[85,8,128]{2,1,0:T(8,128)S(1)}) custom-call(s32[4]{0:T(128)S(1)} %copy-done.4, f32[33,8,128]{2,1,0:T(8,128)S(1)} %collective-permute-done.near_meta.near, f32[33,8,128]{2,1,0:T(8,128)S(1)} %collective-permute-done.1.far_meta.far, f32[128,1024]{1,0:T(8,128)S(1)} %bitcast.10, f32[128,1024]{1,0:T(8,128)S(1)} %bitcast.14, ...), custom_call_target="tpu_custom_call" | custom-call | tf_op jit(solution)/shard_map/corners/pallas_call | solution.py:1065
  7.5 3.3 %collective-permute-start.2 = (f32[85,8,128]{2,1,0:T(8,128)S(1)}, f32[85,8,128]{2,1,0:T(8,128)S(1)}, u32[]{:S(2)}, u32[]{:S(2)}) collective-permute-start(f32[85,8,128]{2,1,0:T(8,128)S(1)} %get-tuple-element.13), channel_id=1, source_target_pairs={{8,0},{16,8},{24,16},{9,1},{17,9},{25,17},{10,2},{18,10},{26,18},{... | collective-permute-start | bytes 1044488 | tf_op jit(solution)/shard_map/ppermute | solution.py:1077
  10.9 2.5 %collective-permute-start.3 = (f32[85,8,128]{2,1,0:T(8,128)S(1)}, f32[85,8,128]{2,1,0:T(8,128)S(1)}, u32[]{:S(2)}, u32[]{:S(2)}) collective-permute-start(f32[85,8,128]{2,1,0:T(8,128)S(1)} %get-tuple-element.14), channel_id=1, source_target_pairs={{0,8},{8,16},{16,24},{1,9},{9,17},{17,25},{2,10},{10,18},{18,26},{... | collective-permute-start | bytes 1044488 | tf_op jit(solution)/shard_map/ppermute | solution.py:1076
  13.4 10.0 %early.1 = (f32[192,8,128]{2,1,0:T(8,128)S(1)}, f32[192,8,128]{2,1,0:T(8,128)S(1)}, f32[2,64,128]{2,1,0:T(8,128)S(1)}) custom-call(s32[4]{0:T(128)S(1)} %copy-done.4, s32[1]{0:T(128)} %bitcast.parity_ref, f32[33,8,128]{2,1,0:T(8,128)S(1)} %collective-permute-done.near_meta.near, f32[33,8,128]{2,1,0:T(8,128)S(1)} %collective-permute-done.1.far_meta.far, ...), custom_call_target="tpu_custom_call" | custom-call | flops 1000000000 | bytes 30000000 | tf_op jit(solution)/shard_map/early/pallas_call | solution.py:1081
  23.3 0.0 collective-permute-done.2.up_meta.z_up
  23.4 1.3 %collective-permute-done.3.down_meta.z_down = f32[85,8,128]{2,1,0:T(8,128)S(1)} collective-permute-done((f32[85,8,128]{2,1,0:T(8,128)S(1)}, f32[85,8,128]{2,1,0:T(8,128)S(1)}, u32[]{:S(2)}, u32[]{:S(2)}) %collective-permute-start.3) | collective-permute-done | bytes 348192 | tf_op jit(solution)/shard_map/ppermute | solution.py:1076
  24.7 6.1 %late.1 = (f32[128,1024]{1,0:T(8,128)}, f32[64,8,128]{2,1,0:T(8,128)S(1)}) custom-call(s32[4]{0:T(128)S(1)} %copy-done.4, s32[1]{0:T(128)} %bitcast.parity_ref, f32[33,8,128]{2,1,0:T(8,128)S(1)} %collective-permute-done.near_meta.near, f32[33,8,128]{2,1,0:T(8,128)S(1)} %collective-permute-done.1.far_meta.far, ...), custom_call_target="tpu_custom_call" | custom-call | tf_op jit(solution)/shard_map/late/pallas_call | solution.py:1105
  30.8 21.1 %all_to_all.5.received = f32[64,8,128]{2,1,0:T(8,128)S(1)} all-to-all(f32[64,8,128]{2,1,0:T(8,128)S(1)} %get-tuple-element.19), channel_id=1, replica_groups=mesh['gz'=4,'ba'=8] {'ba'}, dimensions={0} | all-to-all | bytes 524288 | tf_op jit(solution)/shard_map/all_to_all | solution.py:1152
  51.9 0.0 collective-permute-start.4
  51.9 0.1 pad_add_fusion.spot
  52.0 1.5 %collective-permute-done.4.swapped = f32[64,8,128]{2,1,0:T(8,128)S(1)} collective-permute-done((f32[64,8,128]{2,1,0:T(8,128)S(1)}, f32[64,8,128]{2,1,0:T(8,128)S(1)}, u32[]{:S(2)}, u32[]{:S(2)}) %collective-permute-start.4) | collective-permute-done | bytes 262176 | tf_op jit(solution)/shard_map/ppermute | solution.py:1153
  53.4 4.1 %smooth.1 = f32[8,64,256]{2,1,0:T(8,128)} custom-call(s32[3]{0:T(128)S(1)} %pad_add_fusion.spot, f32[8,8,8,128]{3,2,1,0:T(8,128)S(1)} %bitcast.25, f32[64,8,128]{2,1,0:T(8,128)S(1)} %all_to_all.5.received, f32[64,8,128]{2,1,0:T(8,128)S(1)} %collective-permute-done.4.swapped), custom_call_target="tpu_custom_call" | custom-call | tf_op jit(solution)/shard_map/smooth/pallas_call | solution.py:1159
Async XLA Ops:
  0.6 6.0 %copy-start = (f32[4,32,1024]{2,1,0:T(8,128)S(1)}, f32[4,32,1024]{2,1,0:T(8,128)}, u32[]{:S(2)}) copy-start(f32[4,32,1024]{2,1,0:T(8,128)} %param.5) | copy-start | bytes 1572868
  0.7 6.0 %copy-start.1 = (f32[4,32,1024]{2,1,0:T(8,128)S(1)}, f32[4,32,1024]{2,1,0:T(8,128)}, u32[]{:S(2)}) copy-start(f32[4,32,1024]{2,1,0:T(8,128)} %param.6) | copy-start | bytes 1572868
  0.7 6.0 %copy-start.2 = (f32[4,32,1024]{2,1,0:T(8,128)S(1)}, f32[4,32,1024]{2,1,0:T(8,128)}, u32[]{:S(2)}) copy-start(f32[4,32,1024]{2,1,0:T(8,128)} %param.7) | copy-start | bytes 1572868
  0.7 6.0 %copy-start.3 = (f32[4,32,1024]{2,1,0:T(8,128)S(1)}, f32[4,32,1024]{2,1,0:T(8,128)}, u32[]{:S(2)}) copy-start(f32[4,32,1024]{2,1,0:T(8,128)} %param.8) | copy-start | bytes 1572868
  5.0 1.7 %copy-start.4 = (s32[4]{0:T(128)S(1)}, s32[4]{0:T(128)}, u32[]{:S(2)}) copy-start(s32[4]{0:T(128)} %place.7) | copy-start | bytes 52
  5.0 1.6 %collective-permute-start = (f32[33,8,128]{2,1,0:T(8,128)}, f32[33,8,128]{2,1,0:T(8,128)S(1)}, u32[]{:S(2)}, u32[]{:S(2)}) collective-permute-start(f32[33,8,128]{2,1,0:T(8,128)} %get-tuple-element.11), channel_id=1, source_target_pairs={{0,1},{1,0},{2,3},{3,2},{4,5},{5,4},{6,7},{7,6},{8,9},{9,8},{10,11... | collective-permute-start | bytes 405512 | tf_op jit(solution)/shard_map/ppermute | solution.py:1063
  5.1 1.6 %collective-permute-start.1 = (f32[33,8,128]{2,1,0:T(8,128)}, f32[33,8,128]{2,1,0:T(8,128)S(1)}, u32[]{:S(2)}, u32[]{:S(2)}) collective-permute-start(f32[33,8,128]{2,1,0:T(8,128)} %get-tuple-element.12), channel_id=1, source_target_pairs={{1,2},{2,1},{3,4},{4,3},{5,6},{6,5},{9,10},{10,9},{11,12},{12,11},... | collective-permute-start | bytes 405512 | tf_op jit(solution)/shard_map/ppermute | solution.py:1064
  7.5 15.8 %collective-permute-start.2 = (f32[85,8,128]{2,1,0:T(8,128)S(1)}, f32[85,8,128]{2,1,0:T(8,128)S(1)}, u32[]{:S(2)}, u32[]{:S(2)}) collective-permute-start(f32[85,8,128]{2,1,0:T(8,128)S(1)} %get-tuple-element.13), channel_id=1, source_target_pairs={{8,0},{16,8},{24,16},{9,1},{17,9},{25,17},{10,2},{18,10},{26,18},{... | collective-permute-start | bytes 1044488 | tf_op jit(solution)/shard_map/ppermute | solution.py:1077
  10.9 13.8 %collective-permute-start.3 = (f32[85,8,128]{2,1,0:T(8,128)S(1)}, f32[85,8,128]{2,1,0:T(8,128)S(1)}, u32[]{:S(2)}, u32[]{:S(2)}) collective-permute-start(f32[85,8,128]{2,1,0:T(8,128)S(1)} %get-tuple-element.14), channel_id=1, source_target_pairs={{0,8},{8,16},{16,24},{1,9},{9,17},{17,25},{2,10},{10,18},{18,26},{... | collective-permute-start | bytes 1044488 | tf_op jit(solution)/shard_map/ppermute | solution.py:1076
  51.9 1.5 %collective-permute-start.4 = (f32[64,8,128]{2,1,0:T(8,128)S(1)}, f32[64,8,128]{2,1,0:T(8,128)S(1)}, u32[]{:S(2)}, u32[]{:S(2)}) collective-permute-start(f32[64,8,128]{2,1,0:T(8,128)S(1)} %all_to_all.5.received), channel_id=1, source_target_pairs={{0,1},{1,0},{2,3},{3,2},{4,5},{5,4},{6,7},{7,6},{8,9},{9,8},{10,11... | collective-permute-start | bytes 786440 | tf_op jit(solution)/shard_map/ppermute | solution.py:1153
